TPU v7x, 32 devices: a whole 2x2x4 slice. The times are simulated.
32 devices in a mesh: dp: 16 (over z, y, x), fsdp: 2 (over core).
Axes of the slice: x: 2, y: 2, z: 4, core: 2. Of those that a mesh axis runs over, the one named last changes fastest.
Arguments:
- tokens: bfloat16 [32, 1024, 768], P(('dp', 'fsdp')), may hold values from -6 to 6
- cotangent: bfloat16 [32, 1024, 768], P(('dp', 'fsdp')), may hold values from -6 to 6
- segments: int32 [32, 1024], P(('dp', 'fsdp')), may hold values from 0 to 15, never falling along the last dimension, each value on 1 to 128 neighbouring positions
- keep_mask: int32 [32, 1024], P(('dp', 'fsdp')), may hold values 0 or 1
- qkv_weight: float32 [2, 768, 2304], P(None, 'fsdp'), may hold values from -0.21875 to 0.21875
- qkv_first: float32 [2, 768, 2304], P(None, 'fsdp'), may hold values from -512 to 512
- qkv_second: float32 [2, 768, 2304], P(None, 'fsdp'), may hold values from 4096 to 65536
- proj_weight: float32 [2, 768, 768], P(None, 'fsdp'), may hold values from -0.625 to 0.625
- proj_first: float32 [2, 768, 768], P(None, 'fsdp'), may hold values from -512 to 512
- proj_second: float32 [2, 768, 768], P(None, 'fsdp'), may hold values from 4096 to 65536
- up_weight: float32 [2, 768, 3072], P(None, 'fsdp'), may hold values from -0.21875 to 0.21875
- up_first: float32 [2, 768, 3072], P(None, 'fsdp'), may hold values from -512 to 512
- up_second: float32 [2, 768, 3072], P(None, 'fsdp'), may hold values from 4096 to 65536
- down_weight: float32 [2, 3072, 768], P(None, 'fsdp'), may hold values from -0.109375 to 0.109375
- down_first: float32 [2, 3072, 768], P(None, 'fsdp'), may hold values from -512 to 512
- down_second: float32 [2, 3072, 768], P(None, 'fsdp'), may hold values from 4096 to 65536
- norm_gains: float32 [2, 768, 4], P(None, 'fsdp'), may hold values from 0.5 to 1.5
- gains_first: float32 [2, 768, 4], P(None, 'fsdp'), may hold values from -512 to 512
- gains_second: float32 [2, 768, 4], P(None, 'fsdp'), may hold values from 4096 to 65536
Outputs:
- output: bfloat16 [32, 1024, 768], P(('dp', 'fsdp'))
- input_grad: float32 [32, 1024, 768], P(('dp', 'fsdp'))
- new_qkv_weight: float32 [2, 768, 2304], P(None, 'fsdp')
- new_qkv_first: float32 [2, 768, 2304], P(None, 'fsdp')
- new_qkv_second: float32 [2, 768, 2304], P(None, 'fsdp')
- new_proj_weight: float32 [2, 768, 768], P(None, 'fsdp')
- new_proj_first: float32 [2, 768, 768], P(None, 'fsdp')
- new_proj_second: float32 [2, 768, 768], P(None, 'fsdp')
- new_up_weight: float32 [2, 768, 3072], P(None, 'fsdp')
- new_up_first: float32 [2, 768, 3072], P(None, 'fsdp')
- new_up_second: float32 [2, 768, 3072], P(None, 'fsdp')
- new_down_weight: float32 [2, 3072, 768], P(None, 'fsdp')
- new_down_first: float32 [2, 3072, 768], P(None, 'fsdp')
- new_down_second: float32 [2, 3072, 768], P(None, 'fsdp')
- new_norm_gains: float32 [2, 768, 4], P(None, 'fsdp')
- new_gains_first: float32 [2, 768, 4], P(None, 'fsdp')
- new_gains_second: float32 [2, 768, 4], P(None, 'fsdp')
Inputs may be any that keep to these rules, and one draw needn't show every extreme that they name: `segments`: in each packed sequence the ids never fall, and each image holds 1 to 128 positions.
All inputs are finite; a program needn't handle non-finite values. No bound on the sum of `keep_mask` on one device may be relied on, other than what follows from the above.
Results may differ from a plain program's by a relative error of at most 0.035.
Values may be sent and summed in bfloat16 or wider, within the bound.
A program may use at most 512 MiB of HBM per device.

v0:
```python
import jax
import jax.numpy as jnp
from jax import lax
from jax.sharding import PartitionSpec as P

D = 768
HEADS = 12
HEAD_DIM = 64
STEP = 5


norm_eps = 1e-06
adam_eps = 1e-08


def layer_norm(values, gain):
    average = jnp.mean(values, axis=-1, keepdims=True)
    centred = values - average
    spread = jnp.mean(centred * centred, axis=-1, keepdims=True)
    return centred * lax.rsqrt(spread + norm_eps) * gain


def gelu_tanh(values):
    return jax.nn.gelu(values, approximate=True)


def allowed_pairs(seg_row, keep_row):
    positions = jnp.arange(seg_row.shape[0])
    diagonal = positions[:, None] == positions[None, :]
    return (seg_row[:, None] == seg_row[None, :]) & ((keep_row[None, :] == 1) | diagonal)


def key_window(start, span, length):
    reach = length // 8
    extent = min(length, span + 2 * reach)
    lower_key = max(0, min(start - reach, length - extent))
    return (lower_key, lower_key + extent)


def block_probs(query_block, keys_part, allowed_block, scale_factor):
    scores = (
        jnp.einsum("qhd,khd->hqk", query_block, keys_part, preferred_element_type=jnp.float32)
        * scale_factor
    )
    return jnp.where(allowed_block[None], scores, -1e30)


def attend_forward(queries, keys_all, values, allowed, span, scale_factor):
    length = queries.shape[0]
    outputs, peaks, totals = ([], [], [])
    for start in range(0, length, span):
        lower_key, upper_key = key_window(start, span, length)
        masked = block_probs(
            queries[start : start + span],
            keys_all[lower_key:upper_key],
            allowed[start : start + span, lower_key:upper_key],
            scale_factor,
        )
        peak = jnp.max(masked, axis=-1, keepdims=True)
        expo = jnp.exp(masked - peak)
        total = jnp.sum(expo, axis=-1, keepdims=True)
        probs = (expo / total).astype(jnp.bfloat16)
        outputs.append(
            jnp.einsum(
                "hqk,khd->qhd",
                probs,
                values[lower_key:upper_key],
                preferred_element_type=jnp.float32,
            ).astype(jnp.bfloat16)
        )
        peaks.append(peak)
        totals.append(total)
    return (jnp.concatenate(outputs, axis=0), peaks, totals)


def attend_backward(
    queries, keys_all, values, allowed, d_attended, peaks, totals, span, scale_factor
):
    length = queries.shape[0]
    d_keys = jnp.zeros(keys_all.shape, jnp.float32)
    d_values = jnp.zeros(values.shape, jnp.float32)
    d_query_parts = []
    for block_index, start in enumerate(range(0, length, span)):
        lower_key, upper_key = key_window(start, span, length)
        keys_part = keys_all[lower_key:upper_key]
        values_part = values[lower_key:upper_key]
        query_block = queries[start : start + span]
        d_block = d_attended[start : start + span]
        masked = block_probs(
            query_block, keys_part, allowed[start : start + span, lower_key:upper_key], scale_factor
        )
        probs_raw = jnp.exp(masked - peaks[block_index]) / totals[block_index]
        probs = probs_raw.astype(jnp.bfloat16)
        d_probs = jnp.einsum(
            "qhd,khd->hqk", d_block, values_part, preferred_element_type=jnp.float32
        )
        d_values = d_values.at[lower_key:upper_key].add(
            jnp.einsum("hqk,qhd->khd", probs, d_block, preferred_element_type=jnp.float32)
        )
        inner = jnp.sum(d_probs * probs_raw, axis=-1, keepdims=True)
        d_scores = (probs_raw * (d_probs - inner)).astype(jnp.bfloat16)
        d_query_parts.append(
            jnp.einsum("hqk,khd->qhd", d_scores, keys_part, preferred_element_type=jnp.float32)
            * scale_factor
        )
        d_keys = d_keys.at[lower_key:upper_key].add(
            jnp.einsum("hqk,qhd->khd", d_scores, query_block, preferred_element_type=jnp.float32)
            * scale_factor
        )
    return (jnp.concatenate(d_query_parts, axis=0), d_keys, d_values)


def layer_forward(hidden, gathered, allowed_rows, span, scale_factor):
    joint_mat, proj_mat, upper_mat, lower_mat, gain_set = gathered
    gains_wide = gain_set.astype(jnp.float32)
    normed = layer_norm(hidden, gains_wide[:, 0]).astype(jnp.bfloat16)
    mixed = jnp.dot(normed, joint_mat, preferred_element_type=jnp.float32)
    split = mixed.reshape(-1, 3, HEADS, HEAD_DIM)
    queries = layer_norm(split[:, 0], gains_wide[:, 2].reshape(HEADS, HEAD_DIM)).astype(
        jnp.bfloat16
    )
    keys_all = layer_norm(split[:, 1], gains_wide[:, 3].reshape(HEADS, HEAD_DIM)).astype(
        jnp.bfloat16
    )
    values = split[:, 2].astype(jnp.bfloat16)
    attended_rows, peak_rows, total_rows = ([], [], [])
    row_out, row_peaks, row_totals = attend_forward(
        queries, keys_all, values, allowed_rows[0], span, scale_factor
    )
    attended_rows.append(row_out)
    peak_rows.append(row_peaks)
    total_rows.append(row_totals)
    attended = attended_rows[0].reshape(-1, HEADS * HEAD_DIM)
    middle = hidden + jnp.dot(attended, proj_mat, preferred_element_type=jnp.float32)
    normed_two = layer_norm(middle, gains_wide[:, 1]).astype(jnp.bfloat16)
    before = jnp.dot(normed_two, upper_mat, preferred_element_type=jnp.float32)
    active = gelu_tanh(before).astype(jnp.bfloat16)
    result = middle + jnp.dot(active, lower_mat, preferred_element_type=jnp.float32)
    saved = (
        hidden,
        normed,
        split,
        queries,
        keys_all,
        values,
        peak_rows,
        total_rows,
        attended,
        middle,
        normed_two,
        before,
        active,
    )
    return (result, saved)


def layer_backward(d_hidden, saved, gathered, allowed_rows, span, scale_factor):
    joint_mat, proj_mat, upper_mat, lower_mat, gain_set = gathered
    gains_wide = gain_set.astype(jnp.float32)
    (
        hidden,
        normed,
        split,
        queries,
        keys_all,
        values,
        peak_rows,
        total_rows,
        attended,
        middle,
        normed_two,
        before,
        active,
    ) = saved
    d_branch = d_hidden.astype(jnp.bfloat16)
    d_lower = jnp.einsum("nf,nd->fd", active, d_branch, preferred_element_type=jnp.float32)
    d_active = jnp.einsum("nd,fd->nf", d_branch, lower_mat, preferred_element_type=jnp.float32)
    unused_gelu, gelu_back = jax.vjp(gelu_tanh, before)
    d_before = gelu_back(d_active)[0].astype(jnp.bfloat16)
    d_upper = jnp.einsum("nd,nf->df", normed_two, d_before, preferred_element_type=jnp.float32)
    d_normed_two = jnp.einsum("nf,df->nd", d_before, upper_mat, preferred_element_type=jnp.float32)
    unused_two, norm_two_back = jax.vjp(layer_norm, middle, gains_wide[:, 1])
    d_middle_part, d_gain_two = norm_two_back(d_normed_two)
    d_middle = d_hidden + d_middle_part
    d_attn = d_middle.astype(jnp.bfloat16)
    d_proj = jnp.einsum("nd,ne->de", attended, d_attn, preferred_element_type=jnp.float32)
    d_attended = jnp.einsum(
        "ne,de->nd", d_attn, proj_mat, preferred_element_type=jnp.float32
    ).astype(jnp.bfloat16)
    d_attended = d_attended.reshape(-1, HEADS, HEAD_DIM)
    query_parts, key_parts, value_parts = ([], [], [])
    d_q_row, d_k_row, d_v_row = attend_backward(
        queries,
        keys_all,
        values,
        allowed_rows[0],
        d_attended,
        peak_rows[0],
        total_rows[0],
        span,
        scale_factor,
    )
    query_parts.append(d_q_row)
    key_parts.append(d_k_row)
    value_parts.append(d_v_row)
    d_queries = query_parts[0]
    d_keys = key_parts[0]
    d_values = value_parts[0]
    unused_query, query_back = jax.vjp(
        layer_norm, split[:, 0], gains_wide[:, 2].reshape(HEADS, HEAD_DIM)
    )
    d_q_raw, d_gain_query = query_back(d_queries)
    unused_key, key_back = jax.vjp(
        layer_norm, split[:, 1], gains_wide[:, 3].reshape(HEADS, HEAD_DIM)
    )
    d_k_raw, d_gain_key = key_back(d_keys)
    d_mixed = (
        jnp.stack([d_q_raw, d_k_raw, d_values], axis=1)
        .reshape(d_hidden.shape[0], -1)
        .astype(jnp.bfloat16)
    )
    d_joint = jnp.einsum("nd,ne->de", normed, d_mixed, preferred_element_type=jnp.float32)
    d_normed = jnp.einsum("ne,de->nd", d_mixed, joint_mat, preferred_element_type=jnp.float32)
    unused_one, norm_one_back = jax.vjp(layer_norm, hidden, gains_wide[:, 0])
    d_input_part, d_gain_one = norm_one_back(d_normed)
    d_gains = jnp.stack(
        [d_gain_one, d_gain_two, d_gain_query.reshape(-1), d_gain_key.reshape(-1)], axis=1
    )
    return (d_middle + d_input_part, (d_joint, d_proj, d_upper, d_lower, d_gains))


def local_shards(masters, layer_index):
    return tuple((weight_arr[layer_index].astype(jnp.bfloat16) for weight_arr in masters))


def per_device(
    tokens,
    cotangent,
    segments,
    keep_mask,
    qkv_weight,
    qkv_first,
    qkv_second,
    proj_weight,
    proj_first,
    proj_second,
    up_weight,
    up_first,
    up_second,
    down_weight,
    down_first,
    down_second,
    norm_gains,
    gains_first,
    gains_second,
):
    masters = (qkv_weight, proj_weight, up_weight, down_weight, norm_gains)
    firsts = (qkv_first, proj_first, up_first, down_first, gains_first)
    seconds = (qkv_second, proj_second, up_second, down_second, gains_second)
    packs, length, width = tokens.shape
    layers = qkv_weight.shape[0]
    span = min(512, length)
    scale_factor = HEAD_DIM ** (-0.5)
    allowed_rows = [allowed_pairs(segments[0], keep_mask[0])]
    hidden = tokens.reshape(-1, width).astype(jnp.float32)
    stored, held = ([], [])
    for layer_index in range(layers):
        shards = local_shards(masters, layer_index)
        gathered = (
            lax.all_gather(shards[0], "fsdp", axis=0, tiled=True),
            lax.all_gather(shards[1], "fsdp", axis=0, tiled=True),
            lax.all_gather(shards[2], "fsdp", axis=0, tiled=True),
            lax.all_gather(shards[3], "fsdp", axis=0, tiled=True),
            lax.all_gather(shards[4], "fsdp", axis=0, tiled=True),
        )
        hidden, saved = layer_forward(hidden, gathered, allowed_rows, span, scale_factor)
        stored.append(saved)
        held.append(gathered)
    output = hidden.astype(jnp.bfloat16).reshape(tokens.shape)
    d_hidden = cotangent.reshape(-1, width).astype(jnp.float32)
    layer_grads = [None] * layers
    for layer_index in reversed(range(layers)):
        shards = local_shards(masters, layer_index)
        gathered = (
            lax.all_gather(shards[0], "fsdp", axis=0, tiled=True),
            lax.all_gather(shards[1], "fsdp", axis=0, tiled=True),
            lax.all_gather(shards[2], "fsdp", axis=0, tiled=True),
            lax.all_gather(shards[3], "fsdp", axis=0, tiled=True),
            lax.all_gather(shards[4], "fsdp", axis=0, tiled=True),
        )
        d_hidden, grads = layer_backward(
            d_hidden, stored[layer_index], gathered, allowed_rows, span, scale_factor
        )
        layer_grads[layer_index] = grads
    stacked = tuple(
        (
            jnp.stack([layer_grads[layer_index][kind_index] for layer_index in range(layers)])
            for kind_index in range(5)
        )
    )
    shares = (
        lax.psum_scatter(
            stacked[0].astype(jnp.bfloat16), "fsdp", scatter_dimension=1, tiled=True
        ).astype(jnp.float32),
        lax.psum_scatter(
            stacked[1].astype(jnp.bfloat16), "fsdp", scatter_dimension=1, tiled=True
        ).astype(jnp.float32),
        lax.psum_scatter(
            stacked[2].astype(jnp.bfloat16), "fsdp", scatter_dimension=1, tiled=True
        ).astype(jnp.float32),
        lax.psum_scatter(
            stacked[3].astype(jnp.bfloat16), "fsdp", scatter_dimension=1, tiled=True
        ).astype(jnp.float32),
        lax.psum_scatter(
            stacked[4].astype(jnp.bfloat16), "fsdp", scatter_dimension=1, tiled=True
        ).astype(jnp.float32),
    )
    summed = (
        lax.psum(shares[0].astype(jnp.bfloat16), "dp").astype(jnp.float32),
        lax.psum(shares[1].astype(jnp.bfloat16), "dp").astype(jnp.float32),
        lax.psum(shares[2].astype(jnp.bfloat16), "dp").astype(jnp.float32),
        lax.psum(shares[3].astype(jnp.bfloat16), "dp").astype(jnp.float32),
        lax.psum(shares[4].astype(jnp.bfloat16), "dp").astype(jnp.float32),
    )
    corr_one = 1.0 - 0.5**STEP
    corr_two = 1.0 - 0.5**STEP
    updated = []
    for kind_index in range(5):
        grad_now = summed[kind_index]
        first_new = 0.5 * firsts[kind_index] + 0.5 * grad_now
        second_new = 0.5 * seconds[kind_index] + 0.5 * grad_now * grad_now
        rate_now = 0.5 if kind_index == 4 else D ** (-0.5)
        decay_now = 0.0 if kind_index == 4 else 0.1
        weight_old = masters[kind_index]
        weight_new = weight_old - rate_now * (
            first_new / corr_one / (jnp.sqrt(second_new / corr_two) + adam_eps)
            + decay_now * weight_old
        )
        updated.append((weight_new, first_new, second_new))
    input_grad = d_hidden.reshape(tokens.shape)
    return (
        output,
        input_grad,
        updated[0][0],
        updated[0][1],
        updated[0][2],
        updated[1][0],
        updated[1][1],
        updated[1][2],
        updated[2][0],
        updated[2][1],
        updated[2][2],
        updated[3][0],
        updated[3][1],
        updated[3][2],
        updated[4][0],
        updated[4][1],
        updated[4][2],
    )


def solution(mesh):
    placed = (
        P(("dp", "fsdp"), None, None),
        P(("dp", "fsdp"), None, None),
        P(("dp", "fsdp"), None),
        P(("dp", "fsdp"), None),
        P(None, "fsdp", None),
        P(None, "fsdp", None),
        P(None, "fsdp", None),
        P(None, "fsdp", None),
        P(None, "fsdp", None),
        P(None, "fsdp", None),
        P(None, "fsdp", None),
        P(None, "fsdp", None),
        P(None, "fsdp", None),
        P(None, "fsdp", None),
        P(None, "fsdp", None),
        P(None, "fsdp", None),
        P(None, "fsdp", None),
        P(None, "fsdp", None),
        P(None, "fsdp", None),
    )
    return jax.shard_map(
        per_device,
        mesh=mesh,
        in_specs=placed,
        out_specs=(
            P(("dp", "fsdp"), None, None),
            P(("dp", "fsdp"), None, None),
            P(None, "fsdp", None),
            P(None, "fsdp", None),
            P(None, "fsdp", None),
            P(None, "fsdp", None),
            P(None, "fsdp", None),
            P(None, "fsdp", None),
            P(None, "fsdp", None),
            P(None, "fsdp", None),
            P(None, "fsdp", None),
            P(None, "fsdp", None),
            P(None, "fsdp", None),
            P(None, "fsdp", None),
            P(None, "fsdp", None),
            P(None, "fsdp", None),
            P(None, "fsdp", None),
        ),
        check_vma=False,
    )
```

profile of v0, /device:TPU:0, one launch (start us, length us, event | category | flops | bytes accessed | tf_op | source)
XLA Modules:
  0.0 1156.5 jit_solution(5405106433137993365)
XLA Ops:
  46.1 5.8 copy.45
  51.9 9.4 fusion.234
  66.5 9.4 fusion.181
  75.8 7.8 fusion.184
  83.6 23.5 %fusion.235 = (f32[12,512]{1,0:T(8,128)S(1)}, f32[12,512,768]{2,1,0:T(8,128)}) fusion(f32[12,512,768]{2,1,0:T(8,128)} %fusion.181, pred[512,768]{1,0:T(8,128)(4,1)S(1)} %copy-done.91), kind=kOutput, calls=%fused_computation.379 | output fusion | flops 28312320 | bytes 38166528 | tf_op jit(solution)/shard_map/sub | solution.py:60
  107.1 23.4 %fusion.236 = (f32[12,512]{1,0:T(8,128)S(1)}, f32[12,512,768]{2,1,0:T(8,128)}) fusion(f32[12,512,768]{2,1,0:T(8,128)} %fusion.184, pred[512,768]{1,0:T(8,128)(4,1)S(1)} %get-tuple-element.220), kind=kOutput, calls=%fused_computation.380 | output fusion | flops 28312320 | bytes 38166528 | tf_op jit(solution)/shard_map/sub | solution.py:60
  130.5 10.7 fusion.159
  141.2 8.6 fusion.162
  156.1 11.1 fusion.51
  167.3 12.2 %fusion.238 = (f32[1024]{0:T(1024)S(1)}, f32[1024,768]{0,1:T(8,128)S(1)}) fusion(f32[1024,768]{0,1:T(8,128)S(1)} %copy-done.6, bf16[1,3072,768]{2,1,0:T(8,128)(2,1)} %all-gather.25.cloned.1.call-done, f32[1024,3072]{1,0:T(8,128)} %fusion.51), kind=kOutput, calls=%fused_computation.382 | convolution fusion | flops 4861721600 | bytes 23597056 | tf_op jit(solution)/shard_map/dot_general | solution.py:138
  181.7 7.3 fusion.87
  196.1 8.2 fusion.175
  204.3 7.9 fusion.178
  212.1 23.2 %fusion.239 = (f32[12,512]{1,0:T(8,128)S(1)}, f32[12,512,768]{2,1,0:T(8,128)}) fusion(f32[12,512,768]{2,1,0:T(8,128)} %fusion.175, pred[512,768]{1,0:T(8,128)(4,1)S(1)} %copy-done.92), kind=kOutput, calls=%fused_computation.383 | output fusion | flops 28312320 | bytes 38166528 | tf_op jit(solution)/shard_map/sub | solution.py:60
  235.4 23.6 %fusion.240 = (f32[12,512]{1,0:T(8,128)S(1)}, f32[12,512,768]{2,1,0:T(8,128)}) fusion(f32[12,512,768]{2,1,0:T(8,128)} %fusion.178, pred[512,768]{1,0:T(8,128)(4,1)S(1)} %get-tuple-element.220), kind=kOutput, calls=%fused_computation.384 | output fusion | flops 28312320 | bytes 38166528 | tf_op jit(solution)/shard_map/sub | solution.py:60
  259.0 8.5 fusion.153
  282.0 10.9 fusion.43
  292.9 15.9 %fusion.21 = bf16[1024,3072]{1,0:T(8,128)(2,1)S(1)} fusion(f32[1024,3072]{1,0:T(8,128)} %fusion.43, bf16[1,3072,768]{2,1,0:T(8,128)(2,1)} %all-gather.33.cloned.1.call-done, bf16[1,1024,768]{2,1,0:T(8,128)(2,1)} %param.36), kind=kOutput, calls=%fused_computation.45 | convolution fusion | flops 4894752768 | bytes 25165824 | tf_op jit(solution)/shard_map/nd,fd->nf/dot_general | solution.py:177
  308.8 6.1 multiply_reduce_fusion.6
  328.0 15.0 %multiply_reduce_fusion.3 = (f32[12,512]{1,0:T(8,128)S(1)}, f32[12,512,768]{2,1,0:T(8,128)}) fusion(f32[12,512,768]{2,1,0:T(8,128)} %get-tuple-element.237, f32[12,512]{1,0:T(8,128)S(1)} %copy-done.135, bf16[512,12,64]{0,2,1:T(8,128)(2,1)S(1)} %bitcast.379, bf16[1024,3,12,64]{0,3,2,1:T(8,128)(2,1)S(1)} %bitcast.359), kind=kOutput, calls=%fused_computation.11 | convolution fusion | flops 618129408 | bytes 39772160 | tf_op jit(solution)/shard_map/qhd,khd->hqk/dot_general | solution.py:94
  343.0 12.9 %multiply_convert_fusion.3 = bf16[12,512,768]{2,1,0:T(8,128)(2,1)S(1)} fusion(f32[12,512,768]{2,1,0:T(8,128)} %get-tuple-element.242, f32[12,512]{1,0:T(8,128)S(1)} %get-tuple-element.241, f32[12,512,768]{2,1,0:T(8,128)} %get-tuple-element.237, f32[12,512]{1,0:T(8,128)S(1)} %copy-done.135), kind=kLoop, calls=%fused_computation.10 | loop fusion | flops 18874368 | bytes 47235072 | tf_op jit(solution)/shard_map/convert_element_type | solution.py:101
  362.8 15.1 %multiply_reduce_fusion.2 = (f32[12,512]{1,0:T(8,128)S(1)}, f32[12,512,768]{2,1,0:T(8,128)}) fusion(f32[12,512,768]{2,1,0:T(8,128)} %get-tuple-element.235, f32[12,512]{1,0:T(8,128)S(1)} %copy-done.133, bf16[512,12,64]{0,2,1:T(8,128)(2,1)S(1)} %bitcast.376, bf16[1024,3,12,64]{0,3,2,1:T(8,128)(2,1)S(1)} %bitcast.359), kind=kOutput, calls=%fused_computation.9 | convolution fusion | flops 618129408 | bytes 39772160 | tf_op jit(solution)/shard_map/qhd,khd->hqk/dot_general | solution.py:94
  377.9 8.4 fusion.107
  387.4 12.8 %multiply_convert_fusion.2 = bf16[12,512,768]{2,1,0:T(8,128)(2,1)S(1)} fusion(f32[12,512,768]{2,1,0:T(8,128)} %get-tuple-element.244, f32[12,512]{1,0:T(8,128)S(1)} %get-tuple-element.243, f32[12,512,768]{2,1,0:T(8,128)} %get-tuple-element.235, f32[12,512]{1,0:T(8,128)S(1)} %copy-done.133), kind=kLoop, calls=%fused_computation.8 | loop fusion | flops 18874368 | bytes 47235072 | tf_op jit(solution)/shard_map/convert_element_type | solution.py:101
  430.2 18.3 %fusion.14 = bf16[1024,3072]{1,0:T(8,128)(2,1)} fusion(f32[1024,3072]{1,0:T(8,128)} %fusion.51, bf16[1,3072,768]{2,1,0:T(8,128)(2,1)S(1)} %bitcast.384, f32[1024,768]{0,1:T(8,128)S(1)} %add_add_fusion.11), kind=kOutput, calls=%fused_computation.38 | convolution fusion | flops 4895539200 | bytes 26738688 | tf_op jit(solution)/shard_map/nd,fd->nf/dot_general | solution.py:177
  448.5 8.3 multiply_reduce_fusion.10
  469.8 12.2 %multiply_reduce_fusion.1 = (f32[12,512]{1,0:T(8,128)S(1)}, f32[12,512,768]{2,1,0:T(8,128)}) fusion(f32[12,512,768]{2,1,0:T(8,128)} %get-tuple-element.229, f32[12,512]{1,0:T(8,128)S(1)} %copy-done.131, bf16[512,12,64]{0,2,1:T(8,128)(2,1)S(1)} %bitcast.381, bf16[1024,3,12,64]{0,3,2,1:T(8,128)(2,1)} %get-tuple-element.224), kind=kOutput, calls=%fused_computation.7 | convolution fusion | flops 618129408 | bytes 39763968 | tf_op jit(solution)/shard_map/qhd,khd->hqk/dot_general | solution.py:94
  482.0 12.8 %multiply_convert_fusion.1 = bf16[12,512,768]{2,1,0:T(8,128)(2,1)S(1)} fusion(f32[12,512,768]{2,1,0:T(8,128)} %get-tuple-element.249, f32[12,512]{1,0:T(8,128)S(1)} %get-tuple-element.248, f32[12,512,768]{2,1,0:T(8,128)} %get-tuple-element.229, f32[12,512]{1,0:T(8,128)S(1)} %copy-done.131), kind=kLoop, calls=%fused_computation.6 | loop fusion | flops 18874368 | bytes 47235072 | tf_op jit(solution)/shard_map/convert_element_type | solution.py:101
  505.7 15.2 %multiply_reduce_fusion = (f32[12,512]{1,0:T(8,128)S(1)}, f32[12,512,768]{2,1,0:T(8,128)}) fusion(f32[12,512,768]{2,1,0:T(8,128)} %get-tuple-element.227, f32[12,512]{1,0:T(8,128)S(1)} %copy-done.129, bf16[512,12,64]{0,2,1:T(8,128)(2,1)S(1)} %bitcast.374, bf16[1024,3,12,64]{0,3,2,1:T(8,128)(2,1)} %get-tuple-element.224), kind=kOutput, calls=%fused_computation.5 | convolution fusion | flops 618129408 | bytes 39763968 | tf_op jit(solution)/shard_map/qhd,khd->hqk/dot_general | solution.py:94
  520.9 16.5 %multiply_convert_fusion = bf16[12,512,768]{2,1,0:T(8,128)(2,1)} fusion(f32[12,512,768]{2,1,0:T(8,128)} %get-tuple-element.251, f32[12,512]{1,0:T(8,128)S(1)} %get-tuple-element.250, f32[12,512,768]{2,1,0:T(8,128)} %get-tuple-element.227, f32[12,512]{1,0:T(8,128)S(1)} %copy-done.129), kind=kLoop, calls=%fused_computation.4 | loop fusion | flops 18874368 | bytes 47235072 | tf_op jit(solution)/shard_map/convert_element_type | solution.py:101
  537.5 6.8 convolution_multiply_fusion
  556.7 8.0 fusion.110
  578.8 13.8 %fusion.73 = bf16[1,3072,768]{2,1,0:T(8,128)(2,1)} fusion(f32[1024,768]{0,1:T(8,128)} %copy-done.13, f32[1024,3072]{1,0:T(8,128)} %fusion.51), kind=kOutput, calls=%fused_computation.132 | convolution fusion | flops 4863295488 | bytes 20447232 | tf_op jit(solution)/shard_map/nf,nd->fd/dot_general | solution.py:176
  592.6 11.9 %fusion.74 = bf16[1,3072,768]{2,1,0:T(8,128)(2,1)} fusion(bf16[1,1024,768]{2,1,0:T(8,128)(2,1)S(1)} %copy-done.53, f32[1024,3072]{1,0:T(8,128)} %fusion.43), kind=kOutput, calls=%fused_computation.133 | convolution fusion | flops 4862509056 | bytes 18874368 | tf_op jit(solution)/shard_map/nf,nd->fd/dot_general | solution.py:176
  604.5 8.4 pad_maximum_fusion.1
  613.6 10.3 fusion.72
  623.9 11.2 fusion.71
  635.1 8.4 pad_maximum_fusion
  644.6 6.8 fusion.92
  656.0 7.1 reduce-scatter.12.cloned.1.call-done
  663.1 11.0 fusion.136
  675.6 7.1 add_bitcast_fusion
  687.6 45.7 %psum.39 = bf16[2,384,4]{1,2,0:T(4,128)(2,1)S(1)} all-reduce(bf16[2,384,4]{1,2,0:T(4,128)(2,1)S(1)} %copy.57), channel_id=1, replica_groups=mesh['dp'=16,'fsdp'=2] {'dp'}, use_global_device_ids=true, to_apply=%region_61.62 | all-reduce | flops 3072 | bytes 12288 | tf_op jit(solution)/shard_map/psum | solution.py:323
  733.9 346.8 %all-reduce.7.cloned.1.call-done = (bf16[2,384,2304]{2,1,0:T(8,128)(2,1)}, bf16[2,384,768]{2,1,0:T(8,128)(2,1)}, bf16[2,384,3072]{2,1,0:T(8,128)(2,1)}, bf16[2,1536,768]{2,1,0:T(8,128)(2,1)}) async-done(((bf16[2,384,2304]{2,1,0:T(8,128)(2,1)}, bf16[2,384,768]{2,1,0:T(8,128)(2,1)}, bf16[2,384,3072]{2,1,0:T(8,128)(2,1)}, bf16[2,1536,768]{2,1,0:T(8,128)(2,1)}), (bf16[2,384,2304]{2,1,0:T(8,128)(2,1)}, ...) | async-done | bytes 14155792 | tf_op jit(solution)/shard_map/psum | solution.py:319
  1080.7 6.9 multiply_subtract_fusion.3
  1087.6 18.0 %multiply_subtract_fusion.2 = (f32[2,384,2304]{2,1,0:T(8,128)}, f32[2,384,2304]{2,1,0:T(8,128)}, f32[2,384,2304]{2,1,0:T(8,128)}) fusion(f32[2,384,2304]{2,1,0:T(8,128)} %param.39, bf16[2,384,2304]{2,1,0:T(8,128)(2,1)} %get-tuple-element.181, f32[2,384,2304]{2,1,0:T(8,128)} %param.40, f32[2,384,2304]{2,1,0:T(8,128)} %param.41), kind=kLoop, calls=%fused_computation.75 | loop fusion | flops 26542080 | bytes 46006272 | tf_op jit(solution)/shard_map/sub | solution.py:335
  1105.6 20.7 %multiply_subtract_fusion.1 = (f32[2,384,3072]{2,1,0:T(8,128)}, f32[2,384,3072]{2,1,0:T(8,128)}, f32[2,384,3072]{2,1,0:T(8,128)}) fusion(f32[2,384,3072]{2,1,0:T(8,128)S(1)} %bitcast.339, bf16[2,384,3072]{2,1,0:T(8,128)(2,1)} %get-tuple-element.183, f32[2,384,3072]{2,1,0:T(8,128)} %param.46, f32[2,384,3072]{2,1,0:T(8,128)} %param.47), kind=kLoop, calls=%fused_computation.56 | loop fusion | flops 35389440 | bytes 61341696 | tf_op jit(solution)/shard_map/sub | solution.py:335
  1126.3 23.4 %multiply_subtract_fusion = (f32[2,1536,768]{2,1,0:T(8,128)}, f32[2,1536,768]{2,1,0:T(8,128)}, f32[2,1536,768]{2,1,0:T(8,128)}) fusion(f32[2,1536,768]{2,1,0:T(8,128)} %param.48, bf16[2,1536,768]{2,1,0:T(8,128)(2,1)} %get-tuple-element.184, f32[2,1536,768]{2,1,0:T(8,128)} %param.49, f32[2,1536,768]{2,1,0:T(8,128)} %param.50), kind=kLoop, calls=%fused_computation.55 | loop fusion | flops 35389440 | bytes 61341696 | tf_op jit(solution)/shard_map/sub | solution.py:335
  (542 shorter events, 186.6 us)
Async XLA Ops:
  7.2 38.9 %all-gather.19.cloned.1.call-start = ((), (), s32[]{:S(2)}) async-start(), calls=%async_computation.9 | async-start | bytes 5308416 | tf_op jit(solution)/shard_map/all_gather | solution.py:270
  12.6 137.5 %all-gather.21.cloned.1.call-start = ((), (), s32[]{:S(2)}) async-start(), calls=%async_computation.10 | async-start | bytes 1769472 | tf_op jit(solution)/shard_map/all_gather | solution.py:271
  14.6 141.5 %all-gather.23.cloned.1.call-start = ((), (), s32[]{:S(2)}) async-start(), calls=%async_computation.11 | async-start | bytes 7077888 | tf_op jit(solution)/shard_map/all_gather | solution.py:272
  21.6 145.7 %all-gather.25.cloned.1.call-start = ((), (), s32[]{:S(2)}) async-start(), calls=%async_computation.12 | async-start | bytes 7077888 | tf_op jit(solution)/shard_map/all_gather | solution.py:273
  29.6 152.1 %all-gather.27.cloned.1.call-start = ((), (), s32[]{:S(2)}) async-start(), calls=%async_computation.13 | async-start | bytes 5308416 | tf_op jit(solution)/shard_map/all_gather | solution.py:270
  30.2 246.9 %all-gather.29.cloned.1.call-start = ((), (), s32[]{:S(2)}) async-start(), calls=%async_computation.14 | async-start | bytes 1769472 | tf_op jit(solution)/shard_map/all_gather | solution.py:271
  30.7 251.0 %all-gather.31.cloned.1.call-start = ((), (), s32[]{:S(2)}) async-start(), calls=%async_computation.15 | async-start | bytes 7077888 | tf_op jit(solution)/shard_map/all_gather | solution.py:272
  31.5 261.4 %all-gather.33.cloned.1.call-start = ((), (), s32[]{:S(2)}) async-start(), calls=%async_computation.16 | async-start | bytes 7077888 | tf_op jit(solution)/shard_map/all_gather | solution.py:273
  32.3 623.7 %reduce-scatter.10.cloned.1.call-start = ((), (), s32[]{:S(2)}) async-start(), calls=%async_computation.6 | async-start | bytes 3538944 | tf_op jit(solution)/shard_map/reduce_scatter | solution.py:305
  38.0 13.8 %copy-start.116 = (f32[768]{0:T(1024)}, f32[768]{0:T(1024)S(1)}, u32[]{:S(2)}) copy-start(f32[768]{0:T(1024)S(1)} %get-tuple-element.180) | copy-start | bytes 9220
  38.0 118.1 %copy-start.83 = (f32[768]{0:T(1024)}, f32[768]{0:T(1024)S(1)}, u32[]{:S(2)}) copy-start(f32[768]{0:T(1024)S(1)} %get-tuple-element.177) | copy-start | bytes 9220
  42.4 107.7 %copy-start.2 = (bf16[1,1024,768]{1,2,0:T(8,128)(2,1)}, bf16[1,1024,768]{1,2,0:T(8,128)(2,1)S(1)}, u32[]{:S(2)}) copy-start(bf16[1,1024,768]{1,2,0:T(8,128)(2,1)S(1)} %copy.44) | copy-start | bytes 4718596
  107.1 23.4 %copy-start.128 = (f32[12,512]{1,0:T(8,128)}, f32[12,512]{1,0:T(8,128)S(1)}, u32[]{:S(2)}) copy-start(f32[12,512]{1,0:T(8,128)S(1)} %get-tuple-element.226) | copy-start | bytes 73732
  153.5 13.8 %copy-start.76 = (f32[1024]{0:T(1024)}, f32[1024]{0:T(1024)S(1)}, u32[]{:S(2)}) copy-start(f32[1024]{0:T(1024)S(1)} %broadcast_multiply_fusion.6) | copy-start | bytes 12292
  235.4 23.6 %copy-start.132 = (f32[12,512]{1,0:T(8,128)}, f32[12,512]{1,0:T(8,128)S(1)}, u32[]{:S(2)}) copy-start(f32[12,512]{1,0:T(8,128)S(1)} %get-tuple-element.234) | copy-start | bytes 73732
  259.0 12.1 %copy-start.27 = (f32[12,512,768]{2,1,0:T(8,128)S(1)}, f32[12,512,768]{2,1,0:T(8,128)}, u32[]{:S(2)}) copy-start(f32[12,512,768]{2,1,0:T(8,128)} %get-tuple-element.237) | copy-start | bytes 56623108
  281.3 33.7 %copy-start.4 = (f32[1024,768]{0,1:T(8,128)}, f32[1024,768]{0,1:T(8,128)S(1)}, u32[]{:S(2)}) copy-start(f32[1024,768]{0,1:T(8,128)S(1)} %get-tuple-element.239) | copy-start | bytes 9437188
  281.3 33.6 %copy-start.79 = (f32[1024]{0:T(1024)}, f32[1024]{0:T(1024)S(1)}, u32[]{:S(2)}) copy-start(f32[1024]{0:T(1024)S(1)} %broadcast_multiply_fusion.4) | copy-start | bytes 12292
  281.7 33.2 %copy-start.89 = (f32[1024]{0:T(1024)}, f32[1024]{0:T(1024)S(1)}, u32[]{:S(2)}) copy-start(f32[1024]{0:T(1024)S(1)} %fusion.209) | copy-start | bytes 12292
  292.9 15.9 %copy-start.38 = (bf16[1,768,3072]{2,1,0:T(8,128)(2,1)S(1)}, bf16[1,768,3072]{2,1,0:T(8,128)(2,1)}, u32[]{:S(2)}) copy-start(bf16[1,768,3072]{2,1,0:T(8,128)(2,1)} %all-gather.31.cloned.1.call-done) | copy-start | bytes 14155780
  343.0 13.0 %copy-start.19 = (bf16[1024,12,64]{0,2,1:T(8,128)(2,1)S(1)}, bf16[1024,12,64]{0,2,1:T(8,128)(2,1)}, u32[]{:S(2)}) copy-start(bf16[1024,12,64]{0,2,1:T(8,128)(2,1)} %copy-done.18) | copy-start | bytes 4718596
  377.9 26.5 %slice-start = ((s8[9437184]{0:T(1024)(128)(4,1)}), s8[4194304]{0:T(1024)(128)(4,1)S(1)}, s32[]{:S(2)}) async-start(s8[9437184]{0:T(1024)(128)(4,1)} %bitcast.327), calls=%async_computation.19 | async-start | bytes 8388608
  377.9 26.5 %slice-start.1 = ((s8[9437184]{0:T(1024)(128)(4,1)}), s8[4194304]{0:T(1024)(128)(4,1)S(1)}, s32[]{:S(2)}) async-start(s8[9437184]{0:T(1024)(128)(4,1)} %bitcast.327), calls=%async_computation.20 | async-start | bytes 8388608
  387.4 16.9 %slice-start.2 = ((s8[9437184]{0:T(1024)(128)(4,1)}), s8[1048576]{0:T(1024)(128)(4,1)S(1)}, s32[]{:S(2)}) async-start(s8[9437184]{0:T(1024)(128)(4,1)} %bitcast.327), calls=%async_computation.21 | async-start | bytes 2097152
  428.6 19.9 %slice-start.22 = ((s8[4718592]{0:T(1024)(128)(4,1)}), s8[4194304]{0:T(1024)(128)(4,1)S(1)}, s32[]{:S(2)}) async-start(s8[4718592]{0:T(1024)(128)(4,1)} %bitcast.356), calls=%async_computation.41 | async-start | bytes 8388608
  430.1 27.6 %copy-start.13 = (f32[1024,768]{0,1:T(8,128)}, f32[1024,768]{0,1:T(8,128)S(1)}, u32[]{:S(2)}) copy-start(f32[1024,768]{0,1:T(8,128)S(1)} %add_add_fusion.11) | copy-start | bytes 9437188
  430.1 18.4 %copy-start.7 = (f32[1024,768]{0,1:T(8,128)S(1)}, f32[1024,768]{0,1:T(8,128)}, u32[]{:S(2)}) copy-start(f32[1024,768]{0,1:T(8,128)} %copy-done.5) | copy-start | bytes 9437188
  430.1 18.3 %slice-start.23 = ((s8[4718592]{0:T(1024)(128)(4,1)}), s8[524288]{0:T(1024)(128)(4,1)S(1)}, s32[]{:S(2)}) async-start(s8[4718592]{0:T(1024)(128)(4,1)} %bitcast.356), calls=%async_computation.42 | async-start | bytes 1048576
  430.1 18.3 %copy-start.77 = (f32[1024]{0:T(1024)S(1)}, f32[1024]{0:T(1024)}, u32[]{:S(2)}) copy-start(f32[1024]{0:T(1024)} %copy-done.76) | copy-start | bytes 12292
  430.1 18.3 %copy-start.84 = (f32[768]{0:T(1024)S(1)}, f32[768]{0:T(1024)}, u32[]{:S(2)}) copy-start(f32[768]{0:T(1024)} %copy-done.83) | copy-start | bytes 9220
  430.2 18.3 %copy-start.87 = (f32[1024]{0:T(1024)S(1)}, f32[1024]{0:T(1024)}, u32[]{:S(2)}) copy-start(f32[1024]{0:T(1024)} %copy-done.86) | copy-start | bytes 12292
  482.0 12.8 %copy-start.17 = (bf16[1024,12,64]{0,2,1:T(8,128)(2,1)S(1)}, bf16[1024,12,64]{0,2,1:T(8,128)(2,1)}, u32[]{:S(2)}) copy-start(bf16[1024,12,64]{0,2,1:T(8,128)(2,1)} %copy-done.16) | copy-start | bytes 4718596
  502.5 153.4 %reduce-scatter.8.cloned.1.call-start = ((), (), s32[]{:S(2)}) async-start(), calls=%async_computation.5 | async-start | bytes 10616832 | tf_op jit(solution)/shard_map/reduce_scatter | solution.py:302
  505.7 38.5 %slice-start.3 = ((s8[9437184]{0:T(1024)(128)(4,1)}), s8[4194304]{0:T(1024)(128)(4,1)S(1)}, s32[]{:S(2)}) async-start(s8[9437184]{0:T(1024)(128)(4,1)} %bitcast.334), calls=%async_computation.22 | async-start | bytes 8388608
  505.7 38.5 %slice-start.4 = ((s8[9437184]{0:T(1024)(128)(4,1)}), s8[1048576]{0:T(1024)(128)(4,1)S(1)}, s32[]{:S(2)}) async-start(s8[9437184]{0:T(1024)(128)(4,1)} %bitcast.334), calls=%async_computation.23 | async-start | bytes 2097152
  520.9 23.4 %slice-start.5 = ((s8[9437184]{0:T(1024)(128)(4,1)}), s8[4194304]{0:T(1024)(128)(4,1)S(1)}, s32[]{:S(2)}) async-start(s8[9437184]{0:T(1024)(128)(4,1)} %bitcast.334), calls=%async_computation.24 | async-start | bytes 8388608
  578.7 13.9 %copy-start.53 = (bf16[1,1024,768]{2,1,0:T(8,128)(2,1)S(1)}, bf16[1,1024,768]{2,1,0:T(8,128)(2,1)}, u32[]{:S(2)}) copy-start(bf16[1,1024,768]{2,1,0:T(8,128)(2,1)} %param.36) | copy-start | bytes 4718596
  578.7 77.2 %reduce-scatter.14.cloned.1.call-start = ((), (), s32[]{:S(2)}) async-start(), calls=%async_computation.8 | async-start | bytes 14155776 | tf_op jit(solution)/shard_map/reduce_scatter | solution.py:311
  613.0 50.1 %reduce-scatter.12.cloned.1.call-start = ((), (), s32[]{:S(2)}) async-start(), calls=%async_computation.7 | async-start | bytes 14155776 | tf_op jit(solution)/shard_map/reduce_scatter | solution.py:308
  643.6 42.9 %reduce-scatter.16.cloned.1.call-start = ((), (), s32[]{:S(2)}) async-start(), calls=%async_computation.17 | async-start | bytes 294912
  655.9 424.9 %all-reduce.7.cloned.1.call-start = ((), (), s32[]{:S(2)}) async-start(), calls=%async_computation.18 | async-start | bytes 28311552 | tf_op jit(solution)/shard_map/psum | solution.py:319
  682.8 50.5 %copy-start.107 = (f32[2,384,4]{1,2,0:T(4,128)S(1)}, f32[2,384,4]{1,2,0:T(4,128)}, u32[]{:S(2)}) copy-start(f32[2,384,4]{1,2,0:T(4,128)} %param.51) | copy-start | bytes 36868
  682.8 50.5 %copy-start.139 = (f32[2,384,4]{1,2,0:T(4,128)S(1)}, f32[2,384,4]{1,2,0:T(4,128)}, u32[]{:S(2)}) copy-start(f32[2,384,4]{1,2,0:T(4,128)} %param.52) | copy-start | bytes 36868
  682.8 50.6 %copy-start.140 = (f32[2,384,4]{1,2,0:T(4,128)S(1)}, f32[2,384,4]{1,2,0:T(4,128)}, u32[]{:S(2)}) copy-start(f32[2,384,4]{1,2,0:T(4,128)} %param.53) | copy-start | bytes 36868
  682.8 398.0 %copy-start.34 = (f32[2,384,768]{2,1,0:T(8,128)S(1)}, f32[2,384,768]{2,1,0:T(8,128)}, u32[]{:S(2)}) copy-start(f32[2,384,768]{2,1,0:T(8,128)} %param.42) | copy-start | bytes 7077892
  1080.7 24.9 %slice-start.9 = ((s8[9437184]{0:T(1024)(128)(4,1)}), s8[4194304]{0:T(1024)(128)(4,1)S(1)}, s32[]{:S(2)}) async-start(s8[9437184]{0:T(1024)(128)(4,1)} %bitcast.338), calls=%async_computation.28 | async-start | bytes 8388608
  1087.6 18.0 %slice-start.10 = ((s8[9437184]{0:T(1024)(128)(4,1)}), s8[4194304]{0:T(1024)(128)(4,1)S(1)}, s32[]{:S(2)}) async-start(s8[9437184]{0:T(1024)(128)(4,1)} %bitcast.338), calls=%async_computation.29 | async-start | bytes 8388608
  1087.6 18.0 %slice-start.11 = ((s8[9437184]{0:T(1024)(128)(4,1)}), s8[1048576]{0:T(1024)(128)(4,1)S(1)}, s32[]{:S(2)}) async-start(s8[9437184]{0:T(1024)(128)(4,1)} %bitcast.338), calls=%async_computation.30 | async-start | bytes 2097152
  (145 other events, 583.1 us)
Sparse Core Ops, SparseCore 0:
  12.8 15.3 all-gather.18
  30.3 10.3 all-gather.20
  42.9 15.5 all-gather.22
  60.5 15.6 all-gather.24
  78.1 13.8 all-gather.26
  94.0 10.3 all-gather.28
  106.5 15.5 all-gather.30
  124.3 15.5 all-gather.32
  502.6 11.5 reduce-scatter.9
  578.8 17.0 reduce-scatter.7
  613.1 19.4 reduce-scatter.13
  643.7 19.3 reduce-scatter.11
  665.8 8.8 reduce-scatter.15
  681.0 399.6 all-reduce.6
where the time goes:
time: 1160 us
  matrix products  365 us (31%)
  waiting for transfers between devices  357 us (31%)
  other arithmetic  301 us (26%)
  local copies, waits for them, and re-layouts  66.4 us (6%)
  blocking collectives  50 us (4%)
  between operations  16.6 us (1%)
    psum x1, waiting for transfers between devices, per_device(): lax.psum(shares[0].astype(jnp.bfloat16), 'dp').astype(jnp.float32)  347 us
    sub x4, other arithmetic, attend_forward(): expo = jnp.exp(masked - peak)  93.7 us
    sub x5, other arithmetic, per_device(): weight_old - rate_now * (first_new / corr_one / (jnp.sqrt(second_new / co...  69.6 us
    dot_general x4, matrix products, attend_backward(): jnp.einsum('qhd,khd->hqk', d_block, values_part, preferred_element_type=j...  57.5 us
    convert_element_type x4, other arithmetic, attend_backward(): d_scores = (probs_raw * (d_probs - inner)).astype(jnp.bfloat16)  55.1 us
    psum x1, blocking collectives, per_device(): lax.psum(shares[4].astype(jnp.bfloat16), 'dp').astype(jnp.float32)  45.7 us
    unnamed x366, local copies, waits for them, and re-layouts  42.8 us
    dot_general x2, matrix products, layer_backward(): jnp.einsum('nd,fd->nf', d_branch, lower_mat, preferred_element_type=jnp.f...  34.2 us
  transfers between devices with their start and end apart: 14, of which 2 were waited for; matrix products, arithmetic and copies ran while one was open for 37% of the time, Pallas kernels for 0%

commit v1 on v0

v1 whole, which is shorter than its diff:
```python
import functools
import math

import jax
import jax.numpy as jnp
from jax import lax
from jax.experimental import pallas as pl
from jax.experimental.pallas import tpu as pltpu
from jax.sharding import PartitionSpec as P

D = 768
HEADS = 12
HEAD_DIM = 64
STEP = 5
BF = jnp.bfloat16
F32 = jnp.float32
norm_eps = 1e-06
adam_eps = 1e-08
VMEM_LIMIT = 60 * 1024 * 1024
LOG2E = 1.4426950408889634
MASKED = -1e30


def dot(a, b):
    return lax.dot_general(a, b, (((1,), (0,)), ((), ())), preferred_element_type=F32)


def dot_nt(a, b):
    return lax.dot_general(a, b, (((1,), (1,)), ((), ())), preferred_element_type=F32)


def dot_tn(a, b):
    return lax.dot_general(a, b, (((0,), (0,)), ((), ())), preferred_element_type=F32)


def split_dot(x, mat):
    high = x.astype(BF)
    low = (x - high.astype(F32)).astype(BF)
    return dot(high, mat) + dot(low, mat)


def normalise(values):
    average = jnp.mean(values, axis=-1, keepdims=True)
    centred = values - average
    spread = jnp.mean(centred * centred, axis=-1, keepdims=True)
    scale = lax.rsqrt(spread + norm_eps)
    return centred * scale, scale


def norm_back(grad, gain, unit, scale):
    scaled = grad * gain
    first = jnp.mean(scaled, axis=-1, keepdims=True)
    second = jnp.mean(scaled * unit, axis=-1, keepdims=True)
    return scale * (scaled - first - unit * second)


def column_sum(x):
    return jnp.sum(x.reshape(x.shape[0] // 8, 8, x.shape[1]), axis=0)


def load_halves(own, mine_ref, other_ref, full_ref, sems):
    half = full_ref.shape[0] // 2
    here = pl.multiple_of(own * half, half)
    there = pl.multiple_of((1 - own) * half, half)
    return (
        pltpu.make_async_copy(mine_ref, full_ref.at[pl.ds(here, half)], sems.at[0]),
        pltpu.make_async_copy(other_ref, full_ref.at[pl.ds(there, half)], sems.at[1]),
    )


def start_all(copies):
    for copy in copies:
        copy.start()


def wait_all(copies):
    for copy in copies:
        copy.wait()


def whole(shape):
    zeros = (0,) * len(shape)
    return pl.BlockSpec(shape, lambda *_: zeros, pipeline_mode=pl.Buffered(1))


ANY = pl.BlockSpec(memory_space=pl.ANY)
SMEM = pl.BlockSpec(memory_space=pltpu.SMEM)


def params(steps=1):
    return pltpu.CompilerParams(
        dimension_semantics=("arbitrary",) * steps, vmem_limit_bytes=VMEM_LIMIT
    )


def qkv_kernel(
    own_ref, h_ref, gain_ref, heads_ref, spread_ref, mine_ref, other_ref,
    normed_ref, unit_q_ref, unit_k_ref, q_ref, k_ref, v_ref, scale_q_ref, scale_k_ref,
    weight, sems,
):
    copies = load_halves(own_ref[0], mine_ref, other_ref, weight, sems)

    @pl.when(pl.program_id(0) == 0)
    def _():
        start_all(copies)

    unit, _ = normalise(h_ref[...].astype(F32))
    normed = (unit * gain_ref[0:1, :]).astype(BF)
    normed_ref[...] = normed

    @pl.when(pl.program_id(0) == 0)
    def _():
        wait_all(copies)

    v_ref[...] = dot(normed, weight[:, 2 * D :]).astype(BF)
    for part, unit_ref, out_ref, scale_ref in (
        (0, unit_q_ref, q_ref, scale_q_ref),
        (1, unit_k_ref, k_ref, scale_k_ref),
    ):
        raw = dot(normed, weight[:, part * D : (part + 1) * D])
        average = split_dot(raw, heads_ref[...]) * (1.0 / HEAD_DIM)
        centred = raw - split_dot(average, spread_ref[...])
        spread = split_dot(centred * centred, heads_ref[...]) * (1.0 / HEAD_DIM)
        scale = lax.rsqrt(spread + norm_eps)
        unit = centred * split_dot(scale, spread_ref[...])
        unit_ref[...] = unit.astype(BF)
        out_ref[...] = (unit * gain_ref[2 + part : 3 + part, :]).astype(BF)
        scale_ref[...] = scale


def qkv_forward(own, h, gains, heads, spread, mine, other):
    rows = h.shape[0]
    block = min(512, rows)
    row = lambda width: pl.BlockSpec((block, width), lambda i: (i, 0))
    outs = [(D, BF)] * 6 + [(128, F32)] * 2
    return pl.pallas_call(
        qkv_kernel,
        name="qkv_forward",
        grid=(rows // block,),
        in_specs=[SMEM, row(D), whole(gains.shape), whole(heads.shape), whole(spread.shape), ANY, ANY],
        out_specs=[row(w) for w, _ in outs],
        out_shape=[jax.ShapeDtypeStruct((rows, w), t) for w, t in outs],
        scratch_shapes=[pltpu.VMEM((D, 3 * D), BF), pltpu.SemaphoreType.DMA((2,))],
        compiler_params=params(),
    )(own, h, gains, heads, spread, mine, other)


def window_start(block, count, reach):
    return jnp.clip(block - 1, 0, count - reach)


def pair_stack(x, low_lanes):
    zero = jnp.zeros_like(x)
    return jnp.concatenate([jnp.where(low_lanes, x, zero), jnp.where(low_lanes, zero, x)], axis=0)


def mix_kernel(
    tile, reach,
    own_ref, h_ref, q_ref, k_ref, v_ref, seg_ref, code_ref, gain_ref,
    proj_mine, proj_other, up_mine, up_other, down_mine, down_other,
    attended_ref, middle_ref, before_ref, out_ref,
    proj, up, down, sems,
):
    step = pl.program_id(0)
    own = own_ref[0]
    proj_copies = load_halves(own, proj_mine, proj_other, proj, sems.at[0])
    up_copies = load_halves(own, up_mine, up_other, up, sems.at[1])
    down_copies = load_halves(own, down_mine, down_other, down, sems.at[2])

    @pl.when(step == 0)
    def _():
        start_all(proj_copies)
        start_all(up_copies)
        start_all(down_copies)

    rows = h_ref.shape[0]
    count = k_ref.shape[0] // tile
    keys = reach * tile
    factor = LOG2E * HEAD_DIM ** (-0.5)
    low_lanes = lax.broadcasted_iota(jnp.int32, (tile, 128), 1) < HEAD_DIM

    def attend(inner, carry):
        block = step * (rows // tile) + inner
        first = pl.multiple_of(window_start(block, count, reach) * tile, tile)
        here = pl.multiple_of(inner * tile, tile)
        seg = seg_ref[pl.ds(here, tile), :]
        code = code_ref[:, pl.ds(first, keys)]
        query_at = block * tile + lax.broadcasted_iota(jnp.int32, (tile, keys), 0)
        key_at = first + lax.broadcasted_iota(jnp.int32, (tile, keys), 1)
        bias = jnp.where((seg == code) | (query_at == key_at), 0.0, MASKED)
        bias = jnp.concatenate([bias, bias], axis=0)
        for pair in range(HEADS // 2):
            lanes = slice(pair * 128, (pair + 1) * 128)
            queries = pair_stack(q_ref[pl.ds(here, tile), lanes], low_lanes)
            scores = dot_nt(queries, k_ref[pl.ds(first, keys), lanes])
            expo = jnp.exp2(scores * factor + bias)
            total = jnp.sum(expo, axis=-1, keepdims=True)
            mixed = dot(expo.astype(BF), v_ref[pl.ds(first, keys), lanes]) / total
            attended_ref[pl.ds(here, tile), lanes] = jnp.where(
                low_lanes, mixed[:tile], mixed[tile:]
            ).astype(BF)
        return carry

    lax.fori_loop(0, rows // tile, attend, 0)

    @pl.when(step == 0)
    def _():
        wait_all(proj_copies)

    middle = h_ref[...].astype(F32) + dot(attended_ref[...], proj[...])
    middle_ref[...] = middle
    unit, _ = normalise(middle)
    normed = (unit * gain_ref[1:2, :]).astype(BF)

    @pl.when(step == 0)
    def _():
        wait_all(up_copies)
        wait_all(down_copies)

    result = middle
    for part in range(up.shape[1] // D):
        lanes = slice(part * D, (part + 1) * D)
        before = dot(normed, up[:, lanes])
        before_ref[:, lanes] = before.astype(BF)
        active = jax.nn.gelu(before, approximate=True).astype(BF)
        result = result + dot(active, down[lanes, :])
    out_ref[...] = result.astype(out_ref.dtype)


def mix_forward(own, h, q, k, v, seg, code, gains, shards, out_type):
    rows = h.shape[0]
    block = min(512, rows)
    tile = min(128, rows)
    reach = min(3, rows // tile)
    width = shards[2].shape[1]
    row = lambda w: pl.BlockSpec((block, w), lambda i: (i, 0))
    outs = [(D, BF), (D, F32), (width, BF), (D, out_type)]
    return pl.pallas_call(
        functools.partial(mix_kernel, tile, reach),
        name="mix_forward",
        grid=(rows // block,),
        in_specs=[SMEM, row(D), row(D), whole(k.shape), whole(v.shape), row(1), whole(code.shape), whole(gains.shape)]
        + [ANY] * 6,
        out_specs=[row(w) for w, _ in outs],
        out_shape=[jax.ShapeDtypeStruct((rows, w), t) for w, t in outs],
        scratch_shapes=[
            pltpu.VMEM((D, D), BF),
            pltpu.VMEM((D, width), BF),
            pltpu.VMEM((width, D), BF),
            pltpu.SemaphoreType.DMA((3, 2)),
        ],
        compiler_params=params(),
    )(own, h, q, k, v, seg, code, gains, *shards)


def ffn_back_kernel(
    blocks, aliased,
    own_ref, dh_ref, before_ref, middle_ref, gain_ref, up_mine, up_other, down_mine, down_other,
    *rest,
):
    dmid_ref, dweight_ref, dgain_ref, up, down, active, dbefore, dbranch, normed, sems = rest[aliased:]
    step = pl.program_id(0)
    own = own_ref[0]
    up_copies = load_halves(own, up_mine, up_other, up, sems.at[0])
    down_copies = load_halves(own, down_mine, down_other, down, sems.at[1])

    @pl.when(step == 0)
    def _():
        start_all(down_copies)
        start_all(up_copies)
        dgain_ref[...] = jnp.zeros_like(dgain_ref)

    rows = dh_ref.shape[0]

    @pl.when(step < blocks)
    def _():
        here = pl.ds(pl.multiple_of(step * rows, rows), rows)
        dh = dh_ref[...].astype(F32)
        branch = dh.astype(BF)
        dbranch[here, :] = branch
        gain = gain_ref[1:2, :]
        unit, scale = normalise(middle_ref[...])
        normed[here, :] = (unit * gain).astype(BF)

        @pl.when(step == 0)
        def _():
            wait_all(down_copies)
            wait_all(up_copies)

        dnormed = jnp.zeros((rows, D), F32)
        for part in range(up.shape[1] // D):
            lanes = slice(part * D, (part + 1) * D)
            dactive = dot_nt(branch, down[lanes, :])
            value = before_ref[:, lanes].astype(F32)
            root = math.sqrt(2.0 / math.pi)
            square = value * value
            curve = jnp.tanh(value * (root + (root * 0.044715) * square))
            half = 0.5 * (1.0 + curve)
            active[here, lanes] = (value * half).astype(BF)
            slope = half + (0.5 * value) * (1.0 - curve * curve) * (
                root + (3.0 * 0.044715 * root) * square
            )
            dpart = (dactive * slope).astype(BF)
            dbefore[here, lanes] = dpart
            dnormed = dnormed + dot_nt(dpart, up[:, lanes])
        dmid_ref[...] = dh + norm_back(dnormed, gain, unit, scale)
        dgain_ref[...] += column_sum(dnormed * unit)

    parts = up.shape[1] // D

    @pl.when((step >= blocks) & (step < blocks + parts))
    def _():
        lanes = pl.ds(pl.multiple_of((step - blocks) * D, D), D)
        dweight_ref[0] = dot_tn(normed[...], dbefore[:, lanes]).astype(BF)

    @pl.when(step >= blocks + parts)
    def _():
        part = step - blocks - parts
        half = D // 2
        base = down.shape[0] // 2
        for side in range(2):
            lanes = pl.ds(pl.multiple_of(side * base + part * half, half), half)
            dweight_ref[0, side * half : (side + 1) * half, :] = dot_tn(
                active[:, lanes], dbranch[...]
            ).astype(BF)


def ffn_backward(own, dh, before, middle, gains, shards, grads, first, slots):
    rows, width = before.shape
    block = min(512, rows)
    blocks = rows // block
    parts = width // D
    aliased = grads is not None
    row = lambda w: pl.BlockSpec((block, w), lambda i: (jnp.minimum(i, blocks - 1), 0))
    ins = [own, dh, before, middle, gains, *shards] + [grads] * aliased
    return pl.pallas_call(
        functools.partial(ffn_back_kernel, blocks, aliased),
        name="ffn_backward",
        grid=(blocks + 2 * parts,),
        in_specs=[SMEM, row(D), row(width), row(D), whole(gains.shape)] + [ANY] * (4 + aliased),
        out_specs=[
            row(D),
            pl.BlockSpec((1, D, D), lambda i: (first + jnp.maximum(i - blocks, 0), 0, 0)),
            pl.BlockSpec((8, D), lambda i: (0, 0)),
        ],
        out_shape=[
            jax.ShapeDtypeStruct((rows, D), F32),
            jax.ShapeDtypeStruct((slots, D, D), BF),
            jax.ShapeDtypeStruct((8, D), F32),
        ],
        scratch_shapes=[
            pltpu.VMEM((D, width), BF),
            pltpu.VMEM((width, D), BF),
            pltpu.VMEM((rows, width), BF),
            pltpu.VMEM((rows, width), BF),
            pltpu.VMEM((rows, D), BF),
            pltpu.VMEM((rows, D), BF),
            pltpu.SemaphoreType.DMA((2, 2)),
        ],
        input_output_aliases={len(ins) - 1: 1} if aliased else {},
        compiler_params=params(),
    )(*ins)


def attn_back_kernel(
    tile, reach, rows,
    own_ref, dmid_ref, h_ref, normed_ref, unit_q_ref, unit_k_ref, q_ref, k_ref, v_ref,
    scale_q_ref, scale_k_ref, attended_ref, seg_ref, code_ref, gain_ref, heads_ref, spread_ref,
    qkv_mine, qkv_other, proj_mine, proj_other, grads_ref,
    dh_ref, dweight_ref, dgain_ref,
    qkv, proj, dattn, dattended, inner, dk, dv, dmixed, sems,
):
    step = pl.program_id(0)
    own = own_ref[0]
    total_rows = k_ref.shape[0]
    count = total_rows // tile
    keys = reach * tile
    blocks = total_rows // rows
    proj_copies = load_halves(own, proj_mine, proj_other, proj, sems.at[0])
    qkv_copies = load_halves(own, qkv_mine, qkv_other, qkv, sems.at[1])
    root = HEAD_DIM ** (-0.5)

    def head_norm_back(grad, gain, unit, scale):
        scaled = grad * gain
        first = split_dot(scaled, heads_ref[...]) * (1.0 / HEAD_DIM)
        second = split_dot(scaled * unit, heads_ref[...]) * (1.0 / HEAD_DIM)
        return split_dot(scale, spread_ref[...]) * (
            scaled - split_dot(first, spread_ref[...]) - unit * split_dot(second, spread_ref[...])
        )

    @pl.when(step == 0)
    def _():
        start_all(proj_copies)
        start_all(qkv_copies)
        dgain_ref[...] = jnp.zeros_like(dgain_ref)
        dk[...] = jnp.zeros_like(dk)
        dv[...] = jnp.zeros_like(dv)
        wait_all(proj_copies)
        for block in range(blocks):
            here = slice(block * rows, (block + 1) * rows)
            grad = dmid_ref[here, :].astype(BF)
            dattn[here, :] = grad
            back = dot_nt(grad, proj[...]).astype(BF)
            dattended[here, :] = back
            product = back.astype(F32) * attended_ref[here, :].astype(F32)
            high = product.astype(BF)
            low = (product - high.astype(F32)).astype(BF)
            turn = (((0,), (1,)), ((), ()))
            inner[:, here] = lax.dot_general(
                heads_ref[...], high, turn, preferred_element_type=F32
            ) + lax.dot_general(heads_ref[...], low, turn, preferred_element_type=F32)

    @pl.when(step < count)
    def _():
        first = pl.multiple_of(window_start(step, count, reach) * tile, tile)
        window = pl.ds(first, keys)
        here = pl.ds(pl.multiple_of(step * tile, tile), tile)
        low_lanes = lax.broadcasted_iota(jnp.int32, (tile, 128), 1) < HEAD_DIM
        seg = seg_ref[:, here]
        code = code_ref[window, :]
        key_at = first + lax.broadcasted_iota(jnp.int32, (keys, tile), 0)
        query_at = step * tile + lax.broadcasted_iota(jnp.int32, (keys, tile), 1)
        bias = jnp.where((seg == code) | (query_at == key_at), 0.0, MASKED)
        bias = jnp.concatenate([bias, bias], axis=1)
        dq_parts = []
        for pair in range(HEADS // 2):
            lanes = slice(pair * 128, (pair + 1) * 128)
            queries = pair_stack(q_ref[here, lanes], low_lanes)
            grads = pair_stack(dattended[here, lanes], low_lanes)
            keys_part = k_ref[window, lanes]
            scores = dot_nt(keys_part, queries)
            expo = jnp.exp2(scores * (LOG2E * root) + bias)
            probs = expo * (1.0 / jnp.sum(expo, axis=0, keepdims=True))
            dprobs = dot_nt(v_ref[window, lanes], grads)
            less = jnp.concatenate(
                [inner[2 * pair : 2 * pair + 1, here], inner[2 * pair + 1 : 2 * pair + 2, here]],
                axis=1,
            )
            dscores = (probs * (dprobs - less)).astype(BF)
            dv[window, lanes] += dot(probs.astype(BF), grads)
            dk[window, lanes] += dot(dscores, queries)
            dq = dot_tn(dscores, keys_part)
            dq_parts.append(jnp.where(low_lanes, dq[:tile], dq[tile:]))
        dq = jnp.concatenate(dq_parts, axis=1) * root
        unit = unit_q_ref[here, :].astype(F32)
        dmixed[here, 0:D] = head_norm_back(dq, gain_ref[2:3, :], unit, scale_q_ref[here, :]).astype(BF)
        dgain_ref[8:16, :] += column_sum(dq * unit)

    @pl.when(step == count)
    def _():
        wait_all(qkv_copies)

    @pl.when((step >= count) & (step < count + blocks))
    def _():
        here = pl.ds(pl.multiple_of((step - count) * rows, rows), rows)
        grad = dk[here, :] * root
        unit = unit_k_ref[here, :].astype(F32)
        dmixed[here, D : 2 * D] = head_norm_back(
            grad, gain_ref[3:4, :], unit, scale_k_ref[here, :]
        ).astype(BF)
        dgain_ref[16:24, :] += column_sum(grad * unit)
        dmixed[here, 2 * D :] = dv[here, :].astype(BF)
        dnormed = dot_nt(dmixed[here, :], qkv[...])
        unit, scale = normalise(h_ref[here, :].astype(F32))
        dh_ref[...] = dmid_ref[here, :] + norm_back(dnormed, gain_ref[0:1, :], unit, scale)
        dgain_ref[0:8, :] += column_sum(dnormed * unit)

    for part in range(4):

        @pl.when(step == count + blocks + part)
        def _():
            if part < 3:
                grad = dot_tn(normed_ref[...], dmixed[:, part * D : (part + 1) * D])
            else:
                grad = dot_tn(attended_ref[...], dattn[...])
            dweight_ref[0] = grad.astype(BF)


def attn_backward(own, dmid, h, saved, attended, segs, gains, heads, spread, shards, grads, offset):
    total = h.shape[0]
    rows = min(512, total)
    tile = min(128, total)
    reach = min(3, total // tile)
    count, blocks = total // tile, total // rows
    normed, unit_q, unit_k, q, k, v, scale_q, scale_k = saved
    ins = [dmid, h, normed, unit_q, unit_k, q, k, v, scale_q, scale_k, attended, *segs, gains, heads, spread]
    return pl.pallas_call(
        functools.partial(attn_back_kernel, tile, reach, rows),
        name="attn_backward",
        grid=(count + blocks + 4,),
        in_specs=[SMEM] + [whole(x.shape) for x in ins] + [ANY] * 5,
        out_specs=[
            pl.BlockSpec((rows, D), lambda i: (jnp.clip(i - count, 0, blocks - 1), 0)),
            pl.BlockSpec((1, D, D), lambda i: (offset + jnp.maximum(i - count - blocks, 0), 0, 0)),
            pl.BlockSpec((24, D), lambda i: (0, 0)),
        ],
        out_shape=[
            jax.ShapeDtypeStruct((total, D), F32),
            jax.ShapeDtypeStruct(grads.shape, BF),
            jax.ShapeDtypeStruct((24, D), F32),
        ],
        scratch_shapes=[
            pltpu.VMEM((D, 3 * D), BF),
            pltpu.VMEM((D, D), BF),
            pltpu.VMEM((total, D), BF),
            pltpu.VMEM((total, D), BF),
            pltpu.VMEM((128, total), F32),
            pltpu.VMEM((total, D), F32),
            pltpu.VMEM((total, D), F32),
            pltpu.VMEM((total, 3 * D), BF),
            pltpu.SemaphoreType.DMA((2, 2)),
        ],
        input_output_aliases={len(ins) + 5: 1},
        compiler_params=params(),
    )(own, *ins, *shards, grads)


MESH = pl.DeviceIdType.MESH

ORDERS = ((0, 1, 2, 3), (1, 0, 2, 3), (2, 0, 1, 3))


def flip(index, bit):
    size = 1 << bit
    return index + size * (1 - 2 * ((index // size) % 2))


def add_rows(target, source, at, other, other_at, rows):
    chunk = 48

    def body(i, carry):
        here = pl.ds(pl.multiple_of(at + i * chunk, chunk), chunk)
        there = pl.ds(pl.multiple_of(other_at + i * chunk, chunk), chunk)
        target[here, :] = (source[here, :].astype(F32) + other[there, :].astype(F32)).astype(BF)
        return carry

    lax.fori_loop(0, rows // chunk, body, 0)


def reduce_kernel(
    waves, delta, orders,
    grads, small, total, small_total,
    held, sibling, arrived, small_held, small_arrived,
    local_sems, send_sems, recv_sems, small_send, small_recv,
):
    kinds = len(orders)
    me = lax.axis_index("dp")
    core = lax.axis_index("fsdp")
    rows = held.shape[1]
    half = rows // 2
    bits = 4

    barrier = pltpu.get_barrier_semaphore()
    pl.semaphore_signal(barrier, inc=1, device_id=(me, 1 - core), device_id_type=MESH)
    for bit in range(bits):
        pl.semaphore_signal(barrier, inc=1, device_id=(flip(me, bit), core), device_id_type=MESH)
    pl.semaphore_wait(barrier, bits + 1)

    mine = pl.ds(pl.multiple_of(core * half, half), half)
    theirs = pl.ds(pl.multiple_of((1 - core) * half, half), half)

    def locals_of(unit):
        return [
            pltpu.make_async_copy(
                grads.at[2 * unit + side, mine], held.at[unit, pl.ds(side * half, half)], local_sems.at[unit, side]
            )
            for side in range(2)
        ]

    def siblings_of(unit):
        return [
            pltpu.make_async_remote_copy(
                src_ref=grads.at[2 * unit + side, theirs],
                dst_ref=sibling.at[unit, pl.ds(side * half, half)],
                send_sem=send_sems.at[unit, side], recv_sem=recv_sems.at[unit, side],
                device_id=(me, 1 - core), device_id_type=MESH,
            )
            for side in range(2)
        ]

    def outs_of(unit):
        return [
            pltpu.make_async_copy(
                sibling.at[unit, pl.ds(side * half, half)], total.at[2 * unit + side], local_sems.at[unit, side]
            )
            for side in range(2)
        ]

    def spans(order):
        found, base, size = [], 0, rows
        for bit in order:
            size = size // 2
            side = (me // (1 << bit)) % 2
            found.append((base + side * size, base + (1 - side) * size, size))
            base = base + side * size
        return found

    def scatter_copy(unit, order, step):
        _, give, size = spans(order)[step]
        landing = rows - 2 * size
        return pltpu.make_async_remote_copy(
            src_ref=held.at[unit, pl.ds(pl.multiple_of(give, size), size)],
            dst_ref=arrived.at[unit, pl.ds(landing, size)],
            send_sem=send_sems.at[unit, 2 + step], recv_sem=recv_sems.at[unit, 2 + step],
            device_id=(flip(me, order[step]), core), device_id_type=MESH,
        )

    def gather_copy(unit, order, step):
        keep, _, size = spans(order)[step]
        place = pl.ds(pl.multiple_of(keep, size), size)
        return pltpu.make_async_remote_copy(
            src_ref=sibling.at[unit, place], dst_ref=sibling.at[unit, place],
            send_sem=send_sems.at[unit, 6 + step], recv_sem=recv_sems.at[unit, 6 + step],
            device_id=(flip(me, order[step]), core), device_id_type=MESH,
        )

    def stage(unit, order, s):
        if s == 0:
            for copy in locals_of(unit) + siblings_of(unit):
                copy.start()
        elif s == 1:
            for copy in locals_of(unit) + siblings_of(unit):
                copy.wait()
            add_rows(held.at[unit], held.at[unit], 0, sibling.at[unit], 0, rows)
            scatter_copy(unit, order, 0).start()
        elif s <= 5:
            step = s - 2
            scatter_copy(unit, order, step).wait()
            keep, _, size = spans(order)[step]
            target = sibling if step == 3 else held
            add_rows(target.at[unit], held.at[unit], keep, arrived.at[unit], rows - 2 * size, size)
            if step < 3:
                scatter_copy(unit, order, step + 1).start()
            else:
                gather_copy(unit, order, 3).start()
        elif s <= 9:
            step = 9 - s
            gather_copy(unit, order, step).wait()
            if step > 0:
                gather_copy(unit, order, step - 1).start()
            else:
                for copy in outs_of(unit):
                    copy.start()
        else:
            for copy in outs_of(unit):
                copy.wait()

    def small_copy(step):
        to = (me, 1 - core) if step == 0 else (flip(me, step - 1), core)
        return pltpu.make_async_remote_copy(
            src_ref=small_held.at[step], dst_ref=small_arrived.at[step],
            send_sem=small_send.at[step], recv_sem=small_recv.at[step],
            device_id=to, device_id_type=MESH,
        )

    small_held[0] = small[...]
    small_copy(0).start()

    def slot(t, carry):
        for s in reversed(range(11)):
            off = t - s
            wave = off // delta
            @pl.when((off >= 0) & (off % delta == 0) & (wave < waves))
            def _():
                for kind, order in enumerate(orders):
                    stage(wave * kinds + kind, order, s)
        return carry

    lax.fori_loop(0, (waves - 1) * delta + 11, slot, 0)
    for step in range(bits + 1):
        small_copy(step).wait()
        value = small_held[step] + small_arrived[step]
        if step < bits:
            small_held[step + 1] = value
            small_copy(step + 1).start()
        else:
            small_total[...] = value


def reduce_all(grads, small, delta=2, orders=ORDERS):
    units = grads.shape[0] // 2
    rows = D
    waves = units // len(orders)
    return pl.pallas_call(
        functools.partial(reduce_kernel, waves, delta, orders),
        name="reduce_all",
        in_specs=[pl.BlockSpec(memory_space=pl.ANY), pl.BlockSpec(memory_space=pltpu.VMEM)],
        out_specs=[pl.BlockSpec(memory_space=pl.ANY), pl.BlockSpec(memory_space=pltpu.VMEM)],
        out_shape=[
            jax.ShapeDtypeStruct((grads.shape[0], rows // 2, D), BF),
            jax.ShapeDtypeStruct(small.shape, F32),
        ],
        scratch_shapes=[
            pltpu.VMEM((units, rows, D), BF),
            pltpu.VMEM((units, rows, D), BF),
            pltpu.VMEM((units, rows - 48, D), BF),
            pltpu.VMEM((5, *small.shape), F32),
            pltpu.VMEM((5, *small.shape), F32),
            pltpu.SemaphoreType.DMA((units, 2)),
            pltpu.SemaphoreType.DMA((units, 10)),
            pltpu.SemaphoreType.DMA((units, 10)),
            pltpu.SemaphoreType.DMA((5,)),
            pltpu.SemaphoreType.DMA((5,)),
        ],
        compiler_params=pltpu.CompilerParams(collective_id=0, has_side_effects=True, vmem_limit_bytes=60 << 20),
    )(grads, small)


CORRECTION = 1.0 - 0.5**STEP


def adam(weight, first, second, grad, rate, decay):
    first = 0.5 * first + 0.5 * grad
    second = 0.5 * second + 0.5 * grad * grad
    step = first / CORRECTION / (jnp.sqrt(second / CORRECTION) + adam_eps)
    return weight - rate * (step + decay * weight), first, second


def adam_kernel(weight_ref, first_ref, second_ref, grad_ref, *outs):
    results = adam(
        weight_ref[0], first_ref[0], second_ref[0], grad_ref[0].astype(F32), D ** (-0.5), 0.1
    )
    for out, result in zip(outs, results):
        out[0] = result


def adam_step(weight, first, second, total, base, per_layer):
    layers, rows, width = weight.shape
    half = D // 2
    down, across = rows // half, width // D
    part = pl.BlockSpec((1, half, D), lambda l, i, j: (l, i, j))
    return pl.pallas_call(
        adam_kernel,
        name="adam_step",
        grid=(layers, down, across),
        in_specs=[part] * 3
        + [pl.BlockSpec((1, half, D), lambda l, i, j: (l * per_layer + base + i + j, 0, 0))],
        out_specs=[part] * 3,
        out_shape=[jax.ShapeDtypeStruct(weight.shape, F32)] * 3,
        compiler_params=params(3),
    )(weight, first, second, total)


def per_device(dp, fsdp, *args):
    tokens, cotangent, segments, keep_mask = args[:4]
    masters, firsts, seconds = args[4::3], args[5::3], args[6::3]
    packs, length, width = tokens.shape
    layers = masters[0].shape[0]
    paired = (dp, fsdp) == (16, 2)
    me = lax.axis_index("fsdp")
    own = jnp.zeros((1,), jnp.int32) + (me if fsdp == 2 else 0)

    def halves(shard):
        if fsdp == 2:
            return shard, lax.ppermute(shard, "fsdp", [(0, 1), (1, 0)])
        full = lax.all_gather(shard, "fsdp", axis=0, tiled=True)
        return full[: full.shape[0] // 2], full[full.shape[0] // 2 :]

    gathered = [
        [halves(masters[kind][layer].astype(BF)) for kind in range(4)] for layer in range(layers)
    ]
    gains_all = lax.all_gather(masters[4].astype(BF), "fsdp", axis=1, tiled=True).astype(F32)
    gains_all = jnp.pad(gains_all.transpose(0, 2, 1), ((0, 0), (0, 4), (0, 0)))
    heads = (
        lax.broadcasted_iota(jnp.int32, (D, 128), 0) // HEAD_DIM
        == lax.broadcasted_iota(jnp.int32, (D, 128), 1)
    ).astype(BF)
    spread = heads.T
    seg = segments[0]
    code = jnp.where(keep_mask[0] == 1, seg, -1)

    hidden = tokens[0]
    stored = []
    for layer in range(layers):
        qkv, proj, up, down = gathered[layer]
        gains = gains_all[layer]
        saved = qkv_forward(own, hidden, gains, heads, spread, *qkv)
        q, k, v = saved[3:6]
        last = layer == layers - 1
        attended, middle, before, result = mix_forward(
            own, hidden, q, k, v, seg[:, None], code[None, :], gains,
            (*proj, *up, *down), BF if last else F32,
        )
        stored.append((hidden, saved, attended, middle, before))
        hidden = result
    output = hidden.reshape(tokens.shape)

    parts = 4 + 2 * (stored[0][4].shape[1] // D)
    slots = layers * parts
    grads, small = None, [None] * layers
    d_hidden = cotangent[0]
    for layer in reversed(range(layers)):
        qkv, proj, up, down = gathered[layer]
        gains = gains_all[layer]
        h, saved, attended, middle, before = stored[layer]
        d_middle, grads, gain_two = ffn_backward(
            own, d_hidden, before, middle, gains, (*up, *down), grads, layer * parts + 4, slots
        )
        d_hidden, grads, gain_rest = attn_backward(
            own, d_middle, h, saved, attended, (seg[None, :], code[:, None]), gains, heads, spread,
            (*qkv, *proj), grads, layer * parts,
        )
        gain_rest = gain_rest.reshape(3, 8, D).sum(1)
        small[layer] = jnp.stack([gain_rest[0], gain_two.sum(0), gain_rest[1], gain_rest[2]])
    small = jnp.concatenate(small)
    input_grad = d_hidden.reshape(tokens.shape)

    updated = []
    if paired:
        total, small = reduce_all(grads, small)
        for kind, base in enumerate((0, 3, 4, 4 + (parts - 4) // 2)):
            updated.append(adam_step(masters[kind], firsts[kind], seconds[kind], total, base, parts))
    else:
        small = lax.psum(small, ("dp", "fsdp"))
        blocks = grads.reshape(layers, parts, D, D)
        wide = (parts - 4) // 2
        across = lambda x: x.transpose(0, 2, 1, 3).reshape(layers, D, -1)
        full = (
            across(blocks[:, :3]),
            blocks[:, 3],
            across(blocks[:, 4 : 4 + wide]),
            blocks[:, 4 + wide :].reshape(layers, wide, 2, D // 2, D).transpose(0, 2, 1, 3, 4)
            .reshape(layers, wide * D, D),
        )
        for kind in range(4):
            grad = lax.psum_scatter(full[kind], "fsdp", scatter_dimension=1, tiled=True)
            grad = lax.psum(grad, "dp").astype(F32)
            updated.append(adam(masters[kind], firsts[kind], seconds[kind], grad, D ** (-0.5), 0.1))
    small = small.reshape(layers, 4, D).transpose(0, 2, 1)
    share = masters[4].shape[1]
    small = lax.dynamic_slice_in_dim(small, me * share, share, 1)
    updated.append(adam(masters[4], firsts[4], seconds[4], small, 0.5, 0.0))
    return (output, input_grad, *[x for group in updated for x in group])


def solution(mesh):
    rows = P(("dp", "fsdp"), None, None)
    weight = P(None, "fsdp", None)
    flat = P(("dp", "fsdp"), None)
    return jax.shard_map(
        functools.partial(per_device, mesh.shape["dp"], mesh.shape["fsdp"]),
        mesh=mesh,
        in_specs=(rows, rows, flat, flat) + (weight,) * 15,
        out_specs=(rows, rows) + (weight,) * 15,
        check_vma=False,
    )
```

time: 1160 us -> 664 us (0.57)
  Pallas kernels: 0 us -> 607 us
  matrix products: 365 us -> 0 us
  waiting for transfers between devices: 357 us -> 0.02 us
  other arithmetic: 301 us -> 15.4 us
  local copies, waits for them, and re-layouts: 66.4 us -> 16.9 us
  blocking collectives: 50 us -> 12.8 us
  between operations: 16.6 us -> 1.25 us
    pallas_call x0 -> x13, Pallas kernels: none -> 607 us  [the longest x1 251 us: reduce_all(): pl.pallas_call(functools.partial(reduce_kernel, waves, delta, orders), na...]
    dot_general x48 -> x0, matrix products: 365 us -> none  [the longest x4 57.5 us: attend_backward(): jnp.einsum('qhd,khd->hqk', d_block, values_part, preferred_element_type=j...]
    psum x1 -> x0, waiting for transfers between devices: 347 us -> none  [per_device(): lax.psum(shares[0].astype(jnp.bfloat16), 'dp').astype(jnp.float32)]
    sub x9 -> x1, other arithmetic: 163 us -> 0.64 us  [adam(): return (weight - rate * (step + decay * weight), first, second)]
    convert_element_type x11 -> x3, other arithmetic: 59.8 us -> 2.04 us  [the longest x2 2.04 us: per_device(): heads = (lax.broadcasted_iota(jnp.int32, (D, 128), 0) // HEAD_DIM == lax....]
    psum x1 -> x0, blocking collectives: 45.7 us -> none  [per_device(): lax.psum(shares[4].astype(jnp.bfloat16), 'dp').astype(jnp.float32)]
    unnamed x366 -> x38, local copies, waits for them, and re-layouts: 42.8 us -> 3.06 us
    another operation x17 -> x4, other arithmetic: 42.2 us -> 9.37 us  [the longest x7 22 us: per_device(): jnp.stack([layer_grads[layer_index][kind_index] for layer_index in range(...]
  transfers between devices with their start and end apart: 14 -> 8, of which waited for: 2 -> 0; matrix products, arithmetic and copies ran while one was open for 37% -> 3% of each run, Pallas kernels for 0% -> 11%
where the time goes in v1:
time: 664 us; the launch traced here: 656 us
  Pallas kernels  607 us (91%)
  local copies, waits for them, and re-layouts  16.9 us (3%)
  other arithmetic  15.4 us (2%)
  blocking collectives  12.8 us (2%)
    pallas_call x1, Pallas kernels, reduce_all(): pl.pallas_call(functools.partial(reduce_kernel, waves, delta, orders), na...  251 us
    pallas_call x2, Pallas kernels, attn_backward(): pl.pallas_call(functools.partial(attn_back_kernel, tile, reach, rows), na...  116 us
    pallas_call x2, Pallas kernels, ffn_backward(): pl.pallas_call(functools.partial(ffn_back_kernel, blocks, aliased), name=...  73.5 us
    pallas_call x4, Pallas kernels, adam_step(): pl.pallas_call(adam_kernel, name='adam_step', grid=(layers, down, across)...  68 us
    pallas_call x2, Pallas kernels, mix_forward(): pl.pallas_call(functools.partial(mix_kernel, tile, reach), name='mix_forw...  56.7 us
    pallas_call x2, Pallas kernels, qkv_forward(): pl.pallas_call(qkv_kernel, name='qkv_forward', grid=(rows // block,), in_...  41.3 us
  transfers between devices with their start and end apart: 8, of which 0 were waited for; matrix products, arithmetic and copies ran while one was open for 3% of the time, Pallas kernels for 11%

profile of v1, /device:TPU:0, one launch (start us, length us, event | category | flops | bytes accessed | tf_op | source)
XLA Modules:
  0.0 655.9 jit_solution(9759424654427376428)
XLA Ops:
  0.7 3.5 convert.19
  4.2 2.0 slice_bitcast_fusion.4
  6.2 0.5 collective-permute-start
  6.7 1.0 copy-done
  7.6 3.1 convert.21
  10.7 2.9 slice_bitcast_fusion.1
  13.6 0.0 copy-start.2
  13.6 0.0 copy-start.1
  13.6 0.5 collective-permute-start.2
  14.2 0.1 convert.20
  14.3 0.9 slice_bitcast_fusion.6
  15.2 0.5 collective-permute-start.1
  15.7 1.2 slice-done.2
  16.9 2.6 convert.22
  19.5 4.9 slice_bitcast_fusion
  24.4 0.5 collective-permute-start.3
  24.9 0.1 collective-permute-start.6
  24.9 0.5 collective-permute-start.7
  25.4 0.1 collective-permute-start.4
  25.5 12.8 %all_gather.3 = bf16[2,768,4]{1,2,0:T(4,128)(2,1)S(1)} all-gather(bf16[2,384,4]{1,2,0:T(4,128)(2,1)S(1)} %convert_element_type.47), channel_id=1, replica_groups=mesh['dp'=16,'fsdp'=2] {'fsdp'}, dimensions={1}, use_global_device_ids=true | all-gather | bytes 18432 | tf_op jit(solution)/shard_map/all_gather | solution.py:762
  38.4 0.6 compare_select_fusion.code_ref
  39.0 0.6 slice_bitcast_fusion.8
  39.6 1.3 fusion.heads_ref
  40.9 0.4 collective-permute-start.5
  41.3 0.2 copy.39.seg_ref
  41.5 0.0 copy-start.4
  41.5 0.9 copy.41
  42.4 0.7 fusion.1.spread_ref
  43.2 1.8 broadcast_select_fusion.code_ref
  44.9 20.4 %qkv_forward.2 = (bf16[1024,768]{1,0:T(8,128)(2,1)}, bf16[1024,768]{1,0:T(8,128)(2,1)}, bf16[1024,768]{1,0:T(8,128)(2,1)}, bf16[1024,768]{1,0:T(8,128)(2,1)}, bf...) custom-call(s32[1]{0:T(128)} %bitcast.own_ref, ...), custom_call_target="tpu_custom_call" | custom-call | tf_op jit(solution)/shard_map/qkv_forward/pallas_call | solution.py:136
  65.4 28.4 %mix_forward.2 = (bf16[1024,768]{1,0:T(8,128)(2,1)}, f32[1024,768]{1,0:T(8,128)}, bf16[1024,3072]{1,0:T(8,128)(2,1)}, f32[1024,768]{1,0:T(8,128)}) custom-call(s32[1]{0:T(128)} %bitcast.own_ref, bf16[1024,768]{1,0:T(8,128)(2,1)} %bitcast.41, bf16[1024,768]{1,0:T(8,128)(2,1)} %get-tuple-element.67.q_ref, bf16[1024,768]{1,0:T(8,128)(2,1)} %get-tuple-element.68.k_ref, ...), custom_call_target="tpu_custom_call" | custom-call | tf_op jit(solution)/shard_map/mix_forward/pallas_call | solution.py:238
  93.8 20.9 %qkv_forward.3 = (bf16[1024,768]{1,0:T(8,128)(2,1)}, bf16[1024,768]{1,0:T(8,128)(2,1)}, bf16[1024,768]{1,0:T(8,128)(2,1)}, bf16[1024,768]{1,0:T(8,128)(2,1)}, bf...) custom-call(s32[1]{0:T(128)} %bitcast.own_ref, ...), custom_call_target="tpu_custom_call" | custom-call | tf_op jit(solution)/shard_map/qkv_forward/pallas_call | solution.py:136
  114.7 0.8 copy-done.7
  115.5 28.4 %mix_forward.3 = (bf16[1024,768]{1,0:T(8,128)(2,1)}, f32[1024,768]{1,0:T(8,128)}, bf16[1024,3072]{1,0:T(8,128)(2,1)}, bf16[1024,768]{1,0:T(8,128)(2,1)}) custom-call(s32[1]{0:T(128)} %bitcast.own_ref, f32[1024,768]{1,0:T(8,128)} %get-tuple-element.70.h_ref, bf16[1024,768]{1,0:T(8,128)(2,1)} %get-tuple-element.71.q_ref, ...), custom_call_target="tpu_custom_call" | custom-call | tf_op jit(solution)/shard_map/mix_forward/pallas_call | solution.py:238
  143.9 36.8 %ffn_backward.2 = (f32[1024,768]{1,0:T(8,128)}, bf16[24,768,768]{2,1,0:T(8,128)(2,1)}, f32[8,768]{1,0:T(8,128)}) custom-call(s32[1]{0:T(128)} %bitcast.own_ref, bf16[1024,768]{1,0:T(8,128)(2,1)} %bitcast.43, bf16[1024,3072]{1,0:T(8,128)(2,1)} %get-tuple-element.75.before_ref, f32[1024,768]{1,0:T(8,128)} %get-tuple-element.76.middle_ref, ...), custom_call_target="tpu_custom_call" | custom-call | tf_op jit(solution)/shard_map/ffn_backward/pallas_call | solution.py:336
  180.7 58.1 %attn_backward.2 = (f32[1024,768]{1,0:T(8,128)}, bf16[24,768,768]{2,1,0:T(8,128)(2,1)}, f32[24,768]{1,0:T(8,128)}) custom-call(s32[1]{0:T(128)} %bitcast.own_ref, f32[1024,768]{1,0:T(8,128)} %get-tuple-element.77.dmid_ref, f32[1024,768]{1,0:T(8,128)} %get-tuple-element.70.h_ref, ...), custom_call_target="tpu_custom_call", output_to_operand_aliasing={{1}: (21, {})} | custom-call | tf_op jit(solution)/shard_map/attn_backward/pallas_call | solution.py:487
  238.8 36.7 %ffn_backward.3 = (f32[1024,768]{1,0:T(8,128)}, bf16[24,768,768]{2,1,0:T(8,128)(2,1)}, f32[8,768]{1,0:T(8,128)}) custom-call(s32[1]{0:T(128)} %bitcast.own_ref, f32[1024,768]{1,0:T(8,128)} %get-tuple-element.85.dh_ref, bf16[1024,3072]{1,0:T(8,128)(2,1)} %get-tuple-element.86.before_ref, ...), custom_call_target="tpu_custom_call", output_to_operand_aliasing={{1}: (9, {})} | custom-call | tf_op jit(solution)/shard_map/ffn_backward/pallas_call | solution.py:336
  275.5 0.0 copy-start.8
  275.6 57.7 %attn_backward.3 = (f32[1024,768]{1,0:T(8,128)}, bf16[24,768,768]{2,1,0:T(8,128)(2,1)}, f32[24,768]{1,0:T(8,128)}) custom-call(s32[1]{0:T(128)} %bitcast.own_ref, f32[1024,768]{1,0:T(8,128)} %get-tuple-element.89.dmid_ref, bf16[1024,768]{1,0:T(8,128)(2,1)} %bitcast.42, ...), custom_call_target="tpu_custom_call", output_to_operand_aliasing={{1}: (21, {})} | custom-call | tf_op jit(solution)/shard_map/attn_backward/pallas_call | solution.py:487
  333.2 0.9 bitcast_reduce_fusion.1
  334.3 0.6 concatenate.3.small
  335.0 251.3 %reduce_all.1 = (bf16[24,384,768]{2,1,0:T(8,128)(2,1)}, f32[8,768]{1,0:T(8,128)}) custom-call(bf16[24,768,768]{2,1,0:T(8,128)(2,1)} %get-tuple-element.98.grads, f32[8,768]{1,0:T(8,128)} %concatenate.3.small), custom_call_target="tpu_custom_call" | custom-call | tf_op jit(solution)/shard_map/reduce_all/pallas_call | solution.py:684
  586.2 0.7 reshape.83
  587.0 17.0 %adam_step.4 = (f32[2,384,2304]{2,1,0:T(8,128)}, f32[2,384,2304]{2,1,0:T(8,128)}, f32[2,384,2304]{2,1,0:T(8,128)}) custom-call(f32[2,384,2304]{2,1,0:T(8,128)} %weight_ref.4, f32[2,384,2304]{2,1,0:T(8,128)} %first_ref.4, f32[2,384,2304]{2,1,0:T(8,128)} %second_ref.4, bf16[24,384,768]{2,1,0:T(8,128)(2,1)} %get-tuple-element.103.grad_ref), custom_call_target="tpu_custom_call" | custom-call | tf_op jit(solution)/shard_map/adam_step/pallas_call | solution.py:732
  604.0 6.0 adam_step.5
  610.0 22.5 %adam_step.6 = (f32[2,384,3072]{2,1,0:T(8,128)}, f32[2,384,3072]{2,1,0:T(8,128)}, f32[2,384,3072]{2,1,0:T(8,128)}) custom-call(f32[2,384,3072]{2,1,0:T(8,128)} %weight_ref.6, f32[2,384,3072]{2,1,0:T(8,128)} %first_ref.6, f32[2,384,3072]{2,1,0:T(8,128)} %second_ref.6, bf16[24,384,768]{2,1,0:T(8,128)(2,1)} %get-tuple-element.103.grad_ref), custom_call_target="tpu_custom_call" | custom-call | tf_op jit(solution)/shard_map/adam_step/pallas_call | solution.py:732
  632.5 22.5 %adam_step.7 = (f32[2,1536,768]{2,1,0:T(8,128)}, f32[2,1536,768]{2,1,0:T(8,128)}, f32[2,1536,768]{2,1,0:T(8,128)}) custom-call(f32[2,1536,768]{2,1,0:T(8,128)} %weight_ref.7, f32[2,1536,768]{2,1,0:T(8,128)} %first_ref.7, f32[2,1536,768]{2,1,0:T(8,128)} %second_ref.7, bf16[24,384,768]{2,1,0:T(8,128)(2,1)} %get-tuple-element.103.grad_ref), custom_call_target="tpu_custom_call" | custom-call | tf_op jit(solution)/shard_map/adam_step/pallas_call | solution.py:732
  655.0 0.6 multiply_subtract_fusion
  (54 shorter events, 0.2 us)
Async XLA Ops:
  0.7 7.0 %copy-start = (f32[2,384,3072]{2,1,0:T(8,128)S(1)}, f32[2,384,3072]{2,1,0:T(8,128)}, u32[]{:S(2)}) copy-start(f32[2,384,3072]{2,1,0:T(8,128)} %weight_ref.6) | copy-start | bytes 28311556
  6.2 19.2 %collective-permute-start = (bf16[384,2304]{1,0:T(8,128)(2,1)}, bf16[384,2304]{1,0:T(8,128)(2,1)}, u32[]{:S(2)}, u32[]{:S(2)}) collective-permute-start(bf16[384,2304]{1,0:T(8,128)(2,1)} %get-tuple-element.125.mine_ref.qkv_mine), channel_id=1, source_target_pairs={{0,1},{1,0},{2,3},{3,2},{4,5},{5,4},{6,7},{7,6},{8,9},{9,8},{10,11... | collective-permute-start | bytes 5308424 | tf_op jit(solution)/shard_map/ppermute | solution.py:755
  7.6 8.0 %slice-start = ((s8[9437184]{0:T(1024)(128)(4,1)}), s8[1048576]{0:T(1024)(128)(4,1)S(1)}, s32[]{:S(2)}) async-start(s8[9437184]{0:T(1024)(128)(4,1)} %bitcast.38), calls=%async_computation | async-start | bytes 2097152
  7.6 8.0 %slice-start.1 = ((s8[9437184]{0:T(1024)(128)(4,1)}), s8[4194304]{0:T(1024)(128)(4,1)S(1)}, s32[]{:S(2)}) async-start(s8[9437184]{0:T(1024)(128)(4,1)} %bitcast.38), calls=%async_computation.1 | async-start | bytes 8388608
  10.7 3.4 copy-start.3
  10.7 6.1 slice-start.2
  13.6 1.6 copy-start.2
  13.6 11.3 %copy-start.1 = (bf16[384,3072]{1,0:T(8,128)(2,1)}, bf16[384,3072]{1,0:T(8,128)(2,1)S(1)}, u32[]{:S(2)}) copy-start(bf16[384,3072]{1,0:T(8,128)(2,1)S(1)} %get-tuple-element.122.up_mine) | copy-start | bytes 7077892
  13.6 27.3 %collective-permute-start.2 = (bf16[384,3072]{1,0:T(8,128)(2,1)S(1)}, bf16[384,3072]{1,0:T(8,128)(2,1)}, u32[]{:S(2)}, u32[]{:S(2)}) collective-permute-start(bf16[384,3072]{1,0:T(8,128)(2,1)S(1)} %get-tuple-element.123.up_mine), channel_id=1, source_target_pairs={{0,1},{1,0},{2,3},{3,2},{4,5},{5,4},{6,7},{7,6},{8,9},{9,8},{10,11... | collective-permute-start | bytes 7077896 | tf_op jit(solution)/shard_map/ppermute | solution.py:755
  15.2 4.3 copy-start.5
  15.2 9.7 %collective-permute-start.1 = (bf16[384,768]{1,0:T(8,128)(2,1)S(1)}, bf16[384,768]{1,0:T(8,128)(2,1)S(1)}, u32[]{:S(2)}, u32[]{:S(2)}) collective-permute-start(bf16[384,768]{1,0:T(8,128)(2,1)S(1)} %get-tuple-element.127.proj_mine), channel_id=1, source_target_pairs={{0,1},{1,0},{2,3},{3,2},{4,5},{5,4},{6,7},{7,6},{8,9},{9,8},{10,11... | collective-permute-start | bytes 1769480 | tf_op jit(solution)/shard_map/ppermute | solution.py:755
  19.5 6.0 copy-start.10
  19.5 18.8 %copy-start.9 = (s32[1,1024]{1,0:T(1,128)S(1)}, s32[1,1024]{1,0:T(1,128)}, u32[]{:S(2)}) copy-start(s32[1,1024]{1,0:T(1,128)} %seg_ref.3) | copy-start | bytes 12292
  19.5 18.8 %copy-start.13 = (s32[1,1024]{1,0:T(1,128)S(1)}, s32[1,1024]{1,0:T(1,128)}, u32[]{:S(2)}) copy-start(s32[1,1024]{1,0:T(1,128)} %param.22) | copy-start | bytes 12292
  24.4 41.0 %collective-permute-start.3 = (bf16[1536,768]{1,0:T(8,128)(2,1)}, bf16[1536,768]{1,0:T(8,128)(2,1)}, u32[]{:S(2)}, u32[]{:S(2)}) collective-permute-start(bf16[1536,768]{1,0:T(8,128)(2,1)} %get-tuple-element.121.down_mine), channel_id=1, source_target_pairs={{0,1},{1,0},{2,3},{3,2},{4,5},{5,4},{6,7},{7,6},{8,9},{9,8},{10,11... | collective-permute-start | bytes 7077896 | tf_op jit(solution)/shard_map/ppermute | solution.py:755
  24.9 89.8 %collective-permute-start.6 = (bf16[384,3072]{1,0:T(8,128)(2,1)S(1)}, bf16[384,3072]{1,0:T(8,128)(2,1)}, u32[]{:S(2)}, u32[]{:S(2)}) collective-permute-start(bf16[384,3072]{1,0:T(8,128)(2,1)S(1)} %get-tuple-element.122.up_mine), channel_id=1, source_target_pairs={{0,1},{1,0},{2,3},{3,2},{4,5},{5,4},{6,7},{7,6},{8,9},{9,8},{10,11... | collective-permute-start | bytes 7077896 | tf_op jit(solution)/shard_map/ppermute | solution.py:755
  24.9 16.0 %copy-start.6 = (bf16[384,768]{1,0:T(8,128)(2,1)}, bf16[384,768]{1,0:T(8,128)(2,1)S(1)}, u32[]{:S(2)}) copy-start(bf16[384,768]{1,0:T(8,128)(2,1)S(1)} %collective-permute-done.1.proj_other) | copy-start | bytes 1769476
  24.9 89.8 %collective-permute-start.7 = (bf16[1536,768]{1,0:T(8,128)(2,1)}, bf16[1536,768]{1,0:T(8,128)(2,1)}, u32[]{:S(2)}, u32[]{:S(2)}) collective-permute-start(bf16[1536,768]{1,0:T(8,128)(2,1)} %get-tuple-element.120.down_mine), channel_id=1, source_target_pairs={{0,1},{1,0},{2,3},{3,2},{4,5},{5,4},{6,7},{7,6},{8,9},{9,8},{10,11... | collective-permute-start | bytes 7077896 | tf_op jit(solution)/shard_map/ppermute | solution.py:755
  25.4 68.4 %collective-permute-start.4 = (bf16[384,2304]{1,0:T(8,128)(2,1)}, bf16[384,2304]{1,0:T(8,128)(2,1)}, u32[]{:S(2)}, u32[]{:S(2)}) collective-permute-start(bf16[384,2304]{1,0:T(8,128)(2,1)} %get-tuple-element.124.mine_ref.qkv_mine), channel_id=1, source_target_pairs={{0,1},{1,0},{2,3},{3,2},{4,5},{5,4},{6,7},{7,6},{8,9},{9,8},{10,11... | collective-permute-start | bytes 5308424 | tf_op jit(solution)/shard_map/ppermute | solution.py:755
  40.9 73.8 %collective-permute-start.5 = (bf16[384,768]{1,0:T(8,128)(2,1)}, bf16[384,768]{1,0:T(8,128)(2,1)S(1)}, u32[]{:S(2)}, u32[]{:S(2)}) collective-permute-start(bf16[384,768]{1,0:T(8,128)(2,1)} %get-tuple-element.126.proj_mine), channel_id=1, source_target_pairs={{0,1},{1,0},{2,3},{3,2},{4,5},{5,4},{6,7},{7,6},{8,9},{9,8},{10,11... | collective-permute-start | bytes 1769480 | tf_op jit(solution)/shard_map/ppermute | solution.py:755
  41.5 23.8 %copy-start.4 = (s32[1024,1]{1,0:T(8,128)}, s32[1024,1]{1,0:T(8,128)S(1)}, u32[]{:S(2)}) copy-start(s32[1024,1]{1,0:T(8,128)S(1)} %copy.39.seg_ref) | copy-start | bytes 12292
  114.7 0.8 copy-start.7
  275.5 58.6 %copy-start.8 = (f32[24,768]{1,0:T(8,128)S(1)}, f32[24,768]{1,0:T(8,128)}, u32[]{:S(2)}) copy-start(f32[24,768]{1,0:T(8,128)} %get-tuple-element.101) | copy-start | bytes 221188
  275.5 58.7 %copy-start.12 = (f32[8,768]{1,0:T(8,128)S(1)}, f32[8,768]{1,0:T(8,128)}, u32[]{:S(2)}) copy-start(f32[8,768]{1,0:T(8,128)} %get-tuple-element.100) | copy-start | bytes 73732
  275.6 58.7 %copy-start.11 = (f32[8,768]{1,0:T(8,128)S(1)}, f32[8,768]{1,0:T(8,128)}, u32[]{:S(2)}) copy-start(f32[8,768]{1,0:T(8,128)} %get-tuple-element.102) | copy-start | bytes 73732
  632.5 22.5 %copy-start.14 = (f32[2,384,4]{1,2,0:T(4,128)S(1)}, f32[2,384,4]{1,2,0:T(4,128)}, u32[]{:S(2)}) copy-start(f32[2,384,4]{1,2,0:T(4,128)} %param.36) | copy-start | bytes 36868
  632.5 22.5 %copy-start.15 = (f32[2,384,4]{1,2,0:T(4,128)S(1)}, f32[2,384,4]{1,2,0:T(4,128)}, u32[]{:S(2)}) copy-start(f32[2,384,4]{1,2,0:T(4,128)} %param.37) | copy-start | bytes 36868

commit v2 on v1

v2 whole, which is shorter than its diff:
```python
import functools
import math

import jax
import jax.numpy as jnp
from jax import lax
from jax.experimental import pallas as pl
from jax.experimental.pallas import tpu as pltpu
from jax.sharding import PartitionSpec as P

D = 768
HEADS = 12
HEAD_DIM = 64
STEP = 5
BF = jnp.bfloat16
F32 = jnp.float32
norm_eps = 1e-06
adam_eps = 1e-08
VMEM_LIMIT = 62 * 1024 * 1024
LOG2E = 1.4426950408889634
MASKED = -1e30


def dot(a, b):
    return lax.dot_general(a, b, (((1,), (0,)), ((), ())), preferred_element_type=F32)


def dot_nt(a, b):
    return lax.dot_general(a, b, (((1,), (1,)), ((), ())), preferred_element_type=F32)


def dot_tn(a, b):
    return lax.dot_general(a, b, (((0,), (0,)), ((), ())), preferred_element_type=F32)


def split_dot(x, mat):
    high = x.astype(BF)
    low = (x - high.astype(F32)).astype(BF)
    return dot(high, mat) + dot(low, mat)


def normalise(values):
    average = jnp.mean(values, axis=-1, keepdims=True)
    centred = values - average
    spread = jnp.mean(centred * centred, axis=-1, keepdims=True)
    scale = lax.rsqrt(spread + norm_eps)
    return centred * scale, scale


def norm_back(grad, gain, unit, scale):
    scaled = grad * gain
    first = jnp.mean(scaled, axis=-1, keepdims=True)
    second = jnp.mean(scaled * unit, axis=-1, keepdims=True)
    return scale * (scaled - first - unit * second)


def column_sum(x):
    return jnp.sum(x.reshape(x.shape[0] // 8, 8, x.shape[1]), axis=0)


def load_halves(own, mine_ref, other_ref, full_ref, sems):
    half = full_ref.shape[0] // 2
    here = pl.multiple_of(own * half, half)
    there = pl.multiple_of((1 - own) * half, half)
    return (
        pltpu.make_async_copy(mine_ref, full_ref.at[pl.ds(here, half)], sems.at[0]),
        pltpu.make_async_copy(other_ref, full_ref.at[pl.ds(there, half)], sems.at[1]),
    )


def start_all(copies):
    for copy in copies:
        copy.start()


def wait_all(copies):
    for copy in copies:
        copy.wait()


def whole(shape):
    zeros = (0,) * len(shape)
    return pl.BlockSpec(shape, lambda *_: zeros, pipeline_mode=pl.Buffered(1))


ANY = pl.BlockSpec(memory_space=pl.ANY)
SMEM = pl.BlockSpec(memory_space=pltpu.SMEM)


def params(steps=1):
    return pltpu.CompilerParams(
        dimension_semantics=("arbitrary",) * steps, vmem_limit_bytes=VMEM_LIMIT
    )


def qkv_kernel(
    own_ref, h_ref, gain_ref, heads_ref, spread_ref, mine_ref, other_ref,
    normed_ref, q_ref, k_ref, v_ref, scale_q_ref, scale_k_ref,
    weight, sems,
):
    copies = load_halves(own_ref[0], mine_ref, other_ref, weight, sems)

    @pl.when(pl.program_id(0) == 0)
    def _():
        start_all(copies)

    unit, _ = normalise(h_ref[...].astype(F32))
    normed = (unit * gain_ref[0:1, :]).astype(BF)
    normed_ref[...] = normed

    @pl.when(pl.program_id(0) == 0)
    def _():
        wait_all(copies)

    v_ref[...] = dot(normed, weight[:, 2 * D :]).astype(BF)
    for part, out_ref, scale_ref in ((0, q_ref, scale_q_ref), (1, k_ref, scale_k_ref)):
        raw = dot(normed, weight[:, part * D : (part + 1) * D])
        average = split_dot(raw, heads_ref[...]) * (1.0 / HEAD_DIM)
        centred = raw - split_dot(average, spread_ref[...])
        spread = split_dot(centred * centred, heads_ref[...]) * (1.0 / HEAD_DIM)
        scale = lax.rsqrt(spread + norm_eps)
        unit = centred * split_dot(scale, spread_ref[...])
        out_ref[...] = (unit * gain_ref[2 + part : 3 + part, :]).astype(BF)
        scale_ref[...] = scale


def qkv_forward(own, h, gains, heads, spread, mine, other):
    rows = h.shape[0]
    block = min(512, rows)
    row = lambda width: pl.BlockSpec((block, width), lambda i: (i, 0))
    outs = [(D, BF)] * 4 + [(128, F32)] * 2
    return pl.pallas_call(
        qkv_kernel,
        name="qkv_forward",
        grid=(rows // block,),
        in_specs=[SMEM, row(D), whole(gains.shape), whole(heads.shape), whole(spread.shape), ANY, ANY],
        out_specs=[row(w) for w, _ in outs],
        out_shape=[jax.ShapeDtypeStruct((rows, w), t) for w, t in outs],
        scratch_shapes=[pltpu.VMEM((D, 3 * D), BF), pltpu.SemaphoreType.DMA((2,))],
        compiler_params=params(),
    )(own, h, gains, heads, spread, mine, other)


def window_start(block, count, reach):
    return jnp.clip(block - 1, 0, count - reach)


def pair_stack(x, low_lanes):
    zero = jnp.zeros_like(x)
    return jnp.concatenate([jnp.where(low_lanes, x, zero), jnp.where(low_lanes, zero, x)], axis=0)


def mix_kernel(
    tile, reach,
    own_ref, h_ref, q_ref, k_ref, v_ref, seg_ref, code_ref, gain_ref,
    proj_mine, proj_other, up_mine, up_other, down_mine, down_other,
    attended_ref, middle_ref, before_ref, out_ref,
    proj, up, down, sems,
):
    step = pl.program_id(0)
    own = own_ref[0]
    proj_copies = load_halves(own, proj_mine, proj_other, proj, sems.at[0])
    up_copies = load_halves(own, up_mine, up_other, up, sems.at[1])
    down_copies = load_halves(own, down_mine, down_other, down, sems.at[2])

    @pl.when(step == 0)
    def _():
        start_all(proj_copies)
        start_all(up_copies)
        start_all(down_copies)

    rows = h_ref.shape[0]
    count = k_ref.shape[0] // tile
    keys = reach * tile
    factor = LOG2E * HEAD_DIM ** (-0.5)
    low_lanes = lax.broadcasted_iota(jnp.int32, (tile, 128), 1) < HEAD_DIM

    def attend(inner, carry):
        block = step * (rows // tile) + inner
        first = pl.multiple_of(window_start(block, count, reach) * tile, tile)
        here = pl.multiple_of(inner * tile, tile)
        seg = seg_ref[pl.ds(here, tile), :]
        code = code_ref[:, pl.ds(first, keys)]
        query_at = block * tile + lax.broadcasted_iota(jnp.int32, (tile, keys), 0)
        key_at = first + lax.broadcasted_iota(jnp.int32, (tile, keys), 1)
        bias = jnp.where((seg == code) | (query_at == key_at), 0.0, MASKED)
        bias = jnp.concatenate([bias, bias], axis=0)
        for pair in range(HEADS // 2):
            lanes = slice(pair * 128, (pair + 1) * 128)
            queries = pair_stack(q_ref[pl.ds(here, tile), lanes], low_lanes)
            scores = dot_nt(queries, k_ref[pl.ds(first, keys), lanes])
            expo = jnp.exp2(scores * factor + bias)
            total = jnp.sum(expo, axis=-1, keepdims=True)
            mixed = dot(expo.astype(BF), v_ref[pl.ds(first, keys), lanes]) / total
            attended_ref[pl.ds(here, tile), lanes] = jnp.where(
                low_lanes, mixed[:tile], mixed[tile:]
            ).astype(BF)
        return carry

    lax.fori_loop(0, rows // tile, attend, 0)

    @pl.when(step == 0)
    def _():
        wait_all(proj_copies)

    middle = h_ref[...].astype(F32) + dot(attended_ref[...], proj[...])
    middle_ref[...] = middle
    unit, _ = normalise(middle)
    normed = (unit * gain_ref[1:2, :]).astype(BF)

    @pl.when(step == 0)
    def _():
        wait_all(up_copies)
        wait_all(down_copies)

    result = middle
    for part in range(up.shape[1] // D):
        lanes = slice(part * D, (part + 1) * D)
        before = dot(normed, up[:, lanes])
        before_ref[:, lanes] = before.astype(BF)
        active = jax.nn.gelu(before, approximate=True).astype(BF)
        result = result + dot(active, down[lanes, :])
    out_ref[...] = result.astype(out_ref.dtype)


def mix_forward(own, h, q, k, v, seg, code, gains, shards, out_type):
    rows = h.shape[0]
    block = min(512, rows)
    tile = min(128, rows)
    reach = min(3, rows // tile)
    width = shards[2].shape[1]
    row = lambda w: pl.BlockSpec((block, w), lambda i: (i, 0))
    outs = [(D, BF), (D, F32), (width, BF), (D, out_type)]
    return pl.pallas_call(
        functools.partial(mix_kernel, tile, reach),
        name="mix_forward",
        grid=(rows // block,),
        in_specs=[SMEM, row(D), row(D), whole(k.shape), whole(v.shape), row(1), whole(code.shape), whole(gains.shape)]
        + [ANY] * 6,
        out_specs=[row(w) for w, _ in outs],
        out_shape=[jax.ShapeDtypeStruct((rows, w), t) for w, t in outs],
        scratch_shapes=[
            pltpu.VMEM((D, D), BF),
            pltpu.VMEM((D, width), BF),
            pltpu.VMEM((width, D), BF),
            pltpu.SemaphoreType.DMA((3, 2)),
        ],
        compiler_params=params(),
    )(own, h, q, k, v, seg, code, gains, *shards)


MESH = pl.DeviceIdType.MESH

BITS = 4
XYZ, YXZ, ZXY, YZX, XZY, ZYX = (
    (0, 1, 2, 3), (1, 0, 2, 3), (2, 0, 1, 3), (1, 2, 0, 3), (0, 2, 1, 3), (2, 1, 0, 3),
)
GROUP, SPLIT = 4, 3
UNIT = GROUP * D // 2
WIDTH = D // SPLIT
FINAL = UNIT >> BITS


def flip(index, bit):
    size = 1 << bit
    return index + size * (1 - 2 * ((index // size) % 2))


def meet(partners):
    me, core = lax.axis_index("dp"), lax.axis_index("fsdp")
    barrier = pltpu.get_barrier_semaphore()
    pl.semaphore_signal(barrier, inc=1, device_id=(me, 1 - core), device_id_type=MESH)
    for bit in range(partners):
        pl.semaphore_signal(barrier, inc=1, device_id=(flip(me, bit), core), device_id_type=MESH)
    pl.semaphore_wait(barrier, 1 + partners)


def add_rows(target, source, at, other, other_at, rows):
    chunk = FINAL

    def body(i, carry):
        here = pl.ds(pl.multiple_of(at + i * chunk, chunk), chunk)
        there = pl.ds(pl.multiple_of(other_at + i * chunk, chunk), chunk)
        target[here, :] = (source[here, :].astype(F32) + other[there, :].astype(F32)).astype(BF)
        return carry

    lax.fori_loop(0, rows // chunk, body, 0)


class Sum:
    def __init__(self, kind, orders):
        self.kind, self.orders, self.count = kind, orders, len(orders)
        self.scatters = kind != "gather"
        self.gathers = kind != "scatter"

    def blocks(self):
        return GROUP * self.count // SPLIT

    def out_shapes(self):
        if self.gathers:
            return [jax.ShapeDtypeStruct((self.blocks(), D // 2, D), BF)]
        return [jax.ShapeDtypeStruct((self.count, FINAL, WIDTH), BF)]

    def inputs(self):
        return 2 if self.scatters else 1

    def scratch(self):
        n = self.count
        found = []
        if self.scatters:
            found += [
                pltpu.VMEM((n, UNIT, WIDTH), BF),
                pltpu.VMEM((n, UNIT - FINAL, WIDTH), BF),
                pltpu.VMEM((2, UNIT, WIDTH), BF),
                pltpu.SemaphoreType.DMA((n, 2 * GROUP)),
                pltpu.SemaphoreType.DMA((n, BITS)),
                pltpu.SemaphoreType.DMA((n, BITS)),
            ]
        if self.gathers:
            found += [
                pltpu.VMEM((n, UNIT, WIDTH), BF),
                pltpu.SemaphoreType.DMA((n, GROUP)),
                pltpu.SemaphoreType.DMA((n, BITS)),
                pltpu.SemaphoreType.DMA((n, BITS)),
            ]
        else:
            found += [pltpu.SemaphoreType.DMA((n,))]
        return found

    def bind(self, ins, outs, scratch):
        self.me, self.core = lax.axis_index("dp"), lax.axis_index("fsdp")
        self.ins, self.out = ins, outs[0]
        scratch = list(scratch)
        if self.scatters:
            self.held, self.arrived, self.stage, self.load, self.send, self.recv = scratch[:6]
            scratch = scratch[6:]
        if self.gathers:
            self.final, self.local, self.gsend, self.grecv = scratch
        else:
            self.local = scratch[0]

    def spans(self, unit):
        found, base, size = [], 0, UNIT
        for bit in self.orders[unit]:
            size = size // 2
            side = (self.me // (1 << bit)) % 2
            found.append((base + side * size, base + (1 - side) * size, size))
            base = base + side * size
        return found

    def window(self, ref, unit, side):
        block = GROUP * (unit // SPLIT) + side
        return ref.at[block, :, pl.ds((unit % SPLIT) * WIDTH, WIDTH)]

    def loads(self, unit):
        return [
            pltpu.make_async_copy(
                self.window(source, unit, side),
                target.at[pl.ds(side * (D // 2), D // 2)],
                self.load.at[unit, GROUP * which + side],
            )
            for which, (source, target) in enumerate(
                ((self.ins[0], self.held.at[unit]), (self.ins[1], self.stage.at[unit % 2]))
            )
            for side in range(GROUP)
        ]

    def scatter_copy(self, unit, step):
        _, give, size = self.spans(unit)[step]
        return pltpu.make_async_remote_copy(
            src_ref=self.held.at[unit, pl.ds(pl.multiple_of(give, size), size)],
            dst_ref=self.arrived.at[unit, pl.ds(UNIT - 2 * size, size)],
            send_sem=self.send.at[unit, step], recv_sem=self.recv.at[unit, step],
            device_id=(flip(self.me, self.orders[unit][step]), self.core), device_id_type=MESH,
        )

    def gather_copy(self, unit, step):
        keep, _, size = self.spans(unit)[step]
        place = pl.ds(pl.multiple_of(keep, size), size)
        return pltpu.make_async_remote_copy(
            src_ref=self.final.at[unit, place], dst_ref=self.final.at[unit, place],
            send_sem=self.gsend.at[unit, step], recv_sem=self.grecv.at[unit, step],
            device_id=(flip(self.me, self.orders[unit][step]), self.core), device_id_type=MESH,
        )

    def share_copy(self, unit):
        keep, _, size = self.spans(unit)[BITS - 1]
        place = pl.ds(pl.multiple_of(keep, size), size)
        if self.scatters:
            return pltpu.make_async_copy(self.held.at[unit, place], self.out.at[unit], self.local.at[unit])
        return pltpu.make_async_copy(self.ins[0].at[unit], self.final.at[unit, place], self.local.at[unit, 0])

    def outs(self, unit):
        return [
            pltpu.make_async_copy(
                self.final.at[unit, pl.ds(side * (D // 2), D // 2)],
                self.window(self.out, unit, side),
                self.local.at[unit, side],
            )
            for side in range(GROUP)
        ]

    def begin(self):
        if not self.scatters:
            for unit in range(self.count):
                self.share_copy(unit).start()
            for unit in range(self.count):
                self.share_copy(unit).wait()
                self.gather_copy(unit, BITS - 1).start()
            return
        for unit in range(min(2, self.count)):
            start_all(self.loads(unit))
        for unit in range(self.count):
            wait_all(self.loads(unit))
            add_rows(self.held.at[unit], self.held.at[unit], 0, self.stage.at[unit % 2], 0, UNIT)
            self.scatter_copy(unit, 0).start()
            if unit + 2 < self.count:
                start_all(self.loads(unit + 2))

    def stages(self):
        return BITS * (self.scatters + self.gathers)

    def advance(self, unit, stage):
        if self.scatters and stage < BITS:
            self.scatter_copy(unit, stage).wait()
            keep, _, size = self.spans(unit)[stage]
            landing = UNIT - 2 * size
            target = self.final if self.gathers and stage == BITS - 1 else self.held
            add_rows(target.at[unit], self.held.at[unit], keep, self.arrived.at[unit], landing, size)
            if stage < BITS - 1:
                self.scatter_copy(unit, stage + 1).start()
            elif self.gathers:
                self.gather_copy(unit, BITS - 1).start()
            else:
                self.share_copy(unit).start()
            return
        step = BITS - 1 - (stage - BITS * self.scatters)
        self.gather_copy(unit, step).wait()
        if step:
            self.gather_copy(unit, step - 1).start()
        else:
            start_all(self.outs(unit))

    def finish(self):
        for unit in range(self.count):
            if self.gathers:
                wait_all(self.outs(unit))
            else:
                self.share_copy(unit).wait()


def bind_sums(sums, ins, outs, scratch):
    ins, outs, scratch = list(ins), list(outs), list(scratch)
    for one in sums:
        a, b, c = one.inputs(), 1, len(one.scratch())
        one.bind(ins[:a], outs[:b], scratch[:c])
        ins, outs, scratch = ins[a:], outs[b:], scratch[c:]


def run_steps(sums, steps):
    owners = [(one, unit) for one in sums for unit in range(one.count)]
    for unit, stage in steps:
        one, own = owners[unit]
        one.advance(own, stage)


class Blocks:
    def __init__(self, count, paired):
        self.count, self.paired = count, paired

    def out_shapes(self):
        rows = D // 2 if self.paired else D
        return [jax.ShapeDtypeStruct((self.count, rows, D), BF)] * (1 + self.paired)

    def scratch(self):
        return [pltpu.SemaphoreType.DMA((self.count,))] * (1 + 2 * self.paired)

    def bind(self, outs, sems):
        self.outs, self.sems = outs, sems

    def copies(self, block, lanes, ref, first_row):
        if not self.paired:
            return [
                pltpu.make_async_copy(
                    ref.at[pl.ds(first_row, D), lanes], self.outs[0].at[block], self.sems[0].at[block]
                )
            ]
        core = lax.axis_index("fsdp")
        half = D // 2
        mine = pl.multiple_of(first_row + core * half, half)
        theirs = pl.multiple_of(first_row + (1 - core) * half, half)
        return [
            pltpu.make_async_copy(
                ref.at[pl.ds(mine, half), lanes], self.outs[0].at[block], self.sems[0].at[block]
            ),
            pltpu.make_async_remote_copy(
                src_ref=ref.at[pl.ds(theirs, half), lanes], dst_ref=self.outs[1].at[block],
                send_sem=self.sems[1].at[block], recv_sem=self.sems[2].at[block],
                device_id=(lax.axis_index("dp"), 1 - core), device_id_type=MESH,
            ),
        ]


def my_half(paired):
    return lax.axis_index("fsdp") if paired else 0


def carve(refs, *sizes):
    found, at = [], 0
    for size in sizes:
        found.append(refs[at : at + size])
        at += size
    return found


def sums_in(sums):
    return sum(one.inputs() for one in sums)


def sums_scratch(sums):
    return [shape for one in sums for shape in one.scratch()]


def sums_outs(sums):
    return [shape for one in sums for shape in one.out_shapes()]


def remote_params(paired, collective_id):
    if not paired:
        return params()
    return pltpu.CompilerParams(
        dimension_semantics=("arbitrary",), vmem_limit_bytes=VMEM_LIMIT,
        collective_id=collective_id, has_side_effects=True,
    )


def ffn_back_kernel(blocks, store, sums, plan, dh_ref, before_ref, middle_ref, gain_ref, *refs):
    weights, ins, outs, store_outs, sum_outs, own_scratch, store_sems, sum_scratch = carve(
        refs, 4, sums_in(sums), 2, 1 + store.paired, len(sums), 7, 1 + 2 * store.paired,
        len(sums_scratch(sums)),
    )
    up_mine, up_other, down_mine, down_other = weights
    dmid_ref, dgain_ref = outs
    up, down, active, dbefore, dbranch, normed, sems = own_scratch
    store.bind(store_outs, store_sems)
    bind_sums(sums, ins, sum_outs, sum_scratch)
    step = pl.program_id(0)
    own = my_half(store.paired)
    up_copies = load_halves(own, up_mine, up_other, up, sems.at[0])
    down_copies = load_halves(own, down_mine, down_other, down, sems.at[1])
    parts = up.shape[1] // D
    rows = dh_ref.shape[0]

    @pl.when(step == 0)
    def _():
        start_all(down_copies)
        start_all(up_copies)
        dgain_ref[...] = jnp.zeros_like(dgain_ref)
        if store.paired:
            meet(BITS if sums else 0)
        for one in sums:
            one.begin()

    @pl.when(step < blocks)
    def _():
        here = pl.ds(pl.multiple_of(step * rows, rows), rows)
        dh = dh_ref[...].astype(F32)
        branch = dh.astype(BF)
        dbranch[here, :] = branch
        gain = gain_ref[1:2, :]
        unit, scale = normalise(middle_ref[...])
        normed[here, :] = (unit * gain).astype(BF)

        @pl.when(step == 0)
        def _():
            wait_all(down_copies)
            wait_all(up_copies)

        dnormed = jnp.zeros((rows, D), F32)
        for part in range(parts):
            lanes = slice(part * D, (part + 1) * D)
            dactive = dot_nt(branch, down[lanes, :])
            value = before_ref[:, lanes].astype(F32)
            root = math.sqrt(2.0 / math.pi)
            square = value * value
            curve = jnp.tanh(value * (root + (root * 0.044715) * square))
            half = 0.5 * (1.0 + curve)
            active[here, lanes] = (value * half).astype(BF)
            slope = half + (0.5 * value) * (1.0 - curve * curve) * (
                root + (3.0 * 0.044715 * root) * square
            )
            dpart = (dactive * slope).astype(BF)
            dbefore[here, lanes] = dpart
            dnormed = dnormed + dot_nt(dpart, up[:, lanes])
            for block in range(blocks):
                if block * parts + part in plan:

                    @pl.when(step == block)
                    def _():
                        run_steps(sums, plan[block * parts + part])

        dmid_ref[...] = dh + norm_back(dnormed, gain, unit, scale)
        dgain_ref[...] += column_sum(dnormed * unit)

    late = blocks * parts - blocks
    for tick in sorted(plan):
        if tick >= blocks * parts:

            @pl.when(step == tick - late)
            def _():
                run_steps(sums, plan[tick])

    every = slice(0, D)

    @pl.when((step >= blocks) & (step < blocks + parts))
    def _():
        part = step - blocks
        lanes = pl.ds(pl.multiple_of(part * D, D), D)
        up[:, lanes] = dot_tn(normed[...], dbefore[:, lanes]).astype(BF)
        start_all(store.copies(part, lanes, up, 0))

    @pl.when(step >= blocks + parts)
    def _():
        part = step - blocks - parts
        half = D // 2
        base = down.shape[0] // 2
        first_row = pl.multiple_of(part * D, D)
        for side in range(2):
            lanes = pl.ds(pl.multiple_of(side * base + part * half, half), half)
            here = pl.ds(pl.multiple_of(first_row + side * half, half), half)
            down[here, :] = dot_tn(active[:, lanes], dbranch[...]).astype(BF)
        start_all(store.copies(parts + part, every, down, first_row))

    @pl.when(step == blocks + 2 * parts - 1)
    def _():
        for part in range(parts):
            wait_all(store.copies(part, slice(part * D, (part + 1) * D), up, 0))
        for part in range(parts):
            wait_all(store.copies(parts + part, every, down, part * D))
        for one in sums:
            one.finish()


def ffn_backward(dh, before, middle, gains, shards, paired, sums, plan, sum_ins, collective_id):
    rows, width = before.shape
    block = min(512, rows)
    blocks = rows // block
    parts = width // D
    store = Blocks(2 * parts, paired)
    row = lambda w, **mode: pl.BlockSpec((block, w), lambda i: (jnp.minimum(i, blocks - 1), 0), **mode)
    once = {"pipeline_mode": pl.Buffered(1)}
    outs = store.out_shapes() + sums_outs(sums)
    return pl.pallas_call(
        functools.partial(ffn_back_kernel, blocks, store, sums, plan),
        name="ffn_backward",
        grid=(blocks + 2 * parts,),
        in_specs=[row(D, **once), row(width), row(D, **once), whole(gains.shape)] + [ANY] * (4 + len(sum_ins)),
        out_specs=[row(D), pl.BlockSpec((8, D), lambda i: (0, 0))] + [ANY] * len(outs),
        out_shape=[jax.ShapeDtypeStruct((rows, D), F32), jax.ShapeDtypeStruct((8, D), F32)] + outs,
        scratch_shapes=[
            pltpu.VMEM((D, width), BF),
            pltpu.VMEM((width, D), BF),
            pltpu.VMEM((rows, width), BF),
            pltpu.VMEM((rows, width), BF),
            pltpu.VMEM((rows, D), BF),
            pltpu.VMEM((rows, D), BF),
            pltpu.SemaphoreType.DMA((2, 2)),
        ]
        + store.scratch()
        + sums_scratch(sums),
        compiler_params=remote_params(paired, collective_id),
    )(dh, before, middle, gains, *shards, *sum_ins)


def window_at(block, count):
    return block - 1 + (count - 1 - block) // (count - 1) - block // (count - 1)


def attn_back_kernel(
    tile, reach, rows, store, sums, plan,
    dmid_ref, h_ref, q_ref, k_ref, v_ref, scale_q_ref, scale_k_ref,
    attended_ref, seg_ref, code_ref, gain_ref, heads_ref, spread_ref, *refs,
):
    weights, ins, outs, store_outs, sum_outs, own_scratch, store_sems, sum_scratch = carve(
        refs, 5, sums_in(sums), 2, 1 + store.paired, len(sums), 9, 1 + 2 * store.paired,
        len(sums_scratch(sums)),
    )
    normed_ref, qkv_mine, qkv_other, proj_mine, proj_other = weights
    dh_ref, dgain_ref = outs
    qkv, proj, dattended, inner, dk, dv, dmixed, sems, normed_sem = own_scratch
    store.bind(store_outs, store_sems)
    bind_sums(sums, ins, sum_outs, sum_scratch)
    step = pl.program_id(0)
    own = my_half(store.paired)
    total_rows = k_ref.shape[0]
    count = total_rows // tile
    keys = reach * tile
    blocks = total_rows // rows
    proj_copies = load_halves(own, proj_mine, proj_other, proj, sems.at[0])
    qkv_copies = load_halves(own, qkv_mine, qkv_other, qkv, sems.at[1])
    normed_copy = pltpu.make_async_copy(normed_ref, dattended, normed_sem)
    root = HEAD_DIM ** (-0.5)

    def head_norm_back(grad, gain, unit, scale):
        scaled = grad * gain
        first = split_dot(scaled, heads_ref[...]) * (1.0 / HEAD_DIM)
        second = split_dot(scaled * unit, heads_ref[...]) * (1.0 / HEAD_DIM)
        return split_dot(scale, spread_ref[...]) * (
            scaled - split_dot(first, spread_ref[...]) - unit * split_dot(second, spread_ref[...])
        )

    @pl.when(step == 0)
    def _():
        start_all(proj_copies)
        start_all(qkv_copies)
        dgain_ref[...] = jnp.zeros_like(dgain_ref)
        dk[...] = jnp.zeros_like(dk)
        dv[...] = jnp.zeros_like(dv)
        if store.paired:
            meet(BITS if sums else 0)
        for one in sums:
            one.begin()
        wait_all(proj_copies)
        for block in range(blocks):
            here = slice(block * rows, (block + 1) * rows)
            back = dot_nt(dmid_ref[here, :].astype(BF), proj[...]).astype(BF)
            dattended[here, :] = back
            product = back.astype(F32) * attended_ref[here, :].astype(F32)
            high = product.astype(BF)
            low = (product - high.astype(F32)).astype(BF)
            turn = (((0,), (1,)), ((), ()))
            inner[:, here] = lax.dot_general(
                heads_ref[...], high, turn, preferred_element_type=F32
            ) + lax.dot_general(heads_ref[...], low, turn, preferred_element_type=F32)

    for tick in sorted(plan):

        @pl.when(step == tick)
        def _():
            run_steps(sums, plan[tick])

    @pl.when(step < count)
    def _():
        first = pl.multiple_of(window_at(step, count) * tile if count > reach else 0, tile)
        window = pl.ds(first, keys)
        here = pl.ds(pl.multiple_of(step * tile, tile), tile)
        low_lanes = lax.broadcasted_iota(jnp.int32, (tile, 128), 1) < HEAD_DIM
        seg = seg_ref[:, here]
        code = code_ref[window, :]
        key_at = first + lax.broadcasted_iota(jnp.int32, (keys, tile), 0)
        query_at = step * tile + lax.broadcasted_iota(jnp.int32, (keys, tile), 1)
        bias = jnp.where((seg == code) | (query_at == key_at), 0.0, MASKED)
        bias = jnp.concatenate([bias, bias], axis=1)
        dq_parts = []
        for pair in range(HEADS // 2):
            lanes = slice(pair * 128, (pair + 1) * 128)
            queries = pair_stack(q_ref[here, lanes], low_lanes)
            grads = pair_stack(dattended[here, lanes], low_lanes)
            keys_part = k_ref[window, lanes]
            scores = dot_nt(keys_part, queries)
            expo = jnp.exp2(scores * (LOG2E * root) + bias)
            probs = expo * (1.0 / jnp.sum(expo, axis=0, keepdims=True))
            dprobs = dot_nt(v_ref[window, lanes], grads)
            less = jnp.concatenate(
                [inner[2 * pair : 2 * pair + 1, here], inner[2 * pair + 1 : 2 * pair + 2, here]],
                axis=1,
            )
            dscores = (probs * (dprobs - less)).astype(BF)
            dv[window, lanes] += dot(probs.astype(BF), grads)
            dk[window, lanes] += dot(dscores, queries)
            dq = dot_tn(dscores, keys_part)
            dq_parts.append(jnp.where(low_lanes, dq[:tile], dq[tile:]))
        dq = jnp.concatenate(dq_parts, axis=1) * root
        gain = gain_ref[2:3, :]
        unit = q_ref[here, :].astype(F32) * (1.0 / gain)
        dmixed[here, 0:D] = head_norm_back(dq, gain, unit, scale_q_ref[here, :]).astype(BF)
        dgain_ref[8:16, :] += column_sum(dq * unit)

    @pl.when(step == count)
    def _():
        normed_copy.start()
        wait_all(qkv_copies)

    @pl.when((step >= count) & (step < count + blocks))
    def _():
        here = pl.ds(pl.multiple_of((step - count) * rows, rows), rows)
        grad = dk[here, :] * root
        gain = gain_ref[3:4, :]
        unit = k_ref[here, :].astype(F32) * (1.0 / gain)
        dmixed[here, D : 2 * D] = head_norm_back(grad, gain, unit, scale_k_ref[here, :]).astype(BF)
        dgain_ref[16:24, :] += column_sum(grad * unit)
        dmixed[here, 2 * D :] = dv[here, :].astype(BF)
        dnormed = dot_nt(dmixed[here, :], qkv[...])
        unit, scale = normalise(h_ref[here, :].astype(F32))
        dh_ref[...] = dmid_ref[here, :] + norm_back(dnormed, gain_ref[0:1, :], unit, scale)
        dgain_ref[0:8, :] += column_sum(dnormed * unit)

    @pl.when(step == count + blocks)
    def _():
        normed_copy.wait()

    @pl.when((step >= count + blocks) & (step < count + blocks + 3))
    def _():
        part = step - count - blocks
        lanes = pl.ds(pl.multiple_of(part * D, D), D)
        qkv[:, lanes] = dot_tn(dattended[...], dmixed[:, lanes]).astype(BF)
        start_all(store.copies(part, lanes, qkv, 0))

    every = slice(0, D)

    @pl.when(step == count + blocks + 3)
    def _():
        proj[...] = dot_tn(attended_ref[...], dmid_ref[...].astype(BF)).astype(BF)
        start_all(store.copies(3, every, proj, 0))
        for part in range(3):
            wait_all(store.copies(part, slice(part * D, (part + 1) * D), qkv, 0))
        wait_all(store.copies(3, every, proj, 0))
        for one in sums:
            one.finish()


def attn_backward(
    dmid, h, saved, attended, segs, gains, heads, spread, shards, paired, sums, plan, sum_ins, collective_id
):
    total = h.shape[0]
    rows = min(512, total)
    tile = min(128, total)
    reach = min(3, total // tile)
    count, blocks = total // tile, total // rows
    normed, q, k, v, scale_q, scale_k = saved
    ins = [dmid, h, q, k, v, scale_q, scale_k, attended, *segs, gains, heads, spread]
    store = Blocks(4, paired)
    outs = store.out_shapes() + sums_outs(sums)
    return pl.pallas_call(
        functools.partial(attn_back_kernel, tile, reach, rows, store, sums, plan),
        name="attn_backward",
        grid=(count + blocks + 4,),
        in_specs=[whole(x.shape) for x in ins] + [ANY] * (5 + len(sum_ins)),
        out_specs=[
            pl.BlockSpec((rows, D), lambda i: (jnp.clip(i - count, 0, blocks - 1), 0)),
            pl.BlockSpec((24, D), lambda i: (0, 0)),
        ]
        + [ANY] * len(outs),
        out_shape=[jax.ShapeDtypeStruct((total, D), F32), jax.ShapeDtypeStruct((24, D), F32)] + outs,
        scratch_shapes=[
            pltpu.VMEM((D, 3 * D), BF),
            pltpu.VMEM((D, D), BF),
            pltpu.VMEM((total, D), BF),
            pltpu.VMEM((128, total), F32),
            pltpu.VMEM((total, D), F32),
            pltpu.VMEM((total, D), F32),
            pltpu.VMEM((total, 3 * D), BF),
            pltpu.SemaphoreType.DMA((2, 2)),
            pltpu.SemaphoreType.DMA,
        ]
        + store.scratch()
        + sums_scratch(sums),
        compiler_params=remote_params(paired, collective_id),
    )(*ins, normed, *shards, *sum_ins)


def last_sums_kernel(sums, steps, counts, *refs):
    n_in, n_out = counts
    small, ins = refs[0], refs[1 : 1 + n_in]
    small_total, outs = refs[1 + n_in], refs[2 + n_in : 2 + n_in + n_out]
    small_held, small_arrived, small_send, small_recv = refs[2 + n_in + n_out : 6 + n_in + n_out]
    bind_sums(sums, ins, outs, refs[6 + n_in + n_out :])
    me, core = lax.axis_index("dp"), lax.axis_index("fsdp")
    meet(BITS)

    def small_copy(step):
        to = (me, 1 - core) if step == 0 else (flip(me, step - 1), core)
        return pltpu.make_async_remote_copy(
            src_ref=small_held.at[step], dst_ref=small_arrived.at[step],
            send_sem=small_send.at[step], recv_sem=small_recv.at[step],
            device_id=to, device_id_type=MESH,
        )

    small_held[0] = small[...]
    small_copy(0).start()
    for one in sums:
        one.begin()
    each = -(-len(steps) // (BITS + 1))
    for stage in range(BITS + 1):
        run_steps(sums, steps[stage * each : (stage + 1) * each])
        small_copy(stage).wait()
        value = small_held[stage] + small_arrived[stage]
        if stage < BITS:
            small_held[stage + 1] = value
            small_copy(stage + 1).start()
        else:
            small_total[...] = value
    for one in sums:
        one.finish()


def last_sums(sums, steps, small, ins, collective_id):
    vmem = pl.BlockSpec(memory_space=pltpu.VMEM)
    outs = [shape for one in sums for shape in one.out_shapes()]
    return pl.pallas_call(
        functools.partial(last_sums_kernel, sums, steps, (len(ins), len(outs))),
        name="last_sums",
        in_specs=[vmem] + [ANY] * len(ins),
        out_specs=[vmem] + [ANY] * len(outs),
        out_shape=[jax.ShapeDtypeStruct(small.shape, F32)] + outs,
        scratch_shapes=[
            pltpu.VMEM((BITS + 1, *small.shape), F32),
            pltpu.VMEM((BITS + 1, *small.shape), F32),
            pltpu.SemaphoreType.DMA((BITS + 1,)),
            pltpu.SemaphoreType.DMA((BITS + 1,)),
        ]
        + [shape for one in sums for shape in one.scratch()],
        compiler_params=pltpu.CompilerParams(
            collective_id=collective_id, has_side_effects=True, vmem_limit_bytes=VMEM_LIMIT
        ),
    )(small, *ins)


CORRECTION = 1.0 - 0.5**STEP


def adam(weight, first, second, grad, rate, decay):
    first = 0.5 * first + 0.5 * grad
    second = 0.5 * second + 0.5 * grad * grad
    step = first / CORRECTION / (jnp.sqrt(second / CORRECTION) + adam_eps)
    return weight - rate * (step + decay * weight), first, second


def adam_kernel(weight_ref, first_ref, second_ref, *refs):
    grad_refs, outs = refs[:-3], refs[-3:]
    for layer, grad_ref in enumerate(grad_refs):

        @pl.when(pl.program_id(0) == layer)
        def _():
            results = adam(
                weight_ref[0], first_ref[0], second_ref[0], grad_ref[0].astype(F32), D ** (-0.5), 0.1
            )
            for out, result in zip(outs, results):
                out[0] = result


def adam_step(weight, first, second, totals, base):
    layers, rows, width = weight.shape
    half = D // 2
    down, across = rows // half, width // D
    last = down * across - 1
    part = pl.BlockSpec((1, half, D), lambda l, i, j: (l, i, j))

    def grad_spec(layer):
        def at(l, i, j):
            inside = jnp.where(l < layer, 0, last)
            return (base + jnp.where(l == layer, i * across + j, inside), 0, 0)

        return pl.BlockSpec((1, half, D), at)

    return pl.pallas_call(
        adam_kernel,
        name="adam_step",
        grid=(layers, down, across),
        in_specs=[part] * 3 + [grad_spec(layer) for layer in range(layers)],
        out_specs=[part] * 3,
        out_shape=[jax.ShapeDtypeStruct(weight.shape, F32)] * 3,
        compiler_params=params(3),
    )(weight, first, second, *totals)


def per_device(dp, fsdp, *args):
    tokens, cotangent, segments, keep_mask = args[:4]
    masters, firsts, seconds = args[4::3], args[5::3], args[6::3]
    packs, length, width = tokens.shape
    layers = masters[0].shape[0]
    paired = (dp, fsdp) == (1 << BITS, 2)
    me = lax.axis_index("fsdp")
    own = jnp.zeros((1,), jnp.int32) + (me if paired else 0)

    def halves(shard):
        if paired:
            return shard, lax.ppermute(shard, "fsdp", [(0, 1), (1, 0)])
        full = lax.all_gather(shard, "fsdp", axis=0, tiled=True)
        return full[: full.shape[0] // 2], full[full.shape[0] // 2 :]

    gathered = [
        [halves(masters[kind][layer].astype(BF)) for kind in range(4)] for layer in range(layers)
    ]
    gains_all = lax.all_gather(masters[4].astype(BF), "fsdp", axis=1, tiled=True).astype(F32)
    gains_all = jnp.pad(gains_all.transpose(0, 2, 1), ((0, 0), (0, 4), (0, 0)))
    heads = (
        lax.broadcasted_iota(jnp.int32, (D, 128), 0) // HEAD_DIM
        == lax.broadcasted_iota(jnp.int32, (D, 128), 1)
    ).astype(BF)
    spread = heads.T
    seg = segments[0]
    code = jnp.where(keep_mask[0] == 1, seg, -1)

    hidden = tokens[0]
    stored = []
    for layer in range(layers):
        qkv, proj, up, down = gathered[layer]
        gains = gains_all[layer]
        saved = qkv_forward(own, hidden, gains, heads, spread, *qkv)
        q, k, v = saved[1:4]
        last = layer == layers - 1
        attended, middle, before, result = mix_forward(
            own, hidden, q, k, v, seg[:, None], code[None, :], gains,
            (*proj, *up, *down), BF if last else F32,
        )
        stored.append((hidden, saved, attended, middle, before))
        hidden = result
    output = hidden.reshape(tokens.shape)

    made, shared = None, None
    totals = []
    d_hidden = cotangent[0]
    small = [None] * layers
    leaves = [None] * (2 * layers)
    for order, (layer, kind) in enumerate(
        (layer, kind) for layer in reversed(range(layers)) for kind in ("ffn", "attn")
    ):
        qkv, proj, up, down = gathered[layer]
        gains = gains_all[layer]
        h, saved, attended, middle, before = stored[layer]
        sums, sum_ins = [], []
        if paired and shared is not None:
            sums.append(Sum("gather", shared[1]))
            sum_ins.append(shared[0])
        if paired and made is not None:
            sums.append(Sum("scatter", made[1]))
            sum_ins += made[0]
        plan = PLANS[order - 1] if sums else {}
        if kind == "ffn":
            results = ffn_backward(
                d_hidden, before, middle, gains, (*up, *down), paired, sums, plan, sum_ins, order
            )
            d_middle, gain_two = results[:2]
        else:
            results = attn_backward(
                d_middle, h, saved, attended, (seg[None, :], code[:, None]), gains, heads, spread,
                (*qkv, *proj), paired, sums, plan, sum_ins, order,
            )
            d_hidden, gain_rest = results[:2]
            gain_rest = gain_rest.reshape(3, 8, D).sum(1)
            small[layer] = jnp.stack([gain_rest[0], gain_two.sum(0), gain_rest[1], gain_rest[2]])
        results = results[2:]
        leaves[order] = results[0]
        if paired:
            made, results = (results[:2], ORDERS[order]), results[2:]
            if shared is not None:
                totals.append(results[0])
                results = results[1:]
            shared = (results[0], sums[-1].orders) if results else None
    small = jnp.concatenate(small)
    input_grad = d_hidden.reshape(tokens.shape)

    updated = []
    wide = masters[2].shape[2] // D
    if paired:
        sums = [Sum("gather", shared[1]), Sum("both", made[1])]
        small, *rest = last_sums(sums, LAST_STEPS, small, [shared[0], *made[0]], 2 * layers)
        totals += rest
        totals = list(reversed(totals))
        for kind, (which, base) in enumerate(((0, 0), (0, 3), (1, 0), (1, wide))):
            updated.append(
                adam_step(masters[kind], firsts[kind], seconds[kind], totals[which::2], base)
            )
    else:
        small = lax.psum(small, ("dp", "fsdp"))
        leaves = list(reversed(leaves))
        attn, ffn = jnp.stack(leaves[0::2]), jnp.stack(leaves[1::2])
        across = lambda x: x.transpose(0, 2, 1, 3).reshape(layers, D, -1)
        full = (
            across(attn[:, :3]),
            attn[:, 3],
            across(ffn[:, :wide]),
            ffn[:, wide:].reshape(layers, wide, 2, D // 2, D).transpose(0, 2, 1, 3, 4)
            .reshape(layers, wide * D, D),
        )
        for kind in range(4):
            grad = lax.psum_scatter(full[kind], "fsdp", scatter_dimension=1, tiled=True)
            grad = lax.psum(grad, "dp").astype(F32)
            updated.append(adam(masters[kind], firsts[kind], seconds[kind], grad, D ** (-0.5), 0.1))
    small = small.reshape(layers, 4, D).transpose(0, 2, 1)
    share = masters[4].shape[1]
    small = lax.dynamic_slice_in_dim(small, me * share, share, 1)
    updated.append(adam(masters[4], firsts[4], seconds[4], small, 0.5, 0.0))
    return (output, input_grad, *[x for group in updated for x in group])


ORDERS = (
    (ZXY, XYZ, ZXY, XYZ, YZX, YXZ),
    (XYZ, ZYX, YXZ),
    (ZXY, ZYX, XYZ, YZX, ZYX, YXZ),
    (YXZ, XZY, ZXY),
)
PLANS = (
    {
        2: ((0, 0), (1, 0), (2, 0), (3, 0), (4, 0),),
        3: ((5, 0),),
        4: ((4, 1), (1, 1), (0, 1), (3, 1),),
        5: ((2, 1), (0, 2), (1, 2), (4, 2), (5, 1), (3, 2),),
        6: ((2, 2),),
        7: ((0, 3), (1, 3),),
        8: ((4, 3), (3, 3), (5, 2), (2, 3),),
        9: ((5, 3),),
    },
    {
        2: ((0, 0),),
        3: ((6, 0), (1, 0), (2, 0), (3, 0), (4, 0), (5, 0), (8, 0), (0, 1),),
        5: ((2, 1), (4, 1), (6, 1), (1, 1),),
        6: ((3, 1), (5, 1), (7, 0),),
        7: ((8, 1), (6, 2), (0, 2), (1, 2), (4, 2),),
        9: ((2, 2), (6, 3),),
        10: ((8, 2), (5, 2),),
        11: ((3, 2), (7, 1),),
        13: ((8, 3),),
        14: ((1, 3),),
        15: ((7, 2), (0, 3), (4, 3), (7, 3), (2, 3), (5, 3), (3, 3),),
    },
    {
        0: ((0, 0), (1, 0), (2, 0), (5, 0),),
        1: ((1, 1),),
        3: ((6, 0), (0, 1), (2, 1),),
        4: ((8, 0), (5, 1), (1, 2),),
        5: ((2, 2), (0, 2), (3, 0), (4, 0), (8, 1),),
        6: ((7, 0),),
        7: ((5, 2), (6, 1), (8, 2),),
        8: ((3, 1), (4, 1), (5, 3), (8, 3), (6, 2), (0, 3), (1, 3), (7, 1), (2, 3),),
        9: ((3, 2), (4, 2), (6, 3), (7, 2),),
        12: ((3, 3), (4, 3), (7, 3),),
    },
)
LAST_STEPS = ((0, 0), (1, 0), (6, 0), (2, 0), (7, 0), (3, 0), (4, 0), (5, 0), (0, 1), (1, 1), (2, 1), (5, 1), (3, 1), (4, 1), (7, 1), (6, 1), (1, 2), (0, 2), (8, 0), (5, 2), (2, 2), (7, 2), (8, 1), (6, 2), (4, 2), (3, 2), (7, 3), (8, 2), (6, 3), (2, 3), (7, 4), (8, 3), (6, 4), (5, 3), (7, 5), (3, 3), (8, 4), (8, 5), (6, 5), (1, 3), (0, 3), (8, 6), (7, 6), (6, 6), (4, 3), (8, 7), (7, 7), (6, 7))


def solution(mesh):
    rows = P(("dp", "fsdp"), None, None)
    weight = P(None, "fsdp", None)
    flat = P(("dp", "fsdp"), None)
    return jax.shard_map(
        functools.partial(per_device, mesh.shape["dp"], mesh.shape["fsdp"]),
        mesh=mesh,
        in_specs=(rows, rows, flat, flat) + (weight,) * 15,
        out_specs=(rows, rows) + (weight,) * 15,
        check_vma=False,
    )
```

time: 664 us -> 609 us (0.917)
  Pallas kernels: 607 us -> 553 us
    pallas_call x5, Pallas kernels: 441 us -> 386 us  [the longest x2 175 us: attn_backward(): pl.pallas_call(functools.partial(attn_back_kernel, tile, reach, rows, sto...]
  transfers between devices with their start and end apart: 8 -> 8, of which waited for: 0 -> 0; matrix products, arithmetic and copies ran while one was open for 3% -> 3% of each run, Pallas kernels for 11% -> 12%
where the time goes in v2:
time: 609 us; the launch traced here: 601 us
  Pallas kernels  553 us (91%)
  local copies, waits for them, and re-layouts  18.4 us (3%)
  blocking collectives  12.8 us (2%)
  other arithmetic  12.4 us (2%)
    pallas_call x2, Pallas kernels, attn_backward(): pl.pallas_call(functools.partial(attn_back_kernel, tile, reach, rows, sto...  175 us
    pallas_call x2, Pallas kernels, ffn_backward(): pl.pallas_call(functools.partial(ffn_back_kernel, blocks, store, sums, pl...  112 us
    pallas_call x1, Pallas kernels, last_sums(): pl.pallas_call(functools.partial(last_sums_kernel, sums, steps, (len(ins)...  99.1 us
    pallas_call x4, Pallas kernels, adam_step(): pl.pallas_call(adam_kernel, name='adam_step', grid=(layers, down, across)...  69.4 us
    pallas_call x2, Pallas kernels, mix_forward(): pl.pallas_call(functools.partial(mix_kernel, tile, reach), name='mix_forw...  56.8 us
    pallas_call x2, Pallas kernels, qkv_forward(): pl.pallas_call(qkv_kernel, name='qkv_forward', grid=(rows // block,), in_...  40.7 us
    all_gather x1, blocking collectives, per_device(): lax.all_gather(masters[4].astype(BF), 'fsdp', axis=1, tiled=True)  12.8 us
  transfers between devices with their start and end apart: 8, of which 0 were waited for; matrix products, arithmetic and copies ran while one was open for 3% of the time, Pallas kernels for 12%

profile of v2, /device:TPU:0, one launch (start us, length us, event | category | flops | bytes accessed | tf_op | source)
XLA Modules:
  0.0 600.6 jit_solution(4150334304848653398)
XLA Ops:
  0.7 0.0 copy-start
  0.7 3.5 convert.19
  4.2 2.0 slice_bitcast_fusion.4
  6.2 0.5 collective-permute-start
  6.7 1.0 copy-done
  7.6 3.1 convert.21
  10.7 5.5 slice_bitcast_fusion.1
  16.2 0.5 collective-permute-start.2
  16.7 0.1 convert.20
  16.8 1.0 slice_bitcast_fusion.6
  17.8 0.5 collective-permute-start.1
  18.3 0.5 convert.22
  18.8 0.0 copy-start.2
  18.8 0.0 copy-start.8
  18.8 0.0 copy-start.7
  18.8 0.0 copy-start.11
  18.8 2.5 slice_bitcast_fusion
  21.3 0.3 collective-permute-start.3
  21.6 0.2 collective-permute-start.6
  21.8 0.4 collective-permute-start.7
  22.2 0.1 collective-permute-start.4
  22.4 12.8 %all_gather.3 = bf16[2,768,4]{1,2,0:T(4,128)(2,1)S(1)} all-gather(bf16[2,384,4]{1,2,0:T(4,128)(2,1)S(1)} %convert_element_type.47), channel_id=1, replica_groups=mesh['dp'=16,'fsdp'=2] {'fsdp'}, dimensions={1}, use_global_device_ids=true | all-gather | bytes 18432 | tf_op jit(solution)/shard_map/all_gather | solution.py:985
  35.2 0.6 compare_select_fusion.code_ref
  35.8 0.6 slice_bitcast_fusion.8
  36.4 1.3 fusion.heads_ref
  37.7 0.3 collective-permute-start.5
  38.0 0.2 copy.36.seg_ref
  38.3 0.3 copy.38
  38.6 0.8 fusion.1.spread_ref
  39.3 0.9 broadcast_select_fusion.code_ref
  40.2 20.1 %qkv_forward.2 = (bf16[1024,768]{1,0:T(8,128)(2,1)}, bf16[1024,768]{1,0:T(8,128)(2,1)}, bf16[1024,768]{1,0:T(8,128)(2,1)}, bf16[1024,768]{1,0:T(8,128)(2,1)}, f32[1024,128]{1,0:T(8,128)}, /*index=5*/f32[1024,128]{1,0:T(8,128)}) custom-call(s32[1]{0:T(128)} %bitcast.own_ref, bf16[1024,768]{1,0:T(8,128)(2,1)} %bitcast.40, ...), custom_call_target="tpu_custom_call" | custom-call | tf_op jit(solution)/shard_map/qkv_forward/pallas_call | solution.py:132
  60.3 28.4 %mix_forward.2 = (bf16[1024,768]{1,0:T(8,128)(2,1)}, f32[1024,768]{1,0:T(8,128)}, bf16[1024,3072]{1,0:T(8,128)(2,1)}, f32[1024,768]{1,0:T(8,128)}) custom-call(s32[1]{0:T(128)} %bitcast.own_ref, bf16[1024,768]{1,0:T(8,128)(2,1)} %bitcast.41, bf16[1024,768]{1,0:T(8,128)(2,1)} %get-tuple-element.73.q_ref, bf16[1024,768]{1,0:T(8,128)(2,1)} %get-tuple-element.74.k_ref, ...), custom_call_target="tpu_custom_call" | custom-call | tf_op jit(solution)/shard_map/mix_forward/pallas_call | solution.py:234
  88.7 20.6 %qkv_forward.3 = (bf16[1024,768]{1,0:T(8,128)(2,1)}, bf16[1024,768]{1,0:T(8,128)(2,1)}, bf16[1024,768]{1,0:T(8,128)(2,1)}, bf16[1024,768]{1,0:T(8,128)(2,1)}, f32[1024,128]{1,0:T(8,128)}, /*index=5*/f32[1024,128]{1,0:T(8,128)}) custom-call(s32[1]{0:T(128)} %bitcast.own_ref, f32[1024,768]{1,0:T(8,128)} %get-tuple-element.76.h_ref, ...), custom_call_target="tpu_custom_call" | custom-call | tf_op jit(solution)/shard_map/qkv_forward/pallas_call | solution.py:132
  109.4 28.4 %mix_forward.3 = (bf16[1024,768]{1,0:T(8,128)(2,1)}, f32[1024,768]{1,0:T(8,128)}, bf16[1024,3072]{1,0:T(8,128)(2,1)}, bf16[1024,768]{1,0:T(8,128)(2,1)}) custom-call(s32[1]{0:T(128)} %bitcast.own_ref, f32[1024,768]{1,0:T(8,128)} %get-tuple-element.76.h_ref, bf16[1024,768]{1,0:T(8,128)(2,1)} %get-tuple-element.77.q_ref, ...), custom_call_target="tpu_custom_call" | custom-call | tf_op jit(solution)/shard_map/mix_forward/pallas_call | solution.py:234
  137.8 40.1 %ffn_backward.2 = (f32[1024,768]{1,0:T(8,128)}, f32[8,768]{1,0:T(8,128)}, bf16[8,384,768]{2,1,0:T(8,128)(2,1)}, bf16[8,384,768]{2,1,0:T(8,128)(2,1)}) custom-call(bf16[1024,768]{1,0:T(8,128)(2,1)} %bitcast.44, bf16[1024,3072]{1,0:T(8,128)(2,1)} %get-tuple-element.81.before_ref, f32[1024,768]{1,0:T(8,128)} %get-tuple-element.82.middle_ref, ...), custom_call_target="tpu_custom_call" | custom-call | tf_op jit(solution)/shard_map/ffn_backward/pallas_call | solution.py:653
  177.9 81.9 %attn_backward.2 = (f32[1024,768]{1,0:T(8,128)}, f32[24,768]{1,0:T(8,128)}, bf16[4,384,768]{2,1,0:T(8,128)(2,1)}, bf16[4,384,768]{2,1,0:T(8,128)(2,1)}, bf16[6,96,256]{2,1,0:T(8,128)(2,1)}) custom-call(f32[1024,768]{1,0:T(8,128)} %get-tuple-element.83.dmid_ref, f32[1024,768]{1,0:T(8,128)} %get-tuple-element.76.h_ref, ...), custom_call_target="tpu_custom_call" | custom-call | tf_op jit(solution)/shard_map/attn_backward/pallas_call | solution.py:834
  259.8 72.3 %ffn_backward.3 = (f32[1024,768]{1,0:T(8,128)}, f32[8,768]{1,0:T(8,128)}, bf16[8,384,768]{2,1,0:T(8,128)(2,1)}, bf16[8,384,768]{2,1,0:T(8,128)(2,1)}, bf16[8,384...) custom-call(f32[1024,768]{1,0:T(8,128)} %get-tuple-element.90.dh_ref, bf16[1024,3072]{1,0:T(8,128)(2,1)} %get-tuple-element.91.before_ref, ...), custom_call_target="tpu_custom_call" | custom-call | tf_op jit(solution)/shard_map/ffn_backward/pallas_call | solution.py:653
  332.1 92.7 %attn_backward.3 = (f32[1024,768]{1,0:T(8,128)}, f32[24,768]{1,0:T(8,128)}, bf16[4,384,768]{2,1,0:T(8,128)(2,1)}, bf16[4,384,768]{2,1,0:T(8,128)(2,1)}, bf16[4,3...) custom-call(f32[1024,768]{1,0:T(8,128)} %get-tuple-element.96.dmid_ref, bf16[1024,768]{1,0:T(8,128)(2,1)} %bitcast.42, ...), custom_call_target="tpu_custom_call" | custom-call | tf_op jit(solution)/shard_map/attn_backward/pallas_call | solution.py:834
  424.9 0.9 bitcast_reduce_fusion.1
  426.0 0.6 concatenate.3.refs_0_
  426.6 99.1 %last_sums.1 = (f32[8,768]{1,0:T(8,128)}, bf16[8,384,768]{2,1,0:T(8,128)(2,1)}, bf16[4,384,768]{2,1,0:T(8,128)(2,1)}) custom-call(f32[8,768]{1,0:T(8,128)} %concatenate.3.refs_0_, bf16[6,96,256]{2,1,0:T(8,128)(2,1)} %get-tuple-element.109.refs_1_, bf16[4,384,768]{2,1,0:T(8,128)(2,1)} %get-tuple-element.110.refs_2_, ...), custom_call_target="tpu_custom_call" | custom-call | tf_op jit(solution)/shard_map/last_sums/pallas_call | solution.py:900
  525.8 0.7 reshape.83
  526.5 22.9 %adam_step.7 = (f32[2,1536,768]{2,1,0:T(8,128)}, f32[2,1536,768]{2,1,0:T(8,128)}, f32[2,1536,768]{2,1,0:T(8,128)}) custom-call(f32[2,1536,768]{2,1,0:T(8,128)} %weight_ref.7, f32[2,1536,768]{2,1,0:T(8,128)} %first_ref.7, f32[2,1536,768]{2,1,0:T(8,128)} %second_ref.7, bf16[8,384,768]{2,1,0:T(8,128)(2,1)} %get-tuple-element.120.refs_0_, ...), custom_call_target="tpu_custom_call" | custom-call | tf_op jit(solution)/shard_map/adam_step/pallas_call | solution.py:956
  549.4 22.9 %adam_step.6 = (f32[2,384,3072]{2,1,0:T(8,128)}, f32[2,384,3072]{2,1,0:T(8,128)}, f32[2,384,3072]{2,1,0:T(8,128)}) custom-call(f32[2,384,3072]{2,1,0:T(8,128)} %weight_ref.6, f32[2,384,3072]{2,1,0:T(8,128)} %first_ref.6, f32[2,384,3072]{2,1,0:T(8,128)} %second_ref.6, bf16[8,384,768]{2,1,0:T(8,128)(2,1)} %get-tuple-element.120.refs_0_, ...), custom_call_target="tpu_custom_call" | custom-call | tf_op jit(solution)/shard_map/adam_step/pallas_call | solution.py:956
  572.3 6.1 %adam_step.5 = (f32[2,384,768]{2,1,0:T(8,128)}, f32[2,384,768]{2,1,0:T(8,128)}, f32[2,384,768]{2,1,0:T(8,128)}) custom-call(f32[2,384,768]{2,1,0:T(8,128)} %weight_ref.5, f32[2,384,768]{2,1,0:T(8,128)} %first_ref.5, f32[2,384,768]{2,1,0:T(8,128)} %second_ref.5, bf16[4,384,768]{2,1,0:T(8,128)(2,1)} %get-tuple-element.112.refs_0_, ...), custom_call_target="tpu_custom_call" | custom-call | tf_op jit(solution)/shard_map/adam_step/pallas_call | solution.py:956
  578.5 17.5 %adam_step.4 = (f32[2,384,2304]{2,1,0:T(8,128)}, f32[2,384,2304]{2,1,0:T(8,128)}, f32[2,384,2304]{2,1,0:T(8,128)}) custom-call(f32[2,384,2304]{2,1,0:T(8,128)} %weight_ref.4, f32[2,384,2304]{2,1,0:T(8,128)} %first_ref.4, f32[2,384,2304]{2,1,0:T(8,128)} %second_ref.4, bf16[4,384,768]{2,1,0:T(8,128)(2,1)} %get-tuple-element.112.refs_0_, ...), custom_call_target="tpu_custom_call" | custom-call | tf_op jit(solution)/shard_map/adam_step/pallas_call | solution.py:956
  596.0 0.6 multiply_subtract_fusion
  596.6 3.8 copy.41
  (51 shorter events, 0.2 us)
Async XLA Ops:
  0.7 7.0 %copy-start = (f32[2,384,3072]{2,1,0:T(8,128)S(1)}, f32[2,384,3072]{2,1,0:T(8,128)}, u32[]{:S(2)}) copy-start(f32[2,384,3072]{2,1,0:T(8,128)} %weight_ref.6) | copy-start | bytes 28311556
  6.2 16.0 %collective-permute-start = (bf16[384,2304]{1,0:T(8,128)(2,1)}, bf16[384,2304]{1,0:T(8,128)(2,1)}, u32[]{:S(2)}, u32[]{:S(2)}) collective-permute-start(bf16[384,2304]{1,0:T(8,128)(2,1)} %get-tuple-element.137.mine_ref.refs_1_), channel_id=1, source_target_pairs={{0,1},{1,0},{2,3},{3,2},{4,5},{5,4},{6,7},{7,6},{8,9},{9,8},{10,11... | collective-permute-start | bytes 5308424 | tf_op jit(solution)/shard_map/ppermute | solution.py:978
  7.6 10.7 %slice-start = ((s8[9437184]{0:T(1024)(128)(4,1)}), s8[4194304]{0:T(1024)(128)(4,1)S(1)}, s32[]{:S(2)}) async-start(s8[9437184]{0:T(1024)(128)(4,1)} %bitcast.38), calls=%async_computation | async-start | bytes 8388608
  7.6 10.7 %slice-start.1 = ((s8[9437184]{0:T(1024)(128)(4,1)}), s8[4194304]{0:T(1024)(128)(4,1)S(1)}, s32[]{:S(2)}) async-start(s8[9437184]{0:T(1024)(128)(4,1)} %bitcast.38), calls=%async_computation.1 | async-start | bytes 8388608
  10.7 6.0 copy-start.3
  10.7 7.6 %slice-start.2 = ((s8[9437184]{0:T(1024)(128)(4,1)}), s8[1048576]{0:T(1024)(128)(4,1)S(1)}, s32[]{:S(2)}) async-start(s8[9437184]{0:T(1024)(128)(4,1)} %bitcast.38), calls=%async_computation.2 | async-start | bytes 2097152
  16.2 1.6 copy-start.1
  16.2 21.5 %collective-permute-start.2 = (bf16[384,3072]{1,0:T(8,128)(2,1)S(1)}, bf16[384,3072]{1,0:T(8,128)(2,1)}, u32[]{:S(2)}, u32[]{:S(2)}) collective-permute-start(bf16[384,3072]{1,0:T(8,128)(2,1)S(1)} %get-tuple-element.135.up_mine.refs_0_), channel_id=1, source_target_pairs={{0,1},{1,0},{2,3},{3,2},{4,5},{5,4},{6,7},{7,6},{8,9},{9,8},{10,11... | collective-permute-start | bytes 7077896 | tf_op jit(solution)/shard_map/ppermute | solution.py:978
  17.8 0.9 copy-start.5
  17.8 4.0 collective-permute-start.1
  18.8 3.4 copy-start.2
  18.8 3.6 copy-start.8
  18.8 16.4 %copy-start.7 = (s32[1,1024]{1,0:T(1,128)S(1)}, s32[1,1024]{1,0:T(1,128)}, u32[]{:S(2)}) copy-start(s32[1,1024]{1,0:T(1,128)} %seg_ref.3) | copy-start | bytes 12292
  18.8 16.4 %copy-start.11 = (s32[1,1024]{1,0:T(1,128)S(1)}, s32[1,1024]{1,0:T(1,128)}, u32[]{:S(2)}) copy-start(s32[1,1024]{1,0:T(1,128)} %param.22) | copy-start | bytes 12292
  21.3 39.0 %collective-permute-start.3 = (bf16[1536,768]{1,0:T(8,128)(2,1)}, bf16[1536,768]{1,0:T(8,128)(2,1)}, u32[]{:S(2)}, u32[]{:S(2)}) collective-permute-start(bf16[1536,768]{1,0:T(8,128)(2,1)} %get-tuple-element.133.down_mine.refs_2_), channel_id=1, source_target_pairs={{0,1},{1,0},{2,3},{3,2},{4,5},{5,4},{6,7},{7,6},{8,9},{9,8},{10,11... | collective-permute-start | bytes 7077896 | tf_op jit(solution)/shard_map/ppermute | solution.py:978
  21.6 87.8 %collective-permute-start.6 = (bf16[384,3072]{1,0:T(8,128)(2,1)}, bf16[384,3072]{1,0:T(8,128)(2,1)}, u32[]{:S(2)}, u32[]{:S(2)}) collective-permute-start(bf16[384,3072]{1,0:T(8,128)(2,1)} %get-tuple-element.134.up_mine.refs_0_), channel_id=1, source_target_pairs={{0,1},{1,0},{2,3},{3,2},{4,5},{5,4},{6,7},{7,6},{8,9},{9,8},{10,11... | collective-permute-start | bytes 7077896 | tf_op jit(solution)/shard_map/ppermute | solution.py:978
  21.8 87.5 %collective-permute-start.7 = (bf16[1536,768]{1,0:T(8,128)(2,1)}, bf16[1536,768]{1,0:T(8,128)(2,1)}, u32[]{:S(2)}, u32[]{:S(2)}) collective-permute-start(bf16[1536,768]{1,0:T(8,128)(2,1)} %get-tuple-element.132.down_mine.refs_2_), channel_id=1, source_target_pairs={{0,1},{1,0},{2,3},{3,2},{4,5},{5,4},{6,7},{7,6},{8,9},{9,8},{10,11... | collective-permute-start | bytes 7077896 | tf_op jit(solution)/shard_map/ppermute | solution.py:978
  22.2 66.5 %collective-permute-start.4 = (bf16[384,2304]{1,0:T(8,128)(2,1)S(1)}, bf16[384,2304]{1,0:T(8,128)(2,1)}, u32[]{:S(2)}, u32[]{:S(2)}) collective-permute-start(bf16[384,2304]{1,0:T(8,128)(2,1)S(1)} %copy-done.2), channel_id=1, source_target_pairs={{0,1},{1,0},{2,3},{3,2},{4,5},{5,4},{6,7},{7,6},{8,9},{9,8},{10,11... | collective-permute-start | bytes 5308424 | tf_op jit(solution)/shard_map/ppermute | solution.py:978
  37.7 71.6 %collective-permute-start.5 = (bf16[384,768]{1,0:T(8,128)(2,1)}, bf16[384,768]{1,0:T(8,128)(2,1)}, u32[]{:S(2)}, u32[]{:S(2)}) collective-permute-start(bf16[384,768]{1,0:T(8,128)(2,1)} %get-tuple-element.138.proj_mine.refs_3_), channel_id=1, source_target_pairs={{0,1},{1,0},{2,3},{3,2},{4,5},{5,4},{6,7},{7,6},{8,9},{9,8},{10,11... | collective-permute-start | bytes 1769480 | tf_op jit(solution)/shard_map/ppermute | solution.py:978
  38.3 1.1 copy-start.4
  332.1 93.7 %copy-start.6 = (f32[24,768]{1,0:T(8,128)S(1)}, f32[24,768]{1,0:T(8,128)}, u32[]{:S(2)}) copy-start(f32[24,768]{1,0:T(8,128)} %get-tuple-element.107) | copy-start | bytes 221188
  332.1 93.8 %copy-start.10 = (f32[8,768]{1,0:T(8,128)S(1)}, f32[8,768]{1,0:T(8,128)}, u32[]{:S(2)}) copy-start(f32[8,768]{1,0:T(8,128)} %get-tuple-element.106) | copy-start | bytes 73732
  332.1 93.8 %copy-start.9 = (f32[8,768]{1,0:T(8,128)S(1)}, f32[8,768]{1,0:T(8,128)}, u32[]{:S(2)}) copy-start(f32[8,768]{1,0:T(8,128)} %get-tuple-element.108) | copy-start | bytes 73732
  578.4 17.5 %copy-start.12 = (f32[2,384,4]{1,2,0:T(4,128)S(1)}, f32[2,384,4]{1,2,0:T(4,128)}, u32[]{:S(2)}) copy-start(f32[2,384,4]{1,2,0:T(4,128)} %param.36) | copy-start | bytes 36868
  578.4 17.5 %copy-start.13 = (f32[2,384,4]{1,2,0:T(4,128)S(1)}, f32[2,384,4]{1,2,0:T(4,128)}, u32[]{:S(2)}) copy-start(f32[2,384,4]{1,2,0:T(4,128)} %param.37) | copy-start | bytes 36868

commit v3 on v2

--- a/solution.py
+++ b/solution.py
@@ -3,6 +3,7 @@
 
 import jax
 import jax.numpy as jnp
+import numpy as np
 from jax import lax
 from jax.experimental import pallas as pl
 from jax.experimental.pallas import tpu as pltpu
@@ -33,10 +34,17 @@
     return lax.dot_general(a, b, (((0,), (0,)), ((), ())), preferred_element_type=F32)
 
 
-def split_dot(x, mat):
-    high = x.astype(BF)
-    low = (x - high.astype(F32)).astype(BF)
-    return dot(high, mat) + dot(low, mat)
+def head_mean(x, mean_mat, exact=False):
+    width = mean_mat.shape[0]
+    found = []
+    for at in range(0, x.shape[1], width):
+        part = x[:, at : at + width]
+        high = part.astype(BF)
+        mean = dot(high, mean_mat)
+        if exact:
+            mean = mean + dot((part - high.astype(F32)).astype(BF), mean_mat)
+        found.append(mean)
+    return jnp.concatenate(found, axis=1)
 
 
 def normalise(values):
@@ -58,16 +66,6 @@
     return jnp.sum(x.reshape(x.shape[0] // 8, 8, x.shape[1]), axis=0)
 
 
-def load_halves(own, mine_ref, other_ref, full_ref, sems):
-    half = full_ref.shape[0] // 2
-    here = pl.multiple_of(own * half, half)
-    there = pl.multiple_of((1 - own) * half, half)
-    return (
-        pltpu.make_async_copy(mine_ref, full_ref.at[pl.ds(here, half)], sems.at[0]),
-        pltpu.make_async_copy(other_ref, full_ref.at[pl.ds(there, half)], sems.at[1]),
-    )
-
-
 def start_all(copies):
     for copy in copies:
         copy.start()
@@ -91,162 +89,6 @@
     return pltpu.CompilerParams(
         dimension_semantics=("arbitrary",) * steps, vmem_limit_bytes=VMEM_LIMIT
     )
-
-
-def qkv_kernel(
-    own_ref, h_ref, gain_ref, heads_ref, spread_ref, mine_ref, other_ref,
-    normed_ref, q_ref, k_ref, v_ref, scale_q_ref, scale_k_ref,
-    weight, sems,
-):
-    copies = load_halves(own_ref[0], mine_ref, other_ref, weight, sems)
-
-    @pl.when(pl.program_id(0) == 0)
-    def _():
-        start_all(copies)
-
-    unit, _ = normalise(h_ref[...].astype(F32))
-    normed = (unit * gain_ref[0:1, :]).astype(BF)
-    normed_ref[...] = normed
-
-    @pl.when(pl.program_id(0) == 0)
-    def _():
-        wait_all(copies)
-
-    v_ref[...] = dot(normed, weight[:, 2 * D :]).astype(BF)
-    for part, out_ref, scale_ref in ((0, q_ref, scale_q_ref), (1, k_ref, scale_k_ref)):
-        raw = dot(normed, weight[:, part * D : (part + 1) * D])
-        average = split_dot(raw, heads_ref[...]) * (1.0 / HEAD_DIM)
-        centred = raw - split_dot(average, spread_ref[...])
-        spread = split_dot(centred * centred, heads_ref[...]) * (1.0 / HEAD_DIM)
-        scale = lax.rsqrt(spread + norm_eps)
-        unit = centred * split_dot(scale, spread_ref[...])
-        out_ref[...] = (unit * gain_ref[2 + part : 3 + part, :]).astype(BF)
-        scale_ref[...] = scale
-
-
-def qkv_forward(own, h, gains, heads, spread, mine, other):
-    rows = h.shape[0]
-    block = min(512, rows)
-    row = lambda width: pl.BlockSpec((block, width), lambda i: (i, 0))
-    outs = [(D, BF)] * 4 + [(128, F32)] * 2
-    return pl.pallas_call(
-        qkv_kernel,
-        name="qkv_forward",
-        grid=(rows // block,),
-        in_specs=[SMEM, row(D), whole(gains.shape), whole(heads.shape), whole(spread.shape), ANY, ANY],
-        out_specs=[row(w) for w, _ in outs],
-        out_shape=[jax.ShapeDtypeStruct((rows, w), t) for w, t in outs],
-        scratch_shapes=[pltpu.VMEM((D, 3 * D), BF), pltpu.SemaphoreType.DMA((2,))],
-        compiler_params=params(),
-    )(own, h, gains, heads, spread, mine, other)
-
-
-def window_start(block, count, reach):
-    return jnp.clip(block - 1, 0, count - reach)
-
-
-def pair_stack(x, low_lanes):
-    zero = jnp.zeros_like(x)
-    return jnp.concatenate([jnp.where(low_lanes, x, zero), jnp.where(low_lanes, zero, x)], axis=0)
-
-
-def mix_kernel(
-    tile, reach,
-    own_ref, h_ref, q_ref, k_ref, v_ref, seg_ref, code_ref, gain_ref,
-    proj_mine, proj_other, up_mine, up_other, down_mine, down_other,
-    attended_ref, middle_ref, before_ref, out_ref,
-    proj, up, down, sems,
-):
-    step = pl.program_id(0)
-    own = own_ref[0]
-    proj_copies = load_halves(own, proj_mine, proj_other, proj, sems.at[0])
-    up_copies = load_halves(own, up_mine, up_other, up, sems.at[1])
-    down_copies = load_halves(own, down_mine, down_other, down, sems.at[2])
-
-    @pl.when(step == 0)
-    def _():
-        start_all(proj_copies)
-        start_all(up_copies)
-        start_all(down_copies)
-
-    rows = h_ref.shape[0]
-    count = k_ref.shape[0] // tile
-    keys = reach * tile
-    factor = LOG2E * HEAD_DIM ** (-0.5)
-    low_lanes = lax.broadcasted_iota(jnp.int32, (tile, 128), 1) < HEAD_DIM
-
-    def attend(inner, carry):
-        block = step * (rows // tile) + inner
-        first = pl.multiple_of(window_start(block, count, reach) * tile, tile)
-        here = pl.multiple_of(inner * tile, tile)
-        seg = seg_ref[pl.ds(here, tile), :]
-        code = code_ref[:, pl.ds(first, keys)]
-        query_at = block * tile + lax.broadcasted_iota(jnp.int32, (tile, keys), 0)
-        key_at = first + lax.broadcasted_iota(jnp.int32, (tile, keys), 1)
-        bias = jnp.where((seg == code) | (query_at == key_at), 0.0, MASKED)
-        bias = jnp.concatenate([bias, bias], axis=0)
-        for pair in range(HEADS // 2):
-            lanes = slice(pair * 128, (pair + 1) * 128)
-            queries = pair_stack(q_ref[pl.ds(here, tile), lanes], low_lanes)
-            scores = dot_nt(queries, k_ref[pl.ds(first, keys), lanes])
-            expo = jnp.exp2(scores * factor + bias)
-            total = jnp.sum(expo, axis=-1, keepdims=True)
-            mixed = dot(expo.astype(BF), v_ref[pl.ds(first, keys), lanes]) / total
-            attended_ref[pl.ds(here, tile), lanes] = jnp.where(
-                low_lanes, mixed[:tile], mixed[tile:]
-            ).astype(BF)
-        return carry
-
-    lax.fori_loop(0, rows // tile, attend, 0)
-
-    @pl.when(step == 0)
-    def _():
-        wait_all(proj_copies)
-
-    middle = h_ref[...].astype(F32) + dot(attended_ref[...], proj[...])
-    middle_ref[...] = middle
-    unit, _ = normalise(middle)
-    normed = (unit * gain_ref[1:2, :]).astype(BF)
-
-    @pl.when(step == 0)
-    def _():
-        wait_all(up_copies)
-        wait_all(down_copies)
-
-    result = middle
-    for part in range(up.shape[1] // D):
-        lanes = slice(part * D, (part + 1) * D)
-        before = dot(normed, up[:, lanes])
-        before_ref[:, lanes] = before.astype(BF)
-        active = jax.nn.gelu(before, approximate=True).astype(BF)
-        result = result + dot(active, down[lanes, :])
-    out_ref[...] = result.astype(out_ref.dtype)
-
-
-def mix_forward(own, h, q, k, v, seg, code, gains, shards, out_type):
-    rows = h.shape[0]
-    block = min(512, rows)
-    tile = min(128, rows)
-    reach = min(3, rows // tile)
-    width = shards[2].shape[1]
-    row = lambda w: pl.BlockSpec((block, w), lambda i: (i, 0))
-    outs = [(D, BF), (D, F32), (width, BF), (D, out_type)]
-    return pl.pallas_call(
-        functools.partial(mix_kernel, tile, reach),
-        name="mix_forward",
-        grid=(rows // block,),
-        in_specs=[SMEM, row(D), row(D), whole(k.shape), whole(v.shape), row(1), whole(code.shape), whole(gains.shape)]
-        + [ANY] * 6,
-        out_specs=[row(w) for w, _ in outs],
-        out_shape=[jax.ShapeDtypeStruct((rows, w), t) for w, t in outs],
-        scratch_shapes=[
-            pltpu.VMEM((D, D), BF),
-            pltpu.VMEM((D, width), BF),
-            pltpu.VMEM((width, D), BF),
-            pltpu.SemaphoreType.DMA((3, 2)),
-        ],
-        compiler_params=params(),
-    )(own, h, q, k, v, seg, code, gains, *shards)
 
 
 MESH = pl.DeviceIdType.MESH
@@ -464,6 +306,287 @@
         one.advance(own, stage)
 
 
+class Pull:
+    def __init__(self, shapes):
+        self.chunks = [
+            (which, down, across)
+            for which, (downs, acrosses) in enumerate(shapes)
+            for down in range(downs)
+            for across in range(acrosses)
+        ]
+        self.shapes = shapes
+
+    def scratch(self):
+        n = len(self.chunks)
+        return [
+            pltpu.VMEM((3, D // 2, D), F32),
+            pltpu.SemaphoreType.DMA((n,)),
+            pltpu.SemaphoreType.DMA((n,)),
+            pltpu.SemaphoreType.DMA((n,)),
+        ]
+
+    def bind(self, layer, sources, targets, scratch):
+        self.layer, self.sources, self.targets = layer, sources, targets
+        self.stage, self.loads, self.sends, self.recvs = scratch
+        self.me, self.core = lax.axis_index("dp"), lax.axis_index("fsdp")
+
+    def load(self, i):
+        which, down, across = self.chunks[i]
+        layer = self.layer[which]
+        return pltpu.make_async_copy(
+            self.sources[which].at[layer, pl.ds(down * (D // 2), D // 2), pl.ds(across * D, D)],
+            self.stage.at[i % 3],
+            self.loads.at[i],
+        )
+
+    def place(self, i):
+        which, down, across = self.chunks[i]
+        half = D // 2
+        first = pl.multiple_of(self.core * (self.shapes[which][0] * half) + down * half, half)
+        return pl.ds(first, half), pl.ds(across * D, D)
+
+    def push(self, i):
+        place = self.targets[self.chunks[i][0]].at[self.place(i)]
+        return pltpu.make_async_remote_copy(
+            src_ref=place, dst_ref=place, send_sem=self.sends.at[i], recv_sem=self.recvs.at[i],
+            device_id=(self.me, 1 - self.core), device_id_type=MESH,
+        )
+
+    def begin(self):
+        for i in range(min(3, len(self.chunks))):
+            self.load(i).start()
+
+    def turn(self, i):
+        self.load(i).wait()
+        self.targets[self.chunks[i][0]][self.place(i)] = self.stage[i % 3].astype(BF)
+        self.push(i).start()
+        if i + 3 < len(self.chunks):
+            self.load(i + 3).start()
+
+    def of(self, which):
+        return [i for i, chunk in enumerate(self.chunks) if chunk[0] == which]
+
+    def arrive(self, which):
+        for i in self.of(which):
+            self.push(i).wait()
+
+
+def qkv_kernel(pull, h_ref, gain_ref, mean_ref, source, *refs):
+    normed_ref, q_ref, k_ref, v_ref, scale_q_ref, scale_k_ref, full_ref = refs[:7]
+    weight, sem = refs[7:9]
+    step = pl.program_id(0)
+    keep = pltpu.make_async_copy(weight, full_ref, sem)
+    load = pltpu.make_async_copy(source, weight, sem)
+    if pull:
+        pull.bind([0], [source], [weight], refs[9:])
+
+    @pl.when(step == 0)
+    def _():
+        if pull:
+            pull.begin()
+            meet(0)
+            for i in range(len(pull.chunks)):
+                pull.turn(i)
+        else:
+            load.start()
+
+    unit, _ = normalise(h_ref[...].astype(F32))
+    normed = (unit * gain_ref[0:1, :]).astype(BF)
+    normed_ref[...] = normed
+
+    @pl.when(step == 0)
+    def _():
+        if pull:
+            pull.arrive(0)
+            keep.start()
+        else:
+            load.wait()
+
+    v_ref[...] = dot(normed, weight[:, 2 * D :]).astype(BF)
+    for part, out_ref, scale_ref in ((0, q_ref, scale_q_ref), (1, k_ref, scale_k_ref)):
+        raw = dot(normed, weight[:, part * D : (part + 1) * D])
+        centred = raw - head_mean(raw, mean_ref[...], exact=True)
+        scale = lax.rsqrt(head_mean(centred * centred, mean_ref[...]) + norm_eps)
+        out_ref[...] = (centred * scale * gain_ref[2 + part : 3 + part, :]).astype(BF)
+        scale_ref[...] = scale.astype(BF)
+
+    if pull:
+
+        @pl.when(step == pl.num_programs(0) - 1)
+        def _():
+            keep.wait()
+
+
+def qkv_forward(h, gains, mean_mat, source, fresh, collective_id):
+    rows = h.shape[0]
+    block = min(512, rows)
+    row = lambda width: pl.BlockSpec((block, width), lambda i: (i, 0))
+    pull = Pull([(1, 3)]) if fresh else None
+    full = [jax.ShapeDtypeStruct((D, 3 * D), BF)]
+    results = pl.pallas_call(
+        functools.partial(qkv_kernel, pull) if fresh else functools.partial(qkv_plain_kernel),
+        name="qkv_forward",
+        grid=(rows // block,),
+        in_specs=[row(D), whole(gains.shape), whole(mean_mat.shape), ANY],
+        out_specs=[row(D)] * 6 + [ANY] * fresh,
+        out_shape=[jax.ShapeDtypeStruct((rows, D), BF)] * 6 + full * fresh,
+        scratch_shapes=[pltpu.VMEM((D, 3 * D), BF), pltpu.SemaphoreType.DMA]
+        + (pull.scratch() if fresh else []),
+        compiler_params=remote_params(fresh, collective_id),
+    )(h, gains, mean_mat, source)
+    return results if fresh else [*results, source]
+
+
+def qkv_plain_kernel(h_ref, gain_ref, mean_ref, source, *refs):
+    qkv_kernel(None, h_ref, gain_ref, mean_ref, source, *refs[:6], source, *refs[6:])
+
+
+def window_at(block, count):
+    return block - 1 + (count - 1 - block) // (count - 1) - block // (count - 1)
+
+
+def pair_stack(x, low_lanes):
+    zero = jnp.zeros_like(x)
+    return jnp.concatenate([jnp.where(low_lanes, x, zero), jnp.where(low_lanes, zero, x)], axis=0)
+
+
+def mix_kernel(
+    tile, reach, pull, layer, follow, n_source,
+    h_ref, q_ref, k_ref, v_ref, seg_ref, code_ref, gain_ref, *refs,
+):
+    sources, outs, follows, scratch, pull_scratch = carve(
+        refs, n_source, 4 + (3 if pull else 0), int(follow), 4 + int(follow), len(refs)
+    )
+    attended_ref, middle_ref, before_ref, out_ref = outs[:4]
+    proj, up, down, sems = scratch[:4]
+    weights = (proj, up, down)
+    if pull:
+        targets = list(weights) + ([scratch[4]] if follow else [])
+        pull.bind([layer] * 3 + [layer + 1] * follow, sources, targets, pull_scratch)
+        keeps = [
+            pltpu.make_async_copy(weight, full, sems.at[i])
+            for i, (weight, full) in enumerate(zip(targets, outs[4:] + follows))
+        ]
+    else:
+        loads = [
+            pltpu.make_async_copy(source, weight, sems.at[i])
+            for i, (source, weight) in enumerate(zip(sources, weights))
+        ]
+    step = pl.program_id(0)
+    count = k_ref.shape[0] // tile
+    keys = reach * tile
+    factor = LOG2E * HEAD_DIM ** (-0.5)
+    low_lanes = lax.broadcasted_iota(jnp.int32, (tile, 128), 1) < HEAD_DIM
+
+    @pl.when(step == 0)
+    def _():
+        if pull:
+            pull.begin()
+            meet(0)
+        else:
+            start_all(loads)
+
+    @pl.when(step < count)
+    def _():
+        first = pl.multiple_of(window_at(step, count) * tile if count > reach else 0, tile)
+        window = pl.ds(first, keys)
+        here = pl.ds(pl.multiple_of(step * tile, tile), tile)
+        seg = seg_ref[here, :]
+        code = code_ref[:, window]
+        query_at = step * tile + lax.broadcasted_iota(jnp.int32, (tile, keys), 0)
+        key_at = first + lax.broadcasted_iota(jnp.int32, (tile, keys), 1)
+        bias = jnp.where((seg == code) | (query_at == key_at), 0.0, MASKED)
+        bias = jnp.concatenate([bias, bias], axis=0)
+        for pair in range(HEADS // 2):
+            lanes = slice(pair * 128, (pair + 1) * 128)
+            queries = pair_stack(q_ref[here, lanes], low_lanes)
+            scores = dot_nt(queries, k_ref[window, lanes])
+            expo = jnp.exp2(scores * factor + bias)
+            total = jnp.sum(expo, axis=-1, keepdims=True)
+            mixed = dot(expo.astype(BF), v_ref[window, lanes]) * (1.0 / total)
+            attended_ref[here, lanes] = jnp.where(low_lanes, mixed[:tile], mixed[tile:]).astype(BF)
+
+    if pull:
+        per_step = -(-len(pull.chunks) // count)
+        for turn in range(count):
+            mine = range(turn * per_step, min((turn + 1) * per_step, len(pull.chunks)))
+            if mine:
+
+                @pl.when(step == turn)
+                def _():
+                    for i in mine:
+                        pull.turn(i)
+
+    @pl.when(step == count)
+    def _():
+        if pull:
+            for which in range(3):
+                pull.arrive(which)
+                keeps[which].start()
+        else:
+            wait_all(loads)
+
+    @pl.when(step >= count)
+    def _():
+        rows = h_ref.shape[0]
+        here = pl.ds(pl.multiple_of((step - count) * rows, rows), rows)
+        middle = h_ref[...].astype(F32) + dot(attended_ref[here, :], proj[...])
+        middle_ref[...] = middle
+        unit, _ = normalise(middle)
+        normed = (unit * gain_ref[1:2, :]).astype(BF)
+        result = middle
+        for part in range(up.shape[1] // D):
+            lanes = slice(part * D, (part + 1) * D)
+            before = dot(normed, up[:, lanes])
+            before_ref[:, lanes] = before.astype(BF)
+            active = jax.nn.gelu(before, approximate=True).astype(BF)
+            result = result + dot(active, down[lanes, :])
+        out_ref[...] = result.astype(out_ref.dtype)
+
+    if pull:
+
+        @pl.when(step == pl.num_programs(0) - 1)
+        def _():
+            if follow:
+                pull.arrive(3)
+                keeps[3].start()
+            wait_all(keeps)
+
+
+def mix_forward(h, q, k, v, seg, code, gains, sources, out_type, layer, paired, collective_id):
+    rows = h.shape[0]
+    block = min(512, rows)
+    tile = min(128, rows)
+    reach = min(3, rows // tile)
+    count = rows // tile
+    width = sources[1].shape[-1]
+    follow = len(sources) > 3
+    shapes = [(1, 1), (1, width // D), (width // D, 1)] + [(1, 3)] * follow
+    pull = Pull(shapes) if paired else None
+    row = lambda w: pl.BlockSpec((block, w), lambda i: (jnp.maximum(i - count, 0), 0))
+    outs = [(D, F32), (width, BF), (D, out_type)]
+    fulls = [(D, D), (D, width), (width, D)]
+    follows = [(D, 3 * D)] * follow
+    results = pl.pallas_call(
+        functools.partial(mix_kernel, tile, reach, pull, layer, follow, len(sources)),
+        name="mix_forward",
+        grid=(count + rows // block,),
+        in_specs=[row(D)] + [whole(x.shape) for x in (q, k, v, seg, code, gains)] + [ANY] * len(sources),
+        out_specs=[pl.BlockSpec((rows, D), lambda i: (0, 0), pipeline_mode=pl.Buffered(1))]
+        + [row(w) for w, _ in outs]
+        + [ANY] * (len(fulls + follows) if paired else 0),
+        out_shape=[jax.ShapeDtypeStruct((rows, D), BF)]
+        + [jax.ShapeDtypeStruct((rows, w), t) for w, t in outs]
+        + [jax.ShapeDtypeStruct(x, BF) for x in (fulls + follows if paired else [])],
+        scratch_shapes=[pltpu.VMEM(x, BF) for x in fulls]
+        + [pltpu.SemaphoreType.DMA((4,))]
+        + [pltpu.VMEM(x, BF) for x in follows]
+        + (pull.scratch() if paired else []),
+        compiler_params=remote_params(paired, collective_id),
+    )(h, q, k, v, seg, code, gains, *sources)
+    return results if paired else [*results, *sources]
+
+
 class Blocks:
     def __init__(self, count, paired):
         self.count, self.paired = count, paired
@@ -501,10 +624,6 @@
         ]
 
 
-def my_half(paired):
-    return lax.axis_index("fsdp") if paired else 0
-
-
 def carve(refs, *sizes):
     found, at = [], 0
     for size in sizes:
@@ -536,25 +655,24 @@
 
 def ffn_back_kernel(blocks, store, sums, plan, dh_ref, before_ref, middle_ref, gain_ref, *refs):
     weights, ins, outs, store_outs, sum_outs, own_scratch, store_sems, sum_scratch = carve(
-        refs, 4, sums_in(sums), 2, 1 + store.paired, len(sums), 7, 1 + 2 * store.paired,
+        refs, 2, sums_in(sums), 2, 1 + store.paired, len(sums), 7, 1 + 2 * store.paired,
         len(sums_scratch(sums)),
     )
-    up_mine, up_other, down_mine, down_other = weights
     dmid_ref, dgain_ref = outs
     up, down, active, dbefore, dbranch, normed, sems = own_scratch
     store.bind(store_outs, store_sems)
     bind_sums(sums, ins, sum_outs, sum_scratch)
     step = pl.program_id(0)
-    own = my_half(store.paired)
-    up_copies = load_halves(own, up_mine, up_other, up, sems.at[0])
-    down_copies = load_halves(own, down_mine, down_other, down, sems.at[1])
+    copies = [
+        pltpu.make_async_copy(source, target, sems.at[i])
+        for i, (source, target) in enumerate(zip(weights, (up, down)))
+    ]
     parts = up.shape[1] // D
     rows = dh_ref.shape[0]
 
     @pl.when(step == 0)
     def _():
-        start_all(down_copies)
-        start_all(up_copies)
+        start_all(copies)
         dgain_ref[...] = jnp.zeros_like(dgain_ref)
         if store.paired:
             meet(BITS if sums else 0)
@@ -573,8 +691,7 @@
 
         @pl.when(step == 0)
         def _():
-            wait_all(down_copies)
-            wait_all(up_copies)
+            wait_all(copies)
 
         dnormed = jnp.zeros((rows, D), F32)
         for part in range(parts):
@@ -654,7 +771,7 @@
         functools.partial(ffn_back_kernel, blocks, store, sums, plan),
         name="ffn_backward",
         grid=(blocks + 2 * parts,),
-        in_specs=[row(D, **once), row(width), row(D, **once), whole(gains.shape)] + [ANY] * (4 + len(sum_ins)),
+        in_specs=[row(D, **once), row(width), row(D, **once), whole(gains.shape)] + [ANY] * (2 + len(sum_ins)),
         out_specs=[row(D), pl.BlockSpec((8, D), lambda i: (0, 0))] + [ANY] * len(outs),
         out_shape=[jax.ShapeDtypeStruct((rows, D), F32), jax.ShapeDtypeStruct((8, D), F32)] + outs,
         scratch_shapes=[
@@ -664,7 +781,7 @@
             pltpu.VMEM((rows, width), BF),
             pltpu.VMEM((rows, D), BF),
             pltpu.VMEM((rows, D), BF),
-            pltpu.SemaphoreType.DMA((2, 2)),
+            pltpu.SemaphoreType.DMA((2,)),
         ]
         + store.scratch()
         + sums_scratch(sums),
@@ -672,47 +789,40 @@
     )(dh, before, middle, gains, *shards, *sum_ins)
 
 
-def window_at(block, count):
-    return block - 1 + (count - 1 - block) // (count - 1) - block // (count - 1)
-
-
 def attn_back_kernel(
     tile, reach, rows, store, sums, plan,
     dmid_ref, h_ref, q_ref, k_ref, v_ref, scale_q_ref, scale_k_ref,
-    attended_ref, seg_ref, code_ref, gain_ref, heads_ref, spread_ref, *refs,
+    attended_ref, seg_ref, code_ref, gain_ref, heads_ref, mean_ref, *refs,
 ):
     weights, ins, outs, store_outs, sum_outs, own_scratch, store_sems, sum_scratch = carve(
-        refs, 5, sums_in(sums), 2, 1 + store.paired, len(sums), 9, 1 + 2 * store.paired,
+        refs, 3, sums_in(sums), 2, 1 + store.paired, len(sums), 9, 1 + 2 * store.paired,
         len(sums_scratch(sums)),
     )
-    normed_ref, qkv_mine, qkv_other, proj_mine, proj_other = weights
+    normed_ref, qkv_ref, proj_ref = weights
     dh_ref, dgain_ref = outs
     qkv, proj, dattended, inner, dk, dv, dmixed, sems, normed_sem = own_scratch
     store.bind(store_outs, store_sems)
     bind_sums(sums, ins, sum_outs, sum_scratch)
     step = pl.program_id(0)
-    own = my_half(store.paired)
     total_rows = k_ref.shape[0]
     count = total_rows // tile
     keys = reach * tile
     blocks = total_rows // rows
-    proj_copies = load_halves(own, proj_mine, proj_other, proj, sems.at[0])
-    qkv_copies = load_halves(own, qkv_mine, qkv_other, qkv, sems.at[1])
+    proj_copy = pltpu.make_async_copy(proj_ref, proj, sems.at[0])
+    qkv_copy = pltpu.make_async_copy(qkv_ref, qkv, sems.at[1])
     normed_copy = pltpu.make_async_copy(normed_ref, dattended, normed_sem)
     root = HEAD_DIM ** (-0.5)
 
     def head_norm_back(grad, gain, unit, scale):
         scaled = grad * gain
-        first = split_dot(scaled, heads_ref[...]) * (1.0 / HEAD_DIM)
-        second = split_dot(scaled * unit, heads_ref[...]) * (1.0 / HEAD_DIM)
-        return split_dot(scale, spread_ref[...]) * (
-            scaled - split_dot(first, spread_ref[...]) - unit * split_dot(second, spread_ref[...])
-        )
+        first = head_mean(scaled, mean_ref[...])
+        second = head_mean(scaled * unit, mean_ref[...])
+        return scale.astype(F32) * (scaled - first - unit * second)
 
     @pl.when(step == 0)
     def _():
-        start_all(proj_copies)
-        start_all(qkv_copies)
+        proj_copy.start()
+        qkv_copy.start()
         dgain_ref[...] = jnp.zeros_like(dgain_ref)
         dk[...] = jnp.zeros_like(dk)
         dv[...] = jnp.zeros_like(dv)
@@ -720,7 +830,7 @@
             meet(BITS if sums else 0)
         for one in sums:
             one.begin()
-        wait_all(proj_copies)
+        proj_copy.wait()
         for block in range(blocks):
             here = slice(block * rows, (block + 1) * rows)
             back = dot_nt(dmid_ref[here, :].astype(BF), proj[...]).astype(BF)
@@ -779,7 +889,7 @@
     @pl.when(step == count)
     def _():
         normed_copy.start()
-        wait_all(qkv_copies)
+        qkv_copy.wait()
 
     @pl.when((step >= count) & (step < count + blocks))
     def _():
@@ -820,7 +930,7 @@
 
 
 def attn_backward(
-    dmid, h, saved, attended, segs, gains, heads, spread, shards, paired, sums, plan, sum_ins, collective_id
+    dmid, h, saved, attended, segs, gains, heads, mean_mat, shards, paired, sums, plan, sum_ins, collective_id
 ):
     total = h.shape[0]
     rows = min(512, total)
@@ -828,14 +938,14 @@
     reach = min(3, total // tile)
     count, blocks = total // tile, total // rows
     normed, q, k, v, scale_q, scale_k = saved
-    ins = [dmid, h, q, k, v, scale_q, scale_k, attended, *segs, gains, heads, spread]
+    ins = [dmid, h, q, k, v, scale_q, scale_k, attended, *segs, gains, heads, mean_mat]
     store = Blocks(4, paired)
     outs = store.out_shapes() + sums_outs(sums)
     return pl.pallas_call(
         functools.partial(attn_back_kernel, tile, reach, rows, store, sums, plan),
         name="attn_backward",
         grid=(count + blocks + 4,),
-        in_specs=[whole(x.shape) for x in ins] + [ANY] * (5 + len(sum_ins)),
+        in_specs=[whole(x.shape) for x in ins] + [ANY] * (3 + len(sum_ins)),
         out_specs=[
             pl.BlockSpec((rows, D), lambda i: (jnp.clip(i - count, 0, blocks - 1), 0)),
             pl.BlockSpec((24, D), lambda i: (0, 0)),
@@ -850,7 +960,7 @@
             pltpu.VMEM((total, D), F32),
             pltpu.VMEM((total, D), F32),
             pltpu.VMEM((total, 3 * D), BF),
-            pltpu.SemaphoreType.DMA((2, 2)),
+            pltpu.SemaphoreType.DMA((2,)),
             pltpu.SemaphoreType.DMA,
         ]
         + store.scratch()
@@ -971,41 +1081,40 @@
     layers = masters[0].shape[0]
     paired = (dp, fsdp) == (1 << BITS, 2)
     me = lax.axis_index("fsdp")
-    own = jnp.zeros((1,), jnp.int32) + (me if paired else 0)
-
-    def halves(shard):
-        if paired:
-            return shard, lax.ppermute(shard, "fsdp", [(0, 1), (1, 0)])
-        full = lax.all_gather(shard, "fsdp", axis=0, tiled=True)
-        return full[: full.shape[0] // 2], full[full.shape[0] // 2 :]
-
-    gathered = [
-        [halves(masters[kind][layer].astype(BF)) for kind in range(4)] for layer in range(layers)
-    ]
+
+    def gather(shard):
+        return lax.all_gather(shard.astype(BF), "fsdp", axis=0, tiled=True)
+
     gains_all = lax.all_gather(masters[4].astype(BF), "fsdp", axis=1, tiled=True).astype(F32)
     gains_all = jnp.pad(gains_all.transpose(0, 2, 1), ((0, 0), (0, 4), (0, 0)))
-    heads = (
-        lax.broadcasted_iota(jnp.int32, (D, 128), 0) // HEAD_DIM
-        == lax.broadcasted_iota(jnp.int32, (D, 128), 1)
-    ).astype(BF)
-    spread = heads.T
+    channel = np.arange(D) // HEAD_DIM
+    heads = (channel[:, None] == np.arange(128)[None, :]).astype(BF)
+    mean_mat = ((channel[:256, None] == channel[None, :256]) / HEAD_DIM).astype(BF)
     seg = segments[0]
     code = jnp.where(keep_mask[0] == 1, seg, -1)
 
     hidden = tokens[0]
-    stored = []
+    stored, held = [], []
+    qkv = masters[0] if paired else gather(masters[0][0])
     for layer in range(layers):
-        qkv, proj, up, down = gathered[layer]
         gains = gains_all[layer]
-        saved = qkv_forward(own, hidden, gains, heads, spread, *qkv)
+        last = layer == layers - 1
+        fresh = paired and layer == 0
+        *saved, qkv = qkv_forward(hidden, gains, mean_mat, qkv, fresh, 2 * layers + 1)
         q, k, v = saved[1:4]
-        last = layer == layers - 1
-        attended, middle, before, result = mix_forward(
-            own, hidden, q, k, v, seg[:, None], code[None, :], gains,
-            (*proj, *up, *down), BF if last else F32,
+        if paired:
+            sources = [masters[kind] for kind in (1, 2, 3)] + ([] if last else [masters[0]])
+        else:
+            sources = [gather(masters[kind][layer]) for kind in (1, 2, 3)]
+        attended, middle, before, result, proj, up, down, *following = mix_forward(
+            hidden, q, k, v, seg[:, None], code[None, :], gains, sources, BF if last else F32,
+            layer, paired, 2 * layers + 2 + layer,
         )
         stored.append((hidden, saved, attended, middle, before))
+        held.append((qkv, proj, up, down))
         hidden = result
+        if not last:
+            qkv = following[0] if paired else gather(masters[0][layer + 1])
     output = hidden.reshape(tokens.shape)
 
     made, shared = None, None
@@ -1016,7 +1125,7 @@
     for order, (layer, kind) in enumerate(
         (layer, kind) for layer in reversed(range(layers)) for kind in ("ffn", "attn")
     ):
-        qkv, proj, up, down = gathered[layer]
+        qkv, proj, up, down = held[layer]
         gains = gains_all[layer]
         h, saved, attended, middle, before = stored[layer]
         sums, sum_ins = [], []
@@ -1029,13 +1138,13 @@
         plan = PLANS[order - 1] if sums else {}
         if kind == "ffn":
             results = ffn_backward(
-                d_hidden, before, middle, gains, (*up, *down), paired, sums, plan, sum_ins, order
+                d_hidden, before, middle, gains, (up, down), paired, sums, plan, sum_ins, order
             )
             d_middle, gain_two = results[:2]
         else:
             results = attn_backward(
-                d_middle, h, saved, attended, (seg[None, :], code[:, None]), gains, heads, spread,
-                (*qkv, *proj), paired, sums, plan, sum_ins, order,
+                d_middle, h, saved, attended, (seg[None, :], code[:, None]), gains, heads, mean_mat,
+                (qkv, proj), paired, sums, plan, sum_ins, order,
             )
             d_hidden, gain_rest = results[:2]
             gain_rest = gain_rest.reshape(3, 8, D).sum(1)

time: 609 us -> 563 us (0.924)
  Pallas kernels: 553 us -> 540 us
  local copies, waits for them, and re-layouts: 18.4 us -> 7.25 us
  blocking collectives: 12.8 us -> 1.92 us
  other arithmetic: 12.4 us -> 3.78 us
    convert_element_type x4 -> x0, local copies, waits for them, and re-layouts: 11 us -> none  [per_device(): masters[kind][layer].astype(BF)]
    all_gather x1, blocking collectives: 12.8 us -> 1.92 us  [per_device(): lax.all_gather(masters[4].astype(BF), 'fsdp', axis=1, tiled=True)]
    pallas_call x2, Pallas kernels: 175 us -> 167 us  [attn_backward(): pl.pallas_call(functools.partial(attn_back_kernel, tile, reach, rows, sto...]
    another operation x4 -> x0, other arithmetic: 7.18 us -> none
  transfers between devices with their start and end apart: 8 -> 0, of which waited for: 0 -> 0; matrix products, arithmetic and copies ran while one was open for 3% -> 0% of each run, Pallas kernels for 12% -> 0%
where the time goes in v3:
time: 563 us; the launch traced here: 554 us
  Pallas kernels  540 us (96%)
  local copies, waits for them, and re-layouts  7.25 us (1%)
    pallas_call x2, Pallas kernels, attn_backward(): pl.pallas_call(functools.partial(attn_back_kernel, tile, reach, rows, sto...  167 us
    pallas_call x2, Pallas kernels, ffn_backward(): pl.pallas_call(functools.partial(ffn_back_kernel, blocks, store, sums, pl...  112 us
    pallas_call x1, Pallas kernels, last_sums(): pl.pallas_call(functools.partial(last_sums_kernel, sums, steps, (len(ins)...  98.3 us
    pallas_call x4, Pallas kernels, adam_step(): pl.pallas_call(adam_kernel, name='adam_step', grid=(layers, down, across)...  69.4 us
    pallas_call x2, Pallas kernels, mix_forward(): pl.pallas_call(functools.partial(mix_kernel, tile, reach, pull, layer, fo...  65.3 us
    pallas_call x2, Pallas kernels, qkv_forward(): pl.pallas_call(functools.partial(qkv_kernel, pull) if fresh else functool...  27.6 us

profile of v3, /device:TPU:0, one launch (start us, length us, event | category | flops | bytes accessed | tf_op | source)
XLA Modules:
  0.0 554.0 jit_solution(12866439840658533490)
XLA Ops:
  0.7 0.7 convert_element_type.6
  1.4 1.9 all_gather.3
  3.3 0.6 slice_bitcast_fusion
  3.9 0.0 copy-start.3
  3.9 0.0 copy-start.8
  3.9 15.6 %qkv_forward.2 = (bf16[1024,768]{1,0:T(8,128)(2,1)}, bf16[1024,768]{1,0:T(8,128)(2,1)}, bf16[1024,768]{1,0:T(8,128)(2,1)}, bf16[1024,768]{1,0:T(8,128)(2,1)}, bf...) custom-call(bf16[1024,768]{1,0:T(8,128)(2,1)} %bitcast.21, ...), custom_call_target="tpu_custom_call" | custom-call | tf_op jit(solution)/shard_map/qkv_forward/pallas_call | solution.py:426
  19.5 0.0 copy-done.3
  19.5 1.0 copy.38.seg_ref
  20.6 0.0 copy-done.8
  20.6 0.6 compare_select_fusion.code_ref
  21.2 33.8 %mix_forward.2 = (bf16[1024,768]{1,0:T(8,128)(2,1)}, f32[1024,768]{1,0:T(8,128)}, bf16[1024,3072]{1,0:T(8,128)(2,1)}, f32[1024,768]{1,0:T(8,128)}, bf16[768,768]...) custom-call(bf16[1024,768]{1,0:T(8,128)(2,1)} %bitcast.22, ...), custom_call_target="tpu_custom_call" | custom-call | tf_op jit(solution)/shard_map/mix_forward/pallas_call | solution.py:570
  55.0 12.0 %qkv_forward.3 = (bf16[1024,768]{1,0:T(8,128)(2,1)}, bf16[1024,768]{1,0:T(8,128)(2,1)}, bf16[1024,768]{1,0:T(8,128)(2,1)}, bf16[1024,768]{1,0:T(8,128)(2,1)}, bf...) custom-call(f32[1024,768]{1,0:T(8,128)} %get-tuple-element.84.h_ref, f32[8,768]{1,0:T(8,128)} %get-tuple-element.148.gain_ref, ...), custom_call_target="tpu_custom_call" | custom-call | tf_op jit(solution)/shard_map/qkv_forward/pallas_call | solution.py:426
  67.0 31.5 %mix_forward.3 = (bf16[1024,768]{1,0:T(8,128)(2,1)}, f32[1024,768]{1,0:T(8,128)}, bf16[1024,3072]{1,0:T(8,128)(2,1)}, bf16[1024,768]{1,0:T(8,128)(2,1)}, bf16[76...) custom-call(f32[1024,768]{1,0:T(8,128)} %get-tuple-element.84.h_ref, ...), custom_call_target="tpu_custom_call" | custom-call | tf_op jit(solution)/shard_map/mix_forward/pallas_call | solution.py:570
  98.5 0.0 copy-start
  98.5 39.8 %ffn_backward.2 = (f32[1024,768]{1,0:T(8,128)}, f32[8,768]{1,0:T(8,128)}, bf16[8,384,768]{2,1,0:T(8,128)(2,1)}, bf16[8,384,768]{2,1,0:T(8,128)(2,1)}) custom-call(bf16[1024,768]{1,0:T(8,128)(2,1)} %bitcast.26, bf16[1024,3072]{1,0:T(8,128)(2,1)} %get-tuple-element.90.before_ref, f32[1024,768]{1,0:T(8,128)} %get-tuple-element.91.middle_ref, ...), custom_call_target="tpu_custom_call" | custom-call | tf_op jit(solution)/shard_map/ffn_backward/pallas_call | solution.py:770
  138.3 0.3 copy.40
  138.6 0.0 copy-done
  138.6 0.8 broadcast_select_fusion.code_ref
  139.5 77.6 %attn_backward.2 = (f32[1024,768]{1,0:T(8,128)}, f32[24,768]{1,0:T(8,128)}, bf16[4,384,768]{2,1,0:T(8,128)(2,1)}, bf16[4,384,768]{2,1,0:T(8,128)(2,1)}, bf16[6,96,256]{2,1,0:T(8,128)(2,1)}) custom-call(f32[1024,768]{1,0:T(8,128)} %get-tuple-element.94.dmid_ref, f32[1024,768]{1,0:T(8,128)} %get-tuple-element.84.h_ref, ...), custom_call_target="tpu_custom_call" | custom-call | tf_op jit(solution)/shard_map/attn_backward/pallas_call | solution.py:944
  217.1 72.4 %ffn_backward.3 = (f32[1024,768]{1,0:T(8,128)}, f32[8,768]{1,0:T(8,128)}, bf16[8,384,768]{2,1,0:T(8,128)(2,1)}, bf16[8,384,768]{2,1,0:T(8,128)(2,1)}, bf16[8,384...) custom-call(f32[1024,768]{1,0:T(8,128)} %get-tuple-element.102.dh_ref, bf16[1024,3072]{1,0:T(8,128)(2,1)} %get-tuple-element.103.before_ref, ...), custom_call_target="tpu_custom_call" | custom-call | tf_op jit(solution)/shard_map/ffn_backward/pallas_call | solution.py:770
  289.5 0.0 copy-start.6
  289.5 0.0 copy-start.2
  289.5 0.0 copy-start.5
  289.6 89.3 %attn_backward.3 = (f32[1024,768]{1,0:T(8,128)}, f32[24,768]{1,0:T(8,128)}, bf16[4,384,768]{2,1,0:T(8,128)(2,1)}, bf16[4,384,768]{2,1,0:T(8,128)(2,1)}, bf16[4,3...) custom-call(f32[1024,768]{1,0:T(8,128)} %get-tuple-element.110.dmid_ref, bf16[1024,768]{1,0:T(8,128)(2,1)} %bitcast.23, ...), custom_call_target="tpu_custom_call" | custom-call | tf_op jit(solution)/shard_map/attn_backward/pallas_call | solution.py:944
  378.9 0.9 bitcast_reduce_fusion.1
  379.8 0.0 copy-done.6
  379.8 0.0 copy-done.2
  379.9 0.0 copy-done.5
  379.9 0.6 concatenate.3.refs_0_
  380.6 98.3 %last_sums.1 = (f32[8,768]{1,0:T(8,128)}, bf16[8,384,768]{2,1,0:T(8,128)(2,1)}, bf16[4,384,768]{2,1,0:T(8,128)(2,1)}) custom-call(f32[8,768]{1,0:T(8,128)} %concatenate.3.refs_0_, bf16[6,96,256]{2,1,0:T(8,128)(2,1)} %get-tuple-element.125.refs_1_, bf16[4,384,768]{2,1,0:T(8,128)(2,1)} %get-tuple-element.126.refs_2_, ...), custom_call_target="tpu_custom_call" | custom-call | tf_op jit(solution)/shard_map/last_sums/pallas_call | solution.py:1010
  478.9 22.9 %adam_step.7 = (f32[2,1536,768]{2,1,0:T(8,128)}, f32[2,1536,768]{2,1,0:T(8,128)}, f32[2,1536,768]{2,1,0:T(8,128)}) custom-call(f32[2,1536,768]{2,1,0:T(8,128)} %weight_ref.7, f32[2,1536,768]{2,1,0:T(8,128)} %first_ref.7, f32[2,1536,768]{2,1,0:T(8,128)} %second_ref.7, bf16[8,384,768]{2,1,0:T(8,128)(2,1)} %get-tuple-element.136.refs_0_, ...), custom_call_target="tpu_custom_call" | custom-call | tf_op jit(solution)/shard_map/adam_step/pallas_call | solution.py:1066
  501.7 22.9 %adam_step.6 = (f32[2,384,3072]{2,1,0:T(8,128)}, f32[2,384,3072]{2,1,0:T(8,128)}, f32[2,384,3072]{2,1,0:T(8,128)}) custom-call(f32[2,384,3072]{2,1,0:T(8,128)} %weight_ref.6, f32[2,384,3072]{2,1,0:T(8,128)} %first_ref.6, f32[2,384,3072]{2,1,0:T(8,128)} %second_ref.6, bf16[8,384,768]{2,1,0:T(8,128)(2,1)} %get-tuple-element.136.refs_0_, ...), custom_call_target="tpu_custom_call" | custom-call | tf_op jit(solution)/shard_map/adam_step/pallas_call | solution.py:1066
  524.6 6.1 %adam_step.5 = (f32[2,384,768]{2,1,0:T(8,128)}, f32[2,384,768]{2,1,0:T(8,128)}, f32[2,384,768]{2,1,0:T(8,128)}) custom-call(f32[2,384,768]{2,1,0:T(8,128)} %weight_ref.5, f32[2,384,768]{2,1,0:T(8,128)} %first_ref.5, f32[2,384,768]{2,1,0:T(8,128)} %second_ref.5, bf16[4,384,768]{2,1,0:T(8,128)(2,1)} %get-tuple-element.128.refs_0_, ...), custom_call_target="tpu_custom_call" | custom-call | tf_op jit(solution)/shard_map/adam_step/pallas_call | solution.py:1066
  530.8 0.0 copy-start.7
  530.8 0.0 copy-start.4
  530.8 0.0 copy-start.9
  530.8 0.0 copy-start.10
  530.8 17.5 %adam_step.4 = (f32[2,384,2304]{2,1,0:T(8,128)}, f32[2,384,2304]{2,1,0:T(8,128)}, f32[2,384,2304]{2,1,0:T(8,128)}) custom-call(f32[2,384,2304]{2,1,0:T(8,128)} %weight_ref.4, f32[2,384,2304]{2,1,0:T(8,128)} %first_ref.4, f32[2,384,2304]{2,1,0:T(8,128)} %second_ref.4, bf16[4,384,768]{2,1,0:T(8,128)(2,1)} %get-tuple-element.128.refs_0_, ...), custom_call_target="tpu_custom_call" | custom-call | tf_op jit(solution)/shard_map/adam_step/pallas_call | solution.py:1066
  548.3 0.0 copy-start.1
  548.3 0.0 copy-done.7
  548.3 0.0 copy-done.4
  548.3 0.0 copy-done.9
  548.3 0.0 copy-done.10
  548.3 0.6 multiply_subtract_fusion
  549.0 2.9 copy.44
  551.9 0.0 copy-done.1
  551.9 1.7 copy.45
  (12 shorter events, 0.1 us)
Async XLA Ops:
  3.9 15.6 %copy-start.3 = (s32[1,1024]{1,0:T(1,128)S(1)}, s32[1,1024]{1,0:T(1,128)}, u32[]{:S(2)}) copy-start(s32[1,1024]{1,0:T(1,128)} %seg_ref.3) | copy-start | bytes 12292
  3.9 16.7 %copy-start.8 = (s32[1,1024]{1,0:T(1,128)S(1)}, s32[1,1024]{1,0:T(1,128)}, u32[]{:S(2)}) copy-start(s32[1,1024]{1,0:T(1,128)} %param.24) | copy-start | bytes 12292
  98.5 40.1 %copy-start = (s32[1024,1]{1,0:T(8,128)S(1)}, s32[1024,1]{1,0:T(8,128)}, u32[]{:S(2)}) copy-start(s32[1024,1]{1,0:T(8,128)} %copy.38.seg_ref) | copy-start | bytes 12292
  289.5 90.3 %copy-start.6 = (f32[8,768]{1,0:T(8,128)S(1)}, f32[8,768]{1,0:T(8,128)}, u32[]{:S(2)}) copy-start(f32[8,768]{1,0:T(8,128)} %get-tuple-element.122) | copy-start | bytes 73732
  289.5 90.3 %copy-start.2 = (f32[24,768]{1,0:T(8,128)S(1)}, f32[24,768]{1,0:T(8,128)}, u32[]{:S(2)}) copy-start(f32[24,768]{1,0:T(8,128)} %get-tuple-element.123) | copy-start | bytes 221188
  289.5 90.4 %copy-start.5 = (f32[8,768]{1,0:T(8,128)S(1)}, f32[8,768]{1,0:T(8,128)}, u32[]{:S(2)}) copy-start(f32[8,768]{1,0:T(8,128)} %get-tuple-element.124) | copy-start | bytes 73732
  530.8 17.5 %copy-start.7 = (f32[8,768]{1,0:T(8,128)S(1)}, f32[8,768]{1,0:T(8,128)}, u32[]{:S(2)}) copy-start(f32[8,768]{1,0:T(8,128)} %get-tuple-element.144) | copy-start | bytes 73732
  530.8 17.5 %copy-start.4 = (f32[2,384,4]{1,2,0:T(4,128)S(1)}, f32[2,384,4]{1,2,0:T(4,128)}, u32[]{:S(2)}) copy-start(f32[2,384,4]{1,2,0:T(4,128)} %param.37) | copy-start | bytes 36868
  530.8 17.5 %copy-start.9 = (f32[2,384,4]{1,2,0:T(4,128)S(1)}, f32[2,384,4]{1,2,0:T(4,128)}, u32[]{:S(2)}) copy-start(f32[2,384,4]{1,2,0:T(4,128)} %param.38) | copy-start | bytes 36868
  530.8 17.5 %copy-start.10 = (f32[2,384,4]{1,2,0:T(4,128)S(1)}, f32[2,384,4]{1,2,0:T(4,128)}, u32[]{:S(2)}) copy-start(f32[2,384,4]{1,2,0:T(4,128)} %param.39) | copy-start | bytes 36868
  548.3 3.6 copy-start.1

commit v4 on v3

--- a/solution.py
+++ b/solution.py
@@ -242,16 +242,20 @@
             for side in range(GROUP)
         ]
 
+    def prefetch(self):
+        if self.scatters:
+            for unit in range(min(2, self.count)):
+                start_all(self.loads(unit))
+        else:
+            for unit in range(self.count):
+                self.share_copy(unit).start()
+
     def begin(self):
         if not self.scatters:
-            for unit in range(self.count):
-                self.share_copy(unit).start()
             for unit in range(self.count):
                 self.share_copy(unit).wait()
                 self.gather_copy(unit, BITS - 1).start()
             return
-        for unit in range(min(2, self.count)):
-            start_all(self.loads(unit))
         for unit in range(self.count):
             wait_all(self.loads(unit))
             add_rows(self.held.at[unit], self.held.at[unit], 0, self.stage.at[unit % 2], 0, UNIT)
@@ -497,10 +501,17 @@
         key_at = first + lax.broadcasted_iota(jnp.int32, (tile, keys), 1)
         bias = jnp.where((seg == code) | (query_at == key_at), 0.0, MASKED)
         bias = jnp.concatenate([bias, bias], axis=0)
+
+        def front(pair):
+            lanes = slice(pair * 128, (pair + 1) * 128)
+            return dot_nt(pair_stack(q_ref[here, lanes], low_lanes), k_ref[window, lanes])
+
+        following = front(0)
         for pair in range(HEADS // 2):
             lanes = slice(pair * 128, (pair + 1) * 128)
-            queries = pair_stack(q_ref[here, lanes], low_lanes)
-            scores = dot_nt(queries, k_ref[window, lanes])
+            scores = following
+            if pair + 1 < HEADS // 2:
+                following = front(pair + 1)
             expo = jnp.exp2(scores * factor + bias)
             total = jnp.sum(expo, axis=-1, keepdims=True)
             mixed = dot(expo.astype(BF), v_ref[window, lanes]) * (1.0 / total)
@@ -674,6 +685,8 @@
     def _():
         start_all(copies)
         dgain_ref[...] = jnp.zeros_like(dgain_ref)
+        for one in sums:
+            one.prefetch()
         if store.paired:
             meet(BITS if sums else 0)
         for one in sums:
@@ -791,16 +804,22 @@
 
 def attn_back_kernel(
     tile, reach, rows, store, sums, plan,
-    dmid_ref, h_ref, q_ref, k_ref, v_ref, scale_q_ref, scale_k_ref,
-    attended_ref, seg_ref, code_ref, gain_ref, heads_ref, mean_ref, *refs,
+    seg_ref, code_ref, gain_ref, heads_ref, mean_ref, *refs,
 ):
+    sources, refs = refs[:8], refs[8:]
     weights, ins, outs, store_outs, sum_outs, own_scratch, store_sems, sum_scratch = carve(
-        refs, 3, sums_in(sums), 2, 1 + store.paired, len(sums), 9, 1 + 2 * store.paired,
+        refs, 3, sums_in(sums), 2, 1 + store.paired, len(sums), 18, 1 + 2 * store.paired,
         len(sums_scratch(sums)),
     )
     normed_ref, qkv_ref, proj_ref = weights
     dh_ref, dgain_ref = outs
-    qkv, proj, dattended, inner, dk, dv, dmixed, sems, normed_sem = own_scratch
+    qkv, proj, dattended, inner, dk, dv, dmixed, sems, normed_sem = own_scratch[:9]
+    held = own_scratch[9:17]
+    dmid_ref, attended_ref, q_ref, k_ref, v_ref, scale_q_ref, scale_k_ref, h_ref = held
+    loads = [
+        pltpu.make_async_copy(source, target, own_scratch[17].at[i])
+        for i, (source, target) in enumerate(zip(sources, held))
+    ]
     store.bind(store_outs, store_sems)
     bind_sums(sums, ins, sum_outs, sum_scratch)
     step = pl.program_id(0)
@@ -822,15 +841,19 @@
     @pl.when(step == 0)
     def _():
         proj_copy.start()
+        start_all(loads)
         qkv_copy.start()
         dgain_ref[...] = jnp.zeros_like(dgain_ref)
         dk[...] = jnp.zeros_like(dk)
         dv[...] = jnp.zeros_like(dv)
+        for one in sums:
+            one.prefetch()
         if store.paired:
             meet(BITS if sums else 0)
         for one in sums:
             one.begin()
         proj_copy.wait()
+        wait_all(loads[:2])
         for block in range(blocks):
             here = slice(block * rows, (block + 1) * rows)
             back = dot_nt(dmid_ref[here, :].astype(BF), proj[...]).astype(BF)
@@ -843,6 +866,8 @@
                 heads_ref[...], high, turn, preferred_element_type=F32
             ) + lax.dot_general(heads_ref[...], low, turn, preferred_element_type=F32)
 
+        wait_all(loads[2:6])
+
     for tick in sorted(plan):
 
         @pl.when(step == tick)
@@ -862,15 +887,23 @@
         bias = jnp.where((seg == code) | (query_at == key_at), 0.0, MASKED)
         bias = jnp.concatenate([bias, bias], axis=1)
         dq_parts = []
-        for pair in range(HEADS // 2):
+
+        def front(pair):
             lanes = slice(pair * 128, (pair + 1) * 128)
             queries = pair_stack(q_ref[here, lanes], low_lanes)
             grads = pair_stack(dattended[here, lanes], low_lanes)
             keys_part = k_ref[window, lanes]
             scores = dot_nt(keys_part, queries)
+            return queries, grads, keys_part, scores, dot_nt(v_ref[window, lanes], grads)
+
+        following = front(0)
+        for pair in range(HEADS // 2):
+            lanes = slice(pair * 128, (pair + 1) * 128)
+            queries, grads, keys_part, scores, dprobs = following
+            if pair + 1 < HEADS // 2:
+                following = front(pair + 1)
             expo = jnp.exp2(scores * (LOG2E * root) + bias)
             probs = expo * (1.0 / jnp.sum(expo, axis=0, keepdims=True))
-            dprobs = dot_nt(v_ref[window, lanes], grads)
             less = jnp.concatenate(
                 [inner[2 * pair : 2 * pair + 1, here], inner[2 * pair + 1 : 2 * pair + 2, here]],
                 axis=1,
@@ -890,6 +923,7 @@
     def _():
         normed_copy.start()
         qkv_copy.wait()
+        wait_all(loads[6:])
 
     @pl.when((step >= count) & (step < count + blocks))
     def _():
@@ -938,14 +972,15 @@
     reach = min(3, total // tile)
     count, blocks = total // tile, total // rows
     normed, q, k, v, scale_q, scale_k = saved
-    ins = [dmid, h, q, k, v, scale_q, scale_k, attended, *segs, gains, heads, mean_mat]
+    ins = [*segs, gains, heads, mean_mat]
+    large = [dmid, attended, q, k, v, scale_q, scale_k, h]
     store = Blocks(4, paired)
     outs = store.out_shapes() + sums_outs(sums)
     return pl.pallas_call(
         functools.partial(attn_back_kernel, tile, reach, rows, store, sums, plan),
         name="attn_backward",
         grid=(count + blocks + 4,),
-        in_specs=[whole(x.shape) for x in ins] + [ANY] * (3 + len(sum_ins)),
+        in_specs=[whole(x.shape) for x in ins] + [ANY] * (len(large) + 3 + len(sum_ins)),
         out_specs=[
             pl.BlockSpec((rows, D), lambda i: (jnp.clip(i - count, 0, blocks - 1), 0)),
             pl.BlockSpec((24, D), lambda i: (0, 0)),
@@ -963,10 +998,12 @@
             pltpu.SemaphoreType.DMA((2,)),
             pltpu.SemaphoreType.DMA,
         ]
+        + [pltpu.VMEM(x.shape, x.dtype) for x in large]
+        + [pltpu.SemaphoreType.DMA((len(large),))]
         + store.scratch()
         + sums_scratch(sums),
         compiler_params=remote_params(paired, collective_id),
-    )(*ins, normed, *shards, *sum_ins)
+    )(*ins, *large, normed, *shards, *sum_ins)
 
 
 def last_sums_kernel(sums, steps, counts, *refs):
@@ -976,6 +1013,8 @@
     small_held, small_arrived, small_send, small_recv = refs[2 + n_in + n_out : 6 + n_in + n_out]
     bind_sums(sums, ins, outs, refs[6 + n_in + n_out :])
     me, core = lax.axis_index("dp"), lax.axis_index("fsdp")
+    for one in sums:
+        one.prefetch()
     meet(BITS)
 
     def small_copy(step):
@@ -1195,49 +1234,50 @@
 
 
 ORDERS = (
-    (ZXY, XYZ, ZXY, XYZ, YZX, YXZ),
-    (XYZ, ZYX, YXZ),
-    (ZXY, ZYX, XYZ, YZX, ZYX, YXZ),
-    (YXZ, XZY, ZXY),
+    (XYZ, XZY, YXZ, YXZ, ZXY, ZYX),
+    (XZY, YZX, XYZ),
+    (XYZ, ZYX, YXZ, YZX, XZY, ZXY),
+    (YXZ, XYZ, ZXY),
 )
 PLANS = (
     {
-        2: ((0, 0), (1, 0), (2, 0), (3, 0), (4, 0),),
-        3: ((5, 0),),
-        4: ((4, 1), (1, 1), (0, 1), (3, 1),),
-        5: ((2, 1), (0, 2), (1, 2), (4, 2), (5, 1), (3, 2),),
-        6: ((2, 2),),
-        7: ((0, 3), (1, 3),),
-        8: ((4, 3), (3, 3), (5, 2), (2, 3),),
-        9: ((5, 3),),
+        4: ((0, 0), (1, 0), (2, 0), (3, 0),),
+        5: ((4, 0), (5, 0),),
+        6: ((0, 1), (1, 1),),
+        8: ((5, 1), (0, 2), (1, 2), (2, 1), (3, 1), (4, 1),),
+        9: ((5, 2), (0, 3), (4, 2), (1, 3),),
+        10: ((2, 2), (3, 2),),
+        11: ((5, 3),),
+        12: ((4, 3),),
+        13: ((2, 3), (3, 3),),
     },
     {
-        2: ((0, 0),),
-        3: ((6, 0), (1, 0), (2, 0), (3, 0), (4, 0), (5, 0), (8, 0), (0, 1),),
-        5: ((2, 1), (4, 1), (6, 1), (1, 1),),
-        6: ((3, 1), (5, 1), (7, 0),),
-        7: ((8, 1), (6, 2), (0, 2), (1, 2), (4, 2),),
-        9: ((2, 2), (6, 3),),
-        10: ((8, 2), (5, 2),),
-        11: ((3, 2), (7, 1),),
-        13: ((8, 3),),
-        14: ((1, 3),),
-        15: ((7, 2), (0, 3), (4, 3), (7, 3), (2, 3), (5, 3), (3, 3),),
+        2: ((0, 0), (1, 0), (2, 0), (7, 0), (3, 0), (4, 0), (5, 0),),
+        3: ((1, 1),),
+        4: ((4, 1), (6, 0), (0, 1), (5, 1), (8, 0), (2, 1),),
+        5: ((3, 1),),
+        6: ((7, 1), (4, 2),),
+        7: ((1, 2), (6, 1),),
+        8: ((2, 2), (0, 2), (5, 2), (8, 1),),
+        9: ((7, 2), (6, 2), (3, 2),),
+        13: ((7, 3), (6, 3), (4, 3), (8, 2),),
+        15: ((2, 3), (8, 3), (1, 3), (0, 3), (5, 3), (3, 3),),
     },
     {
-        0: ((0, 0), (1, 0), (2, 0), (5, 0),),
-        1: ((1, 1),),
-        3: ((6, 0), (0, 1), (2, 1),),
-        4: ((8, 0), (5, 1), (1, 2),),
-        5: ((2, 2), (0, 2), (3, 0), (4, 0), (8, 1),),
-        6: ((7, 0),),
-        7: ((5, 2), (6, 1), (8, 2),),
-        8: ((3, 1), (4, 1), (5, 3), (8, 3), (6, 2), (0, 3), (1, 3), (7, 1), (2, 3),),
-        9: ((3, 2), (4, 2), (6, 3), (7, 2),),
-        12: ((3, 3), (4, 3), (7, 3),),
+        0: ((0, 0), (1, 0), (2, 0),),
+        3: ((3, 0), (1, 1), (0, 1), (2, 1),),
+        4: ((7, 0), (5, 0),),
+        5: ((4, 0), (6, 0),),
+        6: ((8, 0), (5, 1),),
+        7: ((3, 1), (2, 2),),
+        8: ((4, 1), (8, 1),),
+        9: ((1, 2), (0, 2), (5, 2), (8, 2), (7, 1), (3, 2), (4, 2), (6, 1),),
+        10: ((2, 3),),
+        12: ((7, 2), (5, 3), (6, 2), (8, 3),),
+        13: ((3, 3), (4, 3), (1, 3), (0, 3), (7, 3), (6, 3),),
     },
 )
-LAST_STEPS = ((0, 0), (1, 0), (6, 0), (2, 0), (7, 0), (3, 0), (4, 0), (5, 0), (0, 1), (1, 1), (2, 1), (5, 1), (3, 1), (4, 1), (7, 1), (6, 1), (1, 2), (0, 2), (8, 0), (5, 2), (2, 2), (7, 2), (8, 1), (6, 2), (4, 2), (3, 2), (7, 3), (8, 2), (6, 3), (2, 3), (7, 4), (8, 3), (6, 4), (5, 3), (7, 5), (3, 3), (8, 4), (8, 5), (6, 5), (1, 3), (0, 3), (8, 6), (7, 6), (6, 6), (4, 3), (8, 7), (7, 7), (6, 7))
+LAST_STEPS = ((0, 0), (1, 0), (6, 0), (2, 0), (7, 0), (3, 0), (4, 0), (5, 0), (0, 1), (1, 1), (2, 1), (3, 1), (6, 1), (4, 1), (5, 1), (2, 2), (7, 1), (8, 0), (5, 2), (6, 2), (0, 2), (1, 2), (8, 1), (3, 2), (7, 2), (6, 3), (8, 2), (4, 2), (0, 3), (2, 3), (7, 3), (6, 4), (8, 3), (3, 3), (7, 4), (4, 3), (8, 4), (6, 5), (8, 5), (7, 5), (5, 3), (1, 3), (6, 6), (7, 6), (8, 6), (6, 7), (7, 7), (8, 7))
 
 
 def solution(mesh):

time: 563 us -> 518 us (0.920)
  Pallas kernels: 540 us -> 495 us
    pallas_call x2, Pallas kernels: 167 us -> 141 us  [attn_backward(): pl.pallas_call(functools.partial(attn_back_kernel, tile, reach, rows, sto...]
    pallas_call x1, Pallas kernels: 98.3 us -> 87.8 us  [last_sums(): pl.pallas_call(functools.partial(last_sums_kernel, sums, steps, (len(ins)...]
where the time goes in v4:
time: 518 us; the launch traced here: 509 us
  Pallas kernels  495 us (96%)
  local copies, waits for them, and re-layouts  7.25 us (1%)
    pallas_call x2, Pallas kernels, attn_backward(): pl.pallas_call(functools.partial(attn_back_kernel, tile, reach, rows, sto...  141 us
    pallas_call x2, Pallas kernels, ffn_backward(): pl.pallas_call(functools.partial(ffn_back_kernel, blocks, store, sums, pl...  110 us
    pallas_call x1, Pallas kernels, last_sums(): pl.pallas_call(functools.partial(last_sums_kernel, sums, steps, (len(ins)...  87.8 us
    pallas_call x4, Pallas kernels, adam_step(): pl.pallas_call(adam_kernel, name='adam_step', grid=(layers, down, across)...  69.4 us
    pallas_call x2, Pallas kernels, mix_forward(): pl.pallas_call(functools.partial(mix_kernel, tile, reach, pull, layer, fo...  59.8 us
    pallas_call x2, Pallas kernels, qkv_forward(): pl.pallas_call(functools.partial(qkv_kernel, pull) if fresh else functool...  27.6 us

profile of v4, /device:TPU:0, one launch (start us, length us, event | category | flops | bytes accessed | tf_op | source)
XLA Modules:
  0.0 509.1 jit_solution(11700633006156880214)
XLA Ops:
  0.7 0.7 convert_element_type.6
  1.4 1.9 all_gather.3
  3.3 0.6 slice_bitcast_fusion
  3.9 0.0 copy-start.3
  3.9 0.0 copy-start.8
  3.9 15.6 %qkv_forward.2 = (bf16[1024,768]{1,0:T(8,128)(2,1)}, bf16[1024,768]{1,0:T(8,128)(2,1)}, bf16[1024,768]{1,0:T(8,128)(2,1)}, bf16[1024,768]{1,0:T(8,128)(2,1)}, bf...) custom-call(bf16[1024,768]{1,0:T(8,128)(2,1)} %bitcast.21, ...), custom_call_target="tpu_custom_call" | custom-call | tf_op jit(solution)/shard_map/qkv_forward/pallas_call | solution.py:430
  19.5 0.0 copy-done.3
  19.5 1.0 copy.38.seg_ref
  20.6 0.0 copy-done.8
  20.6 0.6 compare_select_fusion.code_ref
  21.2 31.2 %mix_forward.2 = (bf16[1024,768]{1,0:T(8,128)(2,1)}, f32[1024,768]{1,0:T(8,128)}, bf16[1024,3072]{1,0:T(8,128)(2,1)}, f32[1024,768]{1,0:T(8,128)}, bf16[768,768]...) custom-call(bf16[1024,768]{1,0:T(8,128)(2,1)} %bitcast.22, ...), custom_call_target="tpu_custom_call" | custom-call | tf_op jit(solution)/shard_map/mix_forward/pallas_call | solution.py:581
  52.3 12.0 %qkv_forward.3 = (bf16[1024,768]{1,0:T(8,128)(2,1)}, bf16[1024,768]{1,0:T(8,128)(2,1)}, bf16[1024,768]{1,0:T(8,128)(2,1)}, bf16[1024,768]{1,0:T(8,128)(2,1)}, bf...) custom-call(f32[1024,768]{1,0:T(8,128)} %get-tuple-element.84.h_ref.refs_7_, f32[8,768]{1,0:T(8,128)} %get-tuple-element.148.gain_ref, ...), custom_call_target="tpu_custom_call" | custom-call | tf_op jit(solution)/shard_map/qkv_forward/pallas_call | solution.py:430
  64.4 28.7 %mix_forward.3 = (bf16[1024,768]{1,0:T(8,128)(2,1)}, f32[1024,768]{1,0:T(8,128)}, bf16[1024,3072]{1,0:T(8,128)(2,1)}, bf16[1024,768]{1,0:T(8,128)(2,1)}, bf16[76...) custom-call(f32[1024,768]{1,0:T(8,128)} %get-tuple-element.84.h_ref.refs_7_, ...), custom_call_target="tpu_custom_call" | custom-call | tf_op jit(solution)/shard_map/mix_forward/pallas_call | solution.py:581
  93.1 0.0 copy-start
  93.1 39.9 %ffn_backward.2 = (f32[1024,768]{1,0:T(8,128)}, f32[8,768]{1,0:T(8,128)}, bf16[8,384,768]{2,1,0:T(8,128)(2,1)}, bf16[8,384,768]{2,1,0:T(8,128)(2,1)}) custom-call(bf16[1024,768]{1,0:T(8,128)(2,1)} %bitcast.26, bf16[1024,3072]{1,0:T(8,128)(2,1)} %get-tuple-element.90.before_ref, f32[1024,768]{1,0:T(8,128)} %get-tuple-element.91.middle_ref, ...), custom_call_target="tpu_custom_call" | custom-call | tf_op jit(solution)/shard_map/ffn_backward/pallas_call | solution.py:783
  133.0 0.3 copy.40
  133.3 0.0 copy-done
  133.3 0.8 broadcast_select_fusion.code_ref
  134.1 64.2 %attn_backward.2 = (f32[1024,768]{1,0:T(8,128)}, f32[24,768]{1,0:T(8,128)}, bf16[4,384,768]{2,1,0:T(8,128)(2,1)}, bf16[4,384,768]{2,1,0:T(8,128)(2,1)}, bf16[6,96,256]{2,1,0:T(8,128)(2,1)}) custom-call(s32[1,1024]{1,0:T(1,128)} %seg_ref.3, s32[1024,1]{1,0:T(8,128)} %broadcast_select_fusion.code_ref, f32[8,768]{1,0:T(8,128)} %get-tuple-element.148.gain_ref, ...), custom_call_target="tpu_custom_call" | custom-call | tf_op jit(solution)/shard_map/attn_backward/pallas_call | solution.py:979
  198.3 69.7 %ffn_backward.3 = (f32[1024,768]{1,0:T(8,128)}, f32[8,768]{1,0:T(8,128)}, bf16[8,384,768]{2,1,0:T(8,128)(2,1)}, bf16[8,384,768]{2,1,0:T(8,128)(2,1)}, bf16[8,384...) custom-call(f32[1024,768]{1,0:T(8,128)} %get-tuple-element.102.dh_ref, bf16[1024,3072]{1,0:T(8,128)(2,1)} %get-tuple-element.103.before_ref, ...), custom_call_target="tpu_custom_call" | custom-call | tf_op jit(solution)/shard_map/ffn_backward/pallas_call | solution.py:783
  268.0 0.0 copy-start.6
  268.0 0.0 copy-start.2
  268.0 0.0 copy-start.5
  268.0 76.5 %attn_backward.3 = (f32[1024,768]{1,0:T(8,128)}, f32[24,768]{1,0:T(8,128)}, bf16[4,384,768]{2,1,0:T(8,128)(2,1)}, bf16[4,384,768]{2,1,0:T(8,128)(2,1)}, bf16[4,3...) custom-call(s32[1,1024]{1,0:T(1,128)} %seg_ref.3, s32[1024,1]{1,0:T(8,128)} %broadcast_select_fusion.code_ref, ...), custom_call_target="tpu_custom_call" | custom-call | tf_op jit(solution)/shard_map/attn_backward/pallas_call | solution.py:979
  344.5 0.9 bitcast_reduce_fusion.1
  345.4 0.0 copy-done.6
  345.5 0.0 copy-done.2
  345.6 0.0 copy-done.5
  345.6 0.6 concatenate.3.refs_0_
  346.2 87.8 %last_sums.1 = (f32[8,768]{1,0:T(8,128)}, bf16[8,384,768]{2,1,0:T(8,128)(2,1)}, bf16[4,384,768]{2,1,0:T(8,128)(2,1)}) custom-call(f32[8,768]{1,0:T(8,128)} %concatenate.3.refs_0_, bf16[6,96,256]{2,1,0:T(8,128)(2,1)} %get-tuple-element.125.refs_1_, bf16[4,384,768]{2,1,0:T(8,128)(2,1)} %get-tuple-element.126.refs_2_, ...), custom_call_target="tpu_custom_call" | custom-call | tf_op jit(solution)/shard_map/last_sums/pallas_call | solution.py:1049
  434.0 22.9 %adam_step.7 = (f32[2,1536,768]{2,1,0:T(8,128)}, f32[2,1536,768]{2,1,0:T(8,128)}, f32[2,1536,768]{2,1,0:T(8,128)}) custom-call(f32[2,1536,768]{2,1,0:T(8,128)} %weight_ref.7, f32[2,1536,768]{2,1,0:T(8,128)} %first_ref.7, f32[2,1536,768]{2,1,0:T(8,128)} %second_ref.7, bf16[8,384,768]{2,1,0:T(8,128)(2,1)} %get-tuple-element.136.refs_0_, ...), custom_call_target="tpu_custom_call" | custom-call | tf_op jit(solution)/shard_map/adam_step/pallas_call | solution.py:1105
  456.9 22.9 %adam_step.6 = (f32[2,384,3072]{2,1,0:T(8,128)}, f32[2,384,3072]{2,1,0:T(8,128)}, f32[2,384,3072]{2,1,0:T(8,128)}) custom-call(f32[2,384,3072]{2,1,0:T(8,128)} %weight_ref.6, f32[2,384,3072]{2,1,0:T(8,128)} %first_ref.6, f32[2,384,3072]{2,1,0:T(8,128)} %second_ref.6, bf16[8,384,768]{2,1,0:T(8,128)(2,1)} %get-tuple-element.136.refs_0_, ...), custom_call_target="tpu_custom_call" | custom-call | tf_op jit(solution)/shard_map/adam_step/pallas_call | solution.py:1105
  479.8 6.1 %adam_step.5 = (f32[2,384,768]{2,1,0:T(8,128)}, f32[2,384,768]{2,1,0:T(8,128)}, f32[2,384,768]{2,1,0:T(8,128)}) custom-call(f32[2,384,768]{2,1,0:T(8,128)} %weight_ref.5, f32[2,384,768]{2,1,0:T(8,128)} %first_ref.5, f32[2,384,768]{2,1,0:T(8,128)} %second_ref.5, bf16[4,384,768]{2,1,0:T(8,128)(2,1)} %get-tuple-element.128.refs_0_, ...), custom_call_target="tpu_custom_call" | custom-call | tf_op jit(solution)/shard_map/adam_step/pallas_call | solution.py:1105
  485.9 0.0 copy-start.7
  485.9 0.0 copy-start.4
  485.9 0.0 copy-start.9
  485.9 0.0 copy-start.10
  485.9 17.5 %adam_step.4 = (f32[2,384,2304]{2,1,0:T(8,128)}, f32[2,384,2304]{2,1,0:T(8,128)}, f32[2,384,2304]{2,1,0:T(8,128)}) custom-call(f32[2,384,2304]{2,1,0:T(8,128)} %weight_ref.4, f32[2,384,2304]{2,1,0:T(8,128)} %first_ref.4, f32[2,384,2304]{2,1,0:T(8,128)} %second_ref.4, bf16[4,384,768]{2,1,0:T(8,128)(2,1)} %get-tuple-element.128.refs_0_, ...), custom_call_target="tpu_custom_call" | custom-call | tf_op jit(solution)/shard_map/adam_step/pallas_call | solution.py:1105
  503.4 0.0 copy-start.1
  503.4 0.0 copy-done.7
  503.4 0.0 copy-done.4
  503.5 0.0 copy-done.9
  503.5 0.0 copy-done.10
  503.5 0.6 multiply_subtract_fusion
  504.1 2.9 copy.44
  507.0 0.0 copy-done.1
  507.0 1.7 copy.45
  (12 shorter events, 0.1 us)
Async XLA Ops:
  3.9 15.6 %copy-start.3 = (s32[1,1024]{1,0:T(1,128)S(1)}, s32[1,1024]{1,0:T(1,128)}, u32[]{:S(2)}) copy-start(s32[1,1024]{1,0:T(1,128)} %seg_ref.3) | copy-start | bytes 12292
  3.9 16.7 %copy-start.8 = (s32[1,1024]{1,0:T(1,128)S(1)}, s32[1,1024]{1,0:T(1,128)}, u32[]{:S(2)}) copy-start(s32[1,1024]{1,0:T(1,128)} %param.24) | copy-start | bytes 12292
  93.1 40.2 %copy-start = (s32[1024,1]{1,0:T(8,128)S(1)}, s32[1024,1]{1,0:T(8,128)}, u32[]{:S(2)}) copy-start(s32[1024,1]{1,0:T(8,128)} %copy.38.seg_ref) | copy-start | bytes 12292
  268.0 77.5 %copy-start.6 = (f32[8,768]{1,0:T(8,128)S(1)}, f32[8,768]{1,0:T(8,128)}, u32[]{:S(2)}) copy-start(f32[8,768]{1,0:T(8,128)} %get-tuple-element.122) | copy-start | bytes 73732
  268.0 77.5 %copy-start.2 = (f32[24,768]{1,0:T(8,128)S(1)}, f32[24,768]{1,0:T(8,128)}, u32[]{:S(2)}) copy-start(f32[24,768]{1,0:T(8,128)} %get-tuple-element.123) | copy-start | bytes 221188
  268.0 77.5 %copy-start.5 = (f32[8,768]{1,0:T(8,128)S(1)}, f32[8,768]{1,0:T(8,128)}, u32[]{:S(2)}) copy-start(f32[8,768]{1,0:T(8,128)} %get-tuple-element.124) | copy-start | bytes 73732
  485.9 17.5 %copy-start.7 = (f32[8,768]{1,0:T(8,128)S(1)}, f32[8,768]{1,0:T(8,128)}, u32[]{:S(2)}) copy-start(f32[8,768]{1,0:T(8,128)} %get-tuple-element.144) | copy-start | bytes 73732
  485.9 17.5 %copy-start.4 = (f32[2,384,4]{1,2,0:T(4,128)S(1)}, f32[2,384,4]{1,2,0:T(4,128)}, u32[]{:S(2)}) copy-start(f32[2,384,4]{1,2,0:T(4,128)} %param.37) | copy-start | bytes 36868
  485.9 17.5 %copy-start.9 = (f32[2,384,4]{1,2,0:T(4,128)S(1)}, f32[2,384,4]{1,2,0:T(4,128)}, u32[]{:S(2)}) copy-start(f32[2,384,4]{1,2,0:T(4,128)} %param.38) | copy-start | bytes 36868
  485.9 17.5 %copy-start.10 = (f32[2,384,4]{1,2,0:T(4,128)S(1)}, f32[2,384,4]{1,2,0:T(4,128)}, u32[]{:S(2)}) copy-start(f32[2,384,4]{1,2,0:T(4,128)} %param.39) | copy-start | bytes 36868
  503.4 3.6 copy-start.1

commit v5 on v4

--- a/solution.py
+++ b/solution.py
@@ -123,7 +123,7 @@
     def body(i, carry):
         here = pl.ds(pl.multiple_of(at + i * chunk, chunk), chunk)
         there = pl.ds(pl.multiple_of(other_at + i * chunk, chunk), chunk)
-        target[here, :] = (source[here, :].astype(F32) + other[there, :].astype(F32)).astype(BF)
+        target[here, :] = source[here, :] + other[there, :]
         return carry
 
     lax.fori_loop(0, rows // chunk, body, 0)
@@ -706,10 +706,17 @@
         def _():
             wait_all(copies)
 
+        def front(part):
+            return dot_nt(branch, down[part * D : (part + 1) * D, :])
+
         dnormed = jnp.zeros((rows, D), F32)
+        early = not sums
+        following = front(0) if early else None
         for part in range(parts):
             lanes = slice(part * D, (part + 1) * D)
-            dactive = dot_nt(branch, down[lanes, :])
+            dactive = following if early else front(part)
+            if early and part + 1 < parts:
+                following = front(part + 1)
             value = before_ref[:, lanes].astype(F32)
             root = math.sqrt(2.0 / math.pi)
             square = value * value
@@ -778,7 +785,7 @@
     parts = width // D
     store = Blocks(2 * parts, paired)
     row = lambda w, **mode: pl.BlockSpec((block, w), lambda i: (jnp.minimum(i, blocks - 1), 0), **mode)
-    once = {"pipeline_mode": pl.Buffered(1)}
+    once = {"pipeline_mode": pl.Buffered(1)} if sums else {}
     outs = store.out_shapes() + sums_outs(sums)
     return pl.pallas_call(
         functools.partial(ffn_back_kernel, blocks, store, sums, plan),

time: 518 us -> 515 us (level)
  no operation moved by 1% of the time
where the time goes in v5:
time: 515 us; the launch traced here: 506 us
  Pallas kernels  491 us (95%)
  local copies, waits for them, and re-layouts  7.25 us (1%)
    pallas_call x2, Pallas kernels, attn_backward(): pl.pallas_call(functools.partial(attn_back_kernel, tile, reach, rows, sto...  139 us
    pallas_call x2, Pallas kernels, ffn_backward(): pl.pallas_call(functools.partial(ffn_back_kernel, blocks, store, sums, pl...  107 us
    pallas_call x1, Pallas kernels, last_sums(): pl.pallas_call(functools.partial(last_sums_kernel, sums, steps, (len(ins)...  88.3 us
    pallas_call x4, Pallas kernels, adam_step(): pl.pallas_call(adam_kernel, name='adam_step', grid=(layers, down, across)...  69.4 us
    pallas_call x2, Pallas kernels, mix_forward(): pl.pallas_call(functools.partial(mix_kernel, tile, reach, pull, layer, fo...  59.8 us
    pallas_call x2, Pallas kernels, qkv_forward(): pl.pallas_call(functools.partial(qkv_kernel, pull) if fresh else functool...  27.6 us

profile of v5, /device:TPU:0, one launch (start us, length us, event | category | flops | bytes accessed | tf_op | source)
XLA Modules:
  0.0 505.7 jit_solution(15968242092387144416)
XLA Ops:
  0.7 0.7 convert_element_type.6
  1.4 1.9 all_gather.3
  3.3 0.6 slice_bitcast_fusion
  3.9 0.0 copy-start.3
  3.9 0.0 copy-start.8
  3.9 15.6 %qkv_forward.2 = (bf16[1024,768]{1,0:T(8,128)(2,1)}, bf16[1024,768]{1,0:T(8,128)(2,1)}, bf16[1024,768]{1,0:T(8,128)(2,1)}, bf16[1024,768]{1,0:T(8,128)(2,1)}, bf...) custom-call(bf16[1024,768]{1,0:T(8,128)(2,1)} %bitcast.21, ...), custom_call_target="tpu_custom_call" | custom-call | tf_op jit(solution)/shard_map/qkv_forward/pallas_call | solution.py:430
  19.5 0.0 copy-done.3
  19.5 1.0 copy.38.seg_ref
  20.6 0.0 copy-done.8
  20.6 0.6 compare_select_fusion.code_ref
  21.2 31.2 %mix_forward.2 = (bf16[1024,768]{1,0:T(8,128)(2,1)}, f32[1024,768]{1,0:T(8,128)}, bf16[1024,3072]{1,0:T(8,128)(2,1)}, f32[1024,768]{1,0:T(8,128)}, bf16[768,768]...) custom-call(bf16[1024,768]{1,0:T(8,128)(2,1)} %bitcast.22, ...), custom_call_target="tpu_custom_call" | custom-call | tf_op jit(solution)/shard_map/mix_forward/pallas_call | solution.py:581
  52.3 12.0 %qkv_forward.3 = (bf16[1024,768]{1,0:T(8,128)(2,1)}, bf16[1024,768]{1,0:T(8,128)(2,1)}, bf16[1024,768]{1,0:T(8,128)(2,1)}, bf16[1024,768]{1,0:T(8,128)(2,1)}, bf...) custom-call(f32[1024,768]{1,0:T(8,128)} %get-tuple-element.84.h_ref.refs_7_, f32[8,768]{1,0:T(8,128)} %get-tuple-element.148.gain_ref, ...), custom_call_target="tpu_custom_call" | custom-call | tf_op jit(solution)/shard_map/qkv_forward/pallas_call | solution.py:430
  64.4 28.7 %mix_forward.3 = (bf16[1024,768]{1,0:T(8,128)(2,1)}, f32[1024,768]{1,0:T(8,128)}, bf16[1024,3072]{1,0:T(8,128)(2,1)}, bf16[1024,768]{1,0:T(8,128)(2,1)}, bf16[76...) custom-call(f32[1024,768]{1,0:T(8,128)} %get-tuple-element.84.h_ref.refs_7_, ...), custom_call_target="tpu_custom_call" | custom-call | tf_op jit(solution)/shard_map/mix_forward/pallas_call | solution.py:581
  93.1 0.0 copy-start
  93.1 37.4 %ffn_backward.2 = (f32[1024,768]{1,0:T(8,128)}, f32[8,768]{1,0:T(8,128)}, bf16[8,384,768]{2,1,0:T(8,128)(2,1)}, bf16[8,384,768]{2,1,0:T(8,128)(2,1)}) custom-call(bf16[1024,768]{1,0:T(8,128)(2,1)} %bitcast.26, bf16[1024,3072]{1,0:T(8,128)(2,1)} %get-tuple-element.90.before_ref, f32[1024,768]{1,0:T(8,128)} %get-tuple-element.91.middle_ref, ...), custom_call_target="tpu_custom_call" | custom-call | tf_op jit(solution)/shard_map/ffn_backward/pallas_call | solution.py:790
  130.5 0.3 copy.40
  130.8 0.0 copy-done
  130.8 0.8 broadcast_select_fusion.code_ref
  131.6 63.7 %attn_backward.2 = (f32[1024,768]{1,0:T(8,128)}, f32[24,768]{1,0:T(8,128)}, bf16[4,384,768]{2,1,0:T(8,128)(2,1)}, bf16[4,384,768]{2,1,0:T(8,128)(2,1)}, bf16[6,96,256]{2,1,0:T(8,128)(2,1)}) custom-call(s32[1,1024]{1,0:T(1,128)} %seg_ref.3, s32[1024,1]{1,0:T(8,128)} %broadcast_select_fusion.code_ref, f32[8,768]{1,0:T(8,128)} %get-tuple-element.148.gain_ref, ...), custom_call_target="tpu_custom_call" | custom-call | tf_op jit(solution)/shard_map/attn_backward/pallas_call | solution.py:986
  195.3 69.5 %ffn_backward.3 = (f32[1024,768]{1,0:T(8,128)}, f32[8,768]{1,0:T(8,128)}, bf16[8,384,768]{2,1,0:T(8,128)(2,1)}, bf16[8,384,768]{2,1,0:T(8,128)(2,1)}, bf16[8,384...) custom-call(f32[1024,768]{1,0:T(8,128)} %get-tuple-element.102.dh_ref, bf16[1024,3072]{1,0:T(8,128)(2,1)} %get-tuple-element.103.before_ref, ...), custom_call_target="tpu_custom_call" | custom-call | tf_op jit(solution)/shard_map/ffn_backward/pallas_call | solution.py:790
  264.8 0.0 copy-start.6
  264.8 0.0 copy-start.2
  264.8 0.0 copy-start.5
  264.8 75.7 %attn_backward.3 = (f32[1024,768]{1,0:T(8,128)}, f32[24,768]{1,0:T(8,128)}, bf16[4,384,768]{2,1,0:T(8,128)(2,1)}, bf16[4,384,768]{2,1,0:T(8,128)(2,1)}, bf16[4,3...) custom-call(s32[1,1024]{1,0:T(1,128)} %seg_ref.3, s32[1024,1]{1,0:T(8,128)} %broadcast_select_fusion.code_ref, ...), custom_call_target="tpu_custom_call" | custom-call | tf_op jit(solution)/shard_map/attn_backward/pallas_call | solution.py:986
  340.6 0.9 bitcast_reduce_fusion.1
  341.5 0.0 copy-done.6
  341.6 0.0 copy-done.2
  341.6 0.0 copy-done.5
  341.7 0.6 concatenate.3.refs_0_
  342.3 88.3 %last_sums.1 = (f32[8,768]{1,0:T(8,128)}, bf16[8,384,768]{2,1,0:T(8,128)(2,1)}, bf16[4,384,768]{2,1,0:T(8,128)(2,1)}) custom-call(f32[8,768]{1,0:T(8,128)} %concatenate.3.refs_0_, bf16[6,96,256]{2,1,0:T(8,128)(2,1)} %get-tuple-element.125.refs_1_, bf16[4,384,768]{2,1,0:T(8,128)(2,1)} %get-tuple-element.126.refs_2_, ...), custom_call_target="tpu_custom_call" | custom-call | tf_op jit(solution)/shard_map/last_sums/pallas_call | solution.py:1056
  430.6 22.9 %adam_step.7 = (f32[2,1536,768]{2,1,0:T(8,128)}, f32[2,1536,768]{2,1,0:T(8,128)}, f32[2,1536,768]{2,1,0:T(8,128)}) custom-call(f32[2,1536,768]{2,1,0:T(8,128)} %weight_ref.7, f32[2,1536,768]{2,1,0:T(8,128)} %first_ref.7, f32[2,1536,768]{2,1,0:T(8,128)} %second_ref.7, bf16[8,384,768]{2,1,0:T(8,128)(2,1)} %get-tuple-element.136.refs_0_, ...), custom_call_target="tpu_custom_call" | custom-call | tf_op jit(solution)/shard_map/adam_step/pallas_call | solution.py:1112
  453.5 22.9 %adam_step.6 = (f32[2,384,3072]{2,1,0:T(8,128)}, f32[2,384,3072]{2,1,0:T(8,128)}, f32[2,384,3072]{2,1,0:T(8,128)}) custom-call(f32[2,384,3072]{2,1,0:T(8,128)} %weight_ref.6, f32[2,384,3072]{2,1,0:T(8,128)} %first_ref.6, f32[2,384,3072]{2,1,0:T(8,128)} %second_ref.6, bf16[8,384,768]{2,1,0:T(8,128)(2,1)} %get-tuple-element.136.refs_0_, ...), custom_call_target="tpu_custom_call" | custom-call | tf_op jit(solution)/shard_map/adam_step/pallas_call | solution.py:1112
  476.4 6.1 %adam_step.5 = (f32[2,384,768]{2,1,0:T(8,128)}, f32[2,384,768]{2,1,0:T(8,128)}, f32[2,384,768]{2,1,0:T(8,128)}) custom-call(f32[2,384,768]{2,1,0:T(8,128)} %weight_ref.5, f32[2,384,768]{2,1,0:T(8,128)} %first_ref.5, f32[2,384,768]{2,1,0:T(8,128)} %second_ref.5, bf16[4,384,768]{2,1,0:T(8,128)(2,1)} %get-tuple-element.128.refs_0_, ...), custom_call_target="tpu_custom_call" | custom-call | tf_op jit(solution)/shard_map/adam_step/pallas_call | solution.py:1112
  482.5 0.0 copy-start.7
  482.5 0.0 copy-start.4
  482.5 0.0 copy-start.9
  482.5 0.0 copy-start.10
  482.5 17.5 %adam_step.4 = (f32[2,384,2304]{2,1,0:T(8,128)}, f32[2,384,2304]{2,1,0:T(8,128)}, f32[2,384,2304]{2,1,0:T(8,128)}) custom-call(f32[2,384,2304]{2,1,0:T(8,128)} %weight_ref.4, f32[2,384,2304]{2,1,0:T(8,128)} %first_ref.4, f32[2,384,2304]{2,1,0:T(8,128)} %second_ref.4, bf16[4,384,768]{2,1,0:T(8,128)(2,1)} %get-tuple-element.128.refs_0_, ...), custom_call_target="tpu_custom_call" | custom-call | tf_op jit(solution)/shard_map/adam_step/pallas_call | solution.py:1112
  500.0 0.0 copy-start.1
  500.0 0.0 copy-done.7
  500.0 0.0 copy-done.4
  500.0 0.0 copy-done.9
  500.0 0.0 copy-done.10
  500.1 0.6 multiply_subtract_fusion
  500.7 2.9 copy.44
  503.6 0.0 copy-done.1
  503.6 1.7 copy.45
  (12 shorter events, 0.1 us)
Async XLA Ops:
  3.9 15.6 %copy-start.3 = (s32[1,1024]{1,0:T(1,128)S(1)}, s32[1,1024]{1,0:T(1,128)}, u32[]{:S(2)}) copy-start(s32[1,1024]{1,0:T(1,128)} %seg_ref.3) | copy-start | bytes 12292
  3.9 16.7 %copy-start.8 = (s32[1,1024]{1,0:T(1,128)S(1)}, s32[1,1024]{1,0:T(1,128)}, u32[]{:S(2)}) copy-start(s32[1,1024]{1,0:T(1,128)} %param.24) | copy-start | bytes 12292
  93.1 37.7 %copy-start = (s32[1024,1]{1,0:T(8,128)S(1)}, s32[1024,1]{1,0:T(8,128)}, u32[]{:S(2)}) copy-start(s32[1024,1]{1,0:T(8,128)} %copy.38.seg_ref) | copy-start | bytes 12292
  264.8 76.7 %copy-start.6 = (f32[8,768]{1,0:T(8,128)S(1)}, f32[8,768]{1,0:T(8,128)}, u32[]{:S(2)}) copy-start(f32[8,768]{1,0:T(8,128)} %get-tuple-element.122) | copy-start | bytes 73732
  264.8 76.8 %copy-start.2 = (f32[24,768]{1,0:T(8,128)S(1)}, f32[24,768]{1,0:T(8,128)}, u32[]{:S(2)}) copy-start(f32[24,768]{1,0:T(8,128)} %get-tuple-element.123) | copy-start | bytes 221188
  264.8 76.8 %copy-start.5 = (f32[8,768]{1,0:T(8,128)S(1)}, f32[8,768]{1,0:T(8,128)}, u32[]{:S(2)}) copy-start(f32[8,768]{1,0:T(8,128)} %get-tuple-element.124) | copy-start | bytes 73732
  482.5 17.5 %copy-start.7 = (f32[8,768]{1,0:T(8,128)S(1)}, f32[8,768]{1,0:T(8,128)}, u32[]{:S(2)}) copy-start(f32[8,768]{1,0:T(8,128)} %get-tuple-element.144) | copy-start | bytes 73732
  482.5 17.5 %copy-start.4 = (f32[2,384,4]{1,2,0:T(4,128)S(1)}, f32[2,384,4]{1,2,0:T(4,128)}, u32[]{:S(2)}) copy-start(f32[2,384,4]{1,2,0:T(4,128)} %param.37) | copy-start | bytes 36868
  482.5 17.5 %copy-start.9 = (f32[2,384,4]{1,2,0:T(4,128)S(1)}, f32[2,384,4]{1,2,0:T(4,128)}, u32[]{:S(2)}) copy-start(f32[2,384,4]{1,2,0:T(4,128)} %param.38) | copy-start | bytes 36868
  482.5 17.5 %copy-start.10 = (f32[2,384,4]{1,2,0:T(4,128)S(1)}, f32[2,384,4]{1,2,0:T(4,128)}, u32[]{:S(2)}) copy-start(f32[2,384,4]{1,2,0:T(4,128)} %param.39) | copy-start | bytes 36868
  500.0 3.6 copy-start.1

commit v6 on v5

--- a/solution.py
+++ b/solution.py
@@ -1082,41 +1082,49 @@
     return weight - rate * (step + decay * weight), first, second
 
 
-def adam_kernel(weight_ref, first_ref, second_ref, *refs):
+def adam_kernel(down, weight_ref, first_ref, second_ref, *refs):
     grad_refs, outs = refs[:-3], refs[-3:]
+    half = D // 2
     for layer, grad_ref in enumerate(grad_refs):
 
         @pl.when(pl.program_id(0) == layer)
         def _():
-            results = adam(
-                weight_ref[0], first_ref[0], second_ref[0], grad_ref[0].astype(F32), D ** (-0.5), 0.1
-            )
-            for out, result in zip(outs, results):
-                out[0] = result
+            for i in range(grad_ref.shape[0]):
+                rows = slice(i * half, (i + 1) * half) if down else slice(0, half)
+                lanes = slice(0, D) if down else slice(i * D, (i + 1) * D)
+                results = adam(
+                    weight_ref[0, rows, lanes], first_ref[0, rows, lanes], second_ref[0, rows, lanes],
+                    grad_ref[i].astype(F32), D ** (-0.5), 0.1,
+                )
+                for out, result in zip(outs, results):
+                    out[0, rows, lanes] = result
 
 
 def adam_step(weight, first, second, totals, base):
     layers, rows, width = weight.shape
     half = D // 2
-    down, across = rows // half, width // D
-    last = down * across - 1
-    part = pl.BlockSpec((1, half, D), lambda l, i, j: (l, i, j))
+    down = width == D
+    blocks = rows * width // (half * D)
+    each = 2 if blocks % 2 == 0 and base % 2 == 0 else 1
+    steps = blocks // each
+    shape = (1, each * half, D) if down else (1, half, each * D)
+    part = pl.BlockSpec(shape, (lambda l, i: (l, i, 0)) if down else (lambda l, i: (l, 0, i)))
 
     def grad_spec(layer):
-        def at(l, i, j):
-            inside = jnp.where(l < layer, 0, last)
-            return (base + jnp.where(l == layer, i * across + j, inside), 0, 0)
-
-        return pl.BlockSpec((1, half, D), at)
+        def at(l, i):
+            inside = jnp.where(l < layer, 0, steps - 1)
+            return (base // each + jnp.where(l == layer, i, inside), 0, 0)
+
+        return pl.BlockSpec((each, half, D), at)
 
     return pl.pallas_call(
-        adam_kernel,
+        functools.partial(adam_kernel, down),
         name="adam_step",
-        grid=(layers, down, across),
+        grid=(layers, steps),
         in_specs=[part] * 3 + [grad_spec(layer) for layer in range(layers)],
         out_specs=[part] * 3,
         out_shape=[jax.ShapeDtypeStruct(weight.shape, F32)] * 3,
-        compiler_params=params(3),
+        compiler_params=params(2),
     )(weight, first, second, *totals)
 
 

time: 515 us -> 510 us (level)
  no operation moved by 1% of the time
where the time goes in v6:
time: 510 us; the launch traced here: 501 us
  Pallas kernels  486 us (95%)
  local copies, waits for them, and re-layouts  7.25 us (1%)
    pallas_call x2, Pallas kernels, attn_backward(): pl.pallas_call(functools.partial(attn_back_kernel, tile, reach, rows, sto...  139 us
    pallas_call x2, Pallas kernels, ffn_backward(): pl.pallas_call(functools.partial(ffn_back_kernel, blocks, store, sums, pl...  107 us
    pallas_call x1, Pallas kernels, last_sums(): pl.pallas_call(functools.partial(last_sums_kernel, sums, steps, (len(ins)...  88.3 us
    pallas_call x4, Pallas kernels, adam_step(): pl.pallas_call(functools.partial(adam_kernel, down), name='adam_step', gr...  64.4 us
    pallas_call x2, Pallas kernels, mix_forward(): pl.pallas_call(functools.partial(mix_kernel, tile, reach, pull, layer, fo...  59.8 us
    pallas_call x2, Pallas kernels, qkv_forward(): pl.pallas_call(functools.partial(qkv_kernel, pull) if fresh else functool...  27.6 us

profile of v6, /device:TPU:0, one launch (start us, length us, event | category | flops | bytes accessed | tf_op | source)
XLA Modules:
  0.0 500.7 jit_solution(16093319460895121222)
XLA Ops:
  0.7 0.7 convert_element_type.6
  1.4 1.9 all_gather.3
  3.3 0.6 slice_bitcast_fusion
  3.9 0.0 copy-start.3
  3.9 0.0 copy-start.8
  3.9 15.6 %qkv_forward.2 = (bf16[1024,768]{1,0:T(8,128)(2,1)}, bf16[1024,768]{1,0:T(8,128)(2,1)}, bf16[1024,768]{1,0:T(8,128)(2,1)}, bf16[1024,768]{1,0:T(8,128)(2,1)}, bf...) custom-call(bf16[1024,768]{1,0:T(8,128)(2,1)} %bitcast.21, ...), custom_call_target="tpu_custom_call" | custom-call | tf_op jit(solution)/shard_map/qkv_forward/pallas_call | solution.py:430
  19.5 0.0 copy-done.3
  19.5 1.0 copy.38.seg_ref
  20.6 0.0 copy-done.8
  20.6 0.6 compare_select_fusion.code_ref
  21.2 31.2 %mix_forward.2 = (bf16[1024,768]{1,0:T(8,128)(2,1)}, f32[1024,768]{1,0:T(8,128)}, bf16[1024,3072]{1,0:T(8,128)(2,1)}, f32[1024,768]{1,0:T(8,128)}, bf16[768,768]...) custom-call(bf16[1024,768]{1,0:T(8,128)(2,1)} %bitcast.22, ...), custom_call_target="tpu_custom_call" | custom-call | tf_op jit(solution)/shard_map/mix_forward/pallas_call | solution.py:581
  52.3 12.0 %qkv_forward.3 = (bf16[1024,768]{1,0:T(8,128)(2,1)}, bf16[1024,768]{1,0:T(8,128)(2,1)}, bf16[1024,768]{1,0:T(8,128)(2,1)}, bf16[1024,768]{1,0:T(8,128)(2,1)}, bf...) custom-call(f32[1024,768]{1,0:T(8,128)} %get-tuple-element.84.h_ref.refs_7_, f32[8,768]{1,0:T(8,128)} %get-tuple-element.148.gain_ref, ...), custom_call_target="tpu_custom_call" | custom-call | tf_op jit(solution)/shard_map/qkv_forward/pallas_call | solution.py:430
  64.4 28.7 %mix_forward.3 = (bf16[1024,768]{1,0:T(8,128)(2,1)}, f32[1024,768]{1,0:T(8,128)}, bf16[1024,3072]{1,0:T(8,128)(2,1)}, bf16[1024,768]{1,0:T(8,128)(2,1)}, bf16[76...) custom-call(f32[1024,768]{1,0:T(8,128)} %get-tuple-element.84.h_ref.refs_7_, ...), custom_call_target="tpu_custom_call" | custom-call | tf_op jit(solution)/shard_map/mix_forward/pallas_call | solution.py:581
  93.1 0.0 copy-start
  93.1 37.4 %ffn_backward.2 = (f32[1024,768]{1,0:T(8,128)}, f32[8,768]{1,0:T(8,128)}, bf16[8,384,768]{2,1,0:T(8,128)(2,1)}, bf16[8,384,768]{2,1,0:T(8,128)(2,1)}) custom-call(bf16[1024,768]{1,0:T(8,128)(2,1)} %bitcast.26, bf16[1024,3072]{1,0:T(8,128)(2,1)} %get-tuple-element.90.before_ref, f32[1024,768]{1,0:T(8,128)} %get-tuple-element.91.middle_ref, ...), custom_call_target="tpu_custom_call" | custom-call | tf_op jit(solution)/shard_map/ffn_backward/pallas_call | solution.py:790
  130.5 0.3 copy.40
  130.8 0.0 copy-done
  130.8 0.8 broadcast_select_fusion.code_ref
  131.6 63.7 %attn_backward.2 = (f32[1024,768]{1,0:T(8,128)}, f32[24,768]{1,0:T(8,128)}, bf16[4,384,768]{2,1,0:T(8,128)(2,1)}, bf16[4,384,768]{2,1,0:T(8,128)(2,1)}, bf16[6,96,256]{2,1,0:T(8,128)(2,1)}) custom-call(s32[1,1024]{1,0:T(1,128)} %seg_ref.3, s32[1024,1]{1,0:T(8,128)} %broadcast_select_fusion.code_ref, f32[8,768]{1,0:T(8,128)} %get-tuple-element.148.gain_ref, ...), custom_call_target="tpu_custom_call" | custom-call | tf_op jit(solution)/shard_map/attn_backward/pallas_call | solution.py:986
  195.3 69.5 %ffn_backward.3 = (f32[1024,768]{1,0:T(8,128)}, f32[8,768]{1,0:T(8,128)}, bf16[8,384,768]{2,1,0:T(8,128)(2,1)}, bf16[8,384,768]{2,1,0:T(8,128)(2,1)}, bf16[8,384...) custom-call(f32[1024,768]{1,0:T(8,128)} %get-tuple-element.102.dh_ref, bf16[1024,3072]{1,0:T(8,128)(2,1)} %get-tuple-element.103.before_ref, ...), custom_call_target="tpu_custom_call" | custom-call | tf_op jit(solution)/shard_map/ffn_backward/pallas_call | solution.py:790
  264.8 0.0 copy-start.6
  264.8 0.0 copy-start.2
  264.8 0.0 copy-start.5
  264.8 75.7 %attn_backward.3 = (f32[1024,768]{1,0:T(8,128)}, f32[24,768]{1,0:T(8,128)}, bf16[4,384,768]{2,1,0:T(8,128)(2,1)}, bf16[4,384,768]{2,1,0:T(8,128)(2,1)}, bf16[4,3...) custom-call(s32[1,1024]{1,0:T(1,128)} %seg_ref.3, s32[1024,1]{1,0:T(8,128)} %broadcast_select_fusion.code_ref, ...), custom_call_target="tpu_custom_call" | custom-call | tf_op jit(solution)/shard_map/attn_backward/pallas_call | solution.py:986
  340.6 0.9 bitcast_reduce_fusion.1
  341.5 0.0 copy-done.6
  341.6 0.0 copy-done.2
  341.6 0.0 copy-done.5
  341.7 0.6 concatenate.3.refs_0_
  342.3 88.3 %last_sums.1 = (f32[8,768]{1,0:T(8,128)}, bf16[8,384,768]{2,1,0:T(8,128)(2,1)}, bf16[4,384,768]{2,1,0:T(8,128)(2,1)}) custom-call(f32[8,768]{1,0:T(8,128)} %concatenate.3.refs_0_, bf16[6,96,256]{2,1,0:T(8,128)(2,1)} %get-tuple-element.125.refs_1_, bf16[4,384,768]{2,1,0:T(8,128)(2,1)} %get-tuple-element.126.refs_2_, ...), custom_call_target="tpu_custom_call" | custom-call | tf_op jit(solution)/shard_map/last_sums/pallas_call | solution.py:1056
  430.6 20.4 %adam_step.7 = (f32[2,1536,768]{2,1,0:T(8,128)}, f32[2,1536,768]{2,1,0:T(8,128)}, f32[2,1536,768]{2,1,0:T(8,128)}) custom-call(f32[2,1536,768]{2,1,0:T(8,128)} %weight_ref.7, f32[2,1536,768]{2,1,0:T(8,128)} %first_ref.7, f32[2,1536,768]{2,1,0:T(8,128)} %second_ref.7, bf16[8,384,768]{2,1,0:T(8,128)(2,1)} %get-tuple-element.136.refs_0_, ...), custom_call_target="tpu_custom_call" | custom-call | tf_op jit(solution)/shard_map/adam_step/pallas_call | solution.py:1120
  451.0 20.4 %adam_step.6 = (f32[2,384,3072]{2,1,0:T(8,128)}, f32[2,384,3072]{2,1,0:T(8,128)}, f32[2,384,3072]{2,1,0:T(8,128)}) custom-call(f32[2,384,3072]{2,1,0:T(8,128)} %weight_ref.6, f32[2,384,3072]{2,1,0:T(8,128)} %first_ref.6, f32[2,384,3072]{2,1,0:T(8,128)} %second_ref.6, bf16[8,384,768]{2,1,0:T(8,128)(2,1)} %get-tuple-element.136.refs_0_, ...), custom_call_target="tpu_custom_call" | custom-call | tf_op jit(solution)/shard_map/adam_step/pallas_call | solution.py:1120
  471.4 6.1 %adam_step.5 = (f32[2,384,768]{2,1,0:T(8,128)}, f32[2,384,768]{2,1,0:T(8,128)}, f32[2,384,768]{2,1,0:T(8,128)}) custom-call(f32[2,384,768]{2,1,0:T(8,128)} %weight_ref.5, f32[2,384,768]{2,1,0:T(8,128)} %first_ref.5, f32[2,384,768]{2,1,0:T(8,128)} %second_ref.5, bf16[4,384,768]{2,1,0:T(8,128)(2,1)} %get-tuple-element.128.refs_0_, ...), custom_call_target="tpu_custom_call" | custom-call | tf_op jit(solution)/shard_map/adam_step/pallas_call | solution.py:1120
  477.5 0.0 copy-start.7
  477.5 0.0 copy-start.4
  477.5 0.0 copy-start.9
  477.5 0.0 copy-start.10
  477.5 17.5 %adam_step.4 = (f32[2,384,2304]{2,1,0:T(8,128)}, f32[2,384,2304]{2,1,0:T(8,128)}, f32[2,384,2304]{2,1,0:T(8,128)}) custom-call(f32[2,384,2304]{2,1,0:T(8,128)} %weight_ref.4, f32[2,384,2304]{2,1,0:T(8,128)} %first_ref.4, f32[2,384,2304]{2,1,0:T(8,128)} %second_ref.4, bf16[4,384,768]{2,1,0:T(8,128)(2,1)} %get-tuple-element.128.refs_0_, ...), custom_call_target="tpu_custom_call" | custom-call | tf_op jit(solution)/shard_map/adam_step/pallas_call | solution.py:1120
  495.0 0.0 copy-start.1
  495.0 0.0 copy-done.7
  495.0 0.0 copy-done.4
  495.0 0.0 copy-done.9
  495.1 0.0 copy-done.10
  495.1 0.6 multiply_subtract_fusion
  495.7 2.9 copy.44
  498.6 0.0 copy-done.1
  498.6 1.7 copy.45
  (12 shorter events, 0.1 us)
Async XLA Ops:
  3.9 15.6 %copy-start.3 = (s32[1,1024]{1,0:T(1,128)S(1)}, s32[1,1024]{1,0:T(1,128)}, u32[]{:S(2)}) copy-start(s32[1,1024]{1,0:T(1,128)} %seg_ref.3) | copy-start | bytes 12292
  3.9 16.7 %copy-start.8 = (s32[1,1024]{1,0:T(1,128)S(1)}, s32[1,1024]{1,0:T(1,128)}, u32[]{:S(2)}) copy-start(s32[1,1024]{1,0:T(1,128)} %param.24) | copy-start | bytes 12292
  93.1 37.7 %copy-start = (s32[1024,1]{1,0:T(8,128)S(1)}, s32[1024,1]{1,0:T(8,128)}, u32[]{:S(2)}) copy-start(s32[1024,1]{1,0:T(8,128)} %copy.38.seg_ref) | copy-start | bytes 12292
  264.8 76.7 %copy-start.6 = (f32[8,768]{1,0:T(8,128)S(1)}, f32[8,768]{1,0:T(8,128)}, u32[]{:S(2)}) copy-start(f32[8,768]{1,0:T(8,128)} %get-tuple-element.122) | copy-start | bytes 73732
  264.8 76.8 %copy-start.2 = (f32[24,768]{1,0:T(8,128)S(1)}, f32[24,768]{1,0:T(8,128)}, u32[]{:S(2)}) copy-start(f32[24,768]{1,0:T(8,128)} %get-tuple-element.123) | copy-start | bytes 221188
  264.8 76.8 %copy-start.5 = (f32[8,768]{1,0:T(8,128)S(1)}, f32[8,768]{1,0:T(8,128)}, u32[]{:S(2)}) copy-start(f32[8,768]{1,0:T(8,128)} %get-tuple-element.124) | copy-start | bytes 73732
  477.5 17.5 %copy-start.7 = (f32[8,768]{1,0:T(8,128)S(1)}, f32[8,768]{1,0:T(8,128)}, u32[]{:S(2)}) copy-start(f32[8,768]{1,0:T(8,128)} %get-tuple-element.144) | copy-start | bytes 73732
  477.5 17.5 %copy-start.4 = (f32[2,384,4]{1,2,0:T(4,128)S(1)}, f32[2,384,4]{1,2,0:T(4,128)}, u32[]{:S(2)}) copy-start(f32[2,384,4]{1,2,0:T(4,128)} %param.37) | copy-start | bytes 36868
  477.5 17.5 %copy-start.9 = (f32[2,384,4]{1,2,0:T(4,128)S(1)}, f32[2,384,4]{1,2,0:T(4,128)}, u32[]{:S(2)}) copy-start(f32[2,384,4]{1,2,0:T(4,128)} %param.38) | copy-start | bytes 36868
  477.5 17.5 %copy-start.10 = (f32[2,384,4]{1,2,0:T(4,128)S(1)}, f32[2,384,4]{1,2,0:T(4,128)}, u32[]{:S(2)}) copy-start(f32[2,384,4]{1,2,0:T(4,128)} %param.39) | copy-start | bytes 36868
  495.0 3.6 copy-start.1
